TPU v7x, 768 devices: a whole 4x8x12 slice. The times are simulated.
768 devices in a mesh: seq: 48 (over x_lo, z, core), head: 16 (over x_hi, y).
Axes of the slice: x: 4 (x_hi: 2, x_lo: 2; x = x_hi * 2 + x_lo), y: 8, z: 12, core: 2. Of those that a mesh axis runs over, the one named last changes fastest.
Arguments:
- query_rows: bfloat16 [30720, 8192], P(('seq', 'head')), may hold values from -6 to 6
- rotated_key_rows: bfloat16 [30720, 1024], P(('seq', 'head')), may hold values from -6 to 6
- value_row_matrix: bfloat16 [30720, 1024], P(('seq', 'head')), may hold values from -6 to 6
- group_assign: int32 [64], replicated, may hold values from 0 to 63, each once
- vertical_blocks: int32 [64, 4], replicated, may hold values from 0 to 239
- slash_offsets: int32 [64, 3], replicated, may hold values from 0 to 5, as said below
Outputs:
- attended: bfloat16 [30720, 8192], P(('seq', 'head'))
Inputs may be any that keep to these rules, and one draw needn't show every extreme that they name: `slash_offsets`: each head's first offset is 0 and its offsets are distinct.
All inputs are finite; a program needn't handle non-finite values.
Results may differ from a plain program's by a relative error of at most 0.0045.
Values may be sent and summed in bfloat16 or wider, within the bound.
No kernel may reach another device: no remote copies, remote signals or barrier semaphores. Data moves between devices by JAX's collectives and lax.ppermute only.
A program may use at most 32 MiB of HBM per device.

v0:
```python
import math

import jax
import jax.numpy as jnp
from jax import lax
from jax.sharding import PartitionSpec as P

QUERY_HEADS = 64
KEY_VALUE_HEADS = 8
HEAD_SIZE = 128
BLOCK_TOKENS = 128
NV = 4


def side_by_side(arrays, axis, split_dim, concat_dim, along):
    both = jnp.concatenate(arrays, axis=along)
    whole, at, finished = (
        lax.all_to_all(both, axis, split_axis=split_dim, concat_axis=concat_dim, tiled=True),
        0,
        [],
    )
    for a in arrays:
        finished.append(lax.slice_in_dim(whole, at, at + a.shape[along], axis=along))
        at += a.shape[along]
    return tuple(finished)


def passed_along(value, axis, steps):
    count = lax.axis_size(axis)
    leading, last = (max(0, -steps), min(count, count - steps))
    return lax.ppermute(value, axis, [(source, source + steps) for source in range(leading, last)])


def packed_total(arrays, axis):
    ravelled, at, finished = (jnp.concatenate([a.reshape(-1) for a in arrays]), 0, [])
    total = lax.psum(ravelled, axis)
    for a in arrays:
        finished.append(total[at : at + a.size].reshape(a.shape))
        at += a.size
    return tuple(finished)


def per_device(
    query_rows, rotated_key_rows, value_row_matrix, group_assign, vertical_blocks, slash_offsets
):
    groups = lax.axis_size("head")
    slot_count = QUERY_HEADS // groups
    sharing_count = QUERY_HEADS // KEY_VALUE_HEADS
    resident_rows = query_rows.shape[0]
    key_value_heads = group_assign // sharing_count
    query_sel = query_rows.reshape(resident_rows, QUERY_HEADS, HEAD_SIZE)[:, group_assign]
    selected_keys = rotated_key_rows.reshape(resident_rows, KEY_VALUE_HEADS, HEAD_SIZE)[
        :, key_value_heads
    ]
    selected_values = value_row_matrix.reshape(resident_rows, KEY_VALUE_HEADS, HEAD_SIZE)[
        :, key_value_heads
    ]
    query_here, key_here, value_here = side_by_side(
        (query_sel, selected_keys, selected_values), "head", 1, 0, 2
    )
    seq_rows = query_here.shape[0]
    local_blocks = seq_rows // BLOCK_TOKENS
    my_heads = lax.dynamic_slice_in_dim(
        group_assign, lax.axis_index("head") * slot_count, slot_count
    )
    my_verticals = vertical_blocks[my_heads]
    my_offsets = slash_offsets[my_heads]
    key_before, value_before = passed_along((key_here, value_here), "seq", 1)
    seq_place = lax.axis_index("seq")
    block_local = my_verticals % local_blocks
    block_owner = my_verticals // local_blocks
    slot_column = jnp.arange(slot_count)[:, None]
    key_candidate = key_here.reshape(local_blocks, BLOCK_TOKENS, slot_count, HEAD_SIZE)[
        block_local, :, slot_column
    ]
    value_candidate = value_here.reshape(local_blocks, BLOCK_TOKENS, slot_count, HEAD_SIZE)[
        block_local, :, slot_column
    ]
    owned_here = (block_owner == seq_place)[:, :, None, None]
    summed_keys, summed_values = packed_total(
        (
            jnp.where(owned_here, key_candidate.astype(jnp.float32), 0.0),
            jnp.where(owned_here, value_candidate.astype(jnp.float32), 0.0),
        ),
        "seq",
    )
    column_keys = summed_keys.astype(jnp.bfloat16)
    column_values = summed_values.astype(jnp.bfloat16)
    query_pos = seq_place * seq_rows + jnp.arange(seq_rows)
    query_block = query_pos // BLOCK_TOKENS
    window_pos = seq_place * seq_rows - seq_rows + jnp.arange(2 * seq_rows)
    window_block = jnp.floor_divide(window_pos, BLOCK_TOKENS)
    window_start = seq_place * local_blocks - local_blocks
    earlier = jnp.arange(NV)[:, None] < jnp.arange(NV)[None, :]
    scaling = 1.0 / math.sqrt(HEAD_SIZE)

    def attend_slot(head_slot):
        verticals = my_verticals[head_slot]
        offsets = my_offsets[head_slot]
        repeated = jnp.any((verticals[:, None] == verticals[None, :]) & earlier, axis=0)
        column_ok = (verticals < window_start) & jnp.logical_not(repeated)
        slash_hit = jnp.any(
            query_block[:, None, None] - window_block[None, :, None] == offsets[None, None, :],
            axis=2,
        )
        vertical_hit = jnp.any(window_block[:, None] == verticals[None, :], axis=1)
        window_ok = (
            (window_pos[None, :] >= 0)
            & (window_pos[None, :] <= query_pos[:, None])
            & (slash_hit | vertical_hit[None, :])
        )
        column_mask = jnp.broadcast_to(
            jnp.repeat(column_ok, BLOCK_TOKENS)[None, :], (seq_rows, NV * BLOCK_TOKENS)
        )
        allowed = jnp.concatenate([window_ok, column_mask], axis=1)
        all_keys = jnp.concatenate(
            [
                key_before[:, head_slot],
                key_here[:, head_slot],
                column_keys[head_slot].reshape(NV * BLOCK_TOKENS, HEAD_SIZE),
            ],
            axis=0,
        )
        all_values = jnp.concatenate(
            [
                value_before[:, head_slot],
                value_here[:, head_slot],
                column_values[head_slot].reshape(NV * BLOCK_TOKENS, HEAD_SIZE),
            ],
            axis=0,
        )
        scores = (
            lax.dot_general(
                query_here[:, head_slot],
                all_keys,
                (((1,), (1,)), ((), ())),
                preferred_element_type=jnp.float32,
            )
            * scaling
        )
        row_top = jnp.max(jnp.where(allowed, scores, -jnp.inf), axis=1, keepdims=True)
        weights = jnp.where(allowed, jnp.exp(scores - row_top), 0.0)
        row_total = jnp.sum(weights, axis=1, keepdims=True)
        blended = (
            jnp.dot(weights.astype(jnp.bfloat16), all_values, preferred_element_type=jnp.float32)
            / row_total
        )
        return blended.astype(jnp.bfloat16)

    attended_here = lax.map(attend_slot, jnp.arange(slot_count))
    arranged = jnp.transpose(attended_here, (1, 0, 2))
    returned = lax.all_to_all(arranged, "head", split_axis=0, concat_axis=1, tiled=True)
    return returned.reshape(returned.shape[0], QUERY_HEADS * HEAD_SIZE)


def solution(mesh):
    placed = (
        P(("seq", "head"), None),
        P(("seq", "head"), None),
        P(("seq", "head"), None),
        P(),
        P(),
        P(),
    )
    return jax.shard_map(
        per_device, mesh=mesh, in_specs=placed, out_specs=P(("seq", "head"), None), check_vma=False
    )
```

profile of v0, /device:TPU:10, one launch (start us, length us, event | category | flops | bytes accessed | tf_op | source)
XLA Modules:
  0.0 347.3 jit_solution(16360471932350061267)
XLA Ops:
  4.8 1.6 pad_maximum_fusion.1
  6.4 9.1 %all-to-all-start = ((bf16[40,64,384]{2,0,1:T(8,128)(2,1)}), bf16[40,64,384]{2,0,1:T(8,128)(2,1)S(1)}, u32[]{:S(2)}, u32[]{:S(2)}) async-start(bf16[40,64,384]{2,0,1:T(8,128)(2,1)} %pad_maximum_fusion.1), calls=%async_computation | async-start | bytes 3932160 | tf_op jit(solution)/shard_map/all_to_all | solution.py:18
  17.0 46.0 %all-to-all-done = bf16[40,64,384]{2,0,1:T(8,128)(2,1)S(1)} async-done(((bf16[40,64,384]{2,0,1:T(8,128)(2,1)}), bf16[40,64,384]{2,0,1:T(8,128)(2,1)S(1)}, u32[]{:S(2)}, u32[]{:S(2)}) %all-to-all-start) | async-done | bytes 1966112 | tf_op jit(solution)/shard_map/all_to_all | solution.py:18
  63.3 1.6 fusion.62
  64.9 1.9 collective-permute-start
  66.8 4.4 %collective-permute-start.1 = (bf16[640,4,128]{2,0,1:T(8,128)(2,1)S(1)}, bf16[640,4,128]{2,0,1:T(8,128)(2,1)}, u32[]{:S(2)}, u32[]{:S(2)}) collective-permute-start(bf16[640,4,128]{2,0,1:T(8,128)(2,1)S(1)} %get-tuple-element.376), channel_id=1, source_target_pairs={{0,16},{16,32},{32,48},{48,64},{64,80},{80,96},{96,112},{112,128},... | collective-permute-start | bytes 1966088 | tf_op jit(solution)/shard_map/ppermute | solution.py:31
  71.2 1.7 gather_fusion.5
  74.0 191.0 %all-reduce.1 = bf16[524288]{0:T(1024)(128)(2,1)} all-reduce(f32[524288]{0:T(1024)S(1)} %pad_maximum_fusion), channel_id=1, replica_groups=mesh['seq'=48,'head'=16] {'seq'}, use_global_device_ids=true, to_apply=%region_0.1 | all-reduce | flops 524288 | bytes 3145728 | tf_op jit(solution)/shard_map/psum | solution.py:36
  265.0 1.3 fusion.63
  266.3 54.5 %while.12 = (s32[]{:T(128)}, bf16[4,640,128]{2,1,0:T(8,128)(2,1)}, s32[4]{0:T(128)S(1)}, s32[4,3]{1,0:T(4,128)S(1)}, s32[4,4]{1,0:T(4,128)S(1)}, /*index=5*/s32[...) while((s32[]{:T(128)}, bf16[4,640,128]{2,1,0:T(8,128)(2,1)}, ...), condition=%wide.region_7.8_spmd.clone.clone, body=%wide.region_1.7_spmd.clone.clone.sunk | while | flops 614408256 | bytes 28374412 | solution.py:150
  269.2 2.4 compare_reduce_fusion.4
  272.8 1.0 dynamic-slice_bitcast_fusion.6
  273.9 2.0 select_reduce_fusion.2
  275.8 1.3 fusion.81
  278.1 1.9 fusion.82
  282.9 2.4 compare_reduce_fusion.4
  286.4 1.0 dynamic-slice_bitcast_fusion.6
  287.5 2.0 select_reduce_fusion.2
  289.5 1.3 fusion.81
  291.7 1.9 fusion.82
  296.5 2.4 compare_reduce_fusion.4
  300.1 1.0 dynamic-slice_bitcast_fusion.6
  301.1 2.0 select_reduce_fusion.2
  303.1 1.3 fusion.81
  305.4 1.9 fusion.82
  310.1 2.4 compare_reduce_fusion.4
  314.7 2.0 select_reduce_fusion.2
  316.7 1.3 fusion.81
  319.0 1.9 fusion.82
  320.9 1.6 copy.46
  322.5 23.2 %all_to_all.33 = bf16[640,4,128]{2,1,0:T(4,128)(2,1)S(1)} all-to-all(bf16[640,4,128]{2,1,0:T(4,128)(2,1)S(1)} %bitcast.109), channel_id=1, replica_groups=mesh['seq'=48,'head'=16] {'head'}, dimensions={0} | all-to-all | bytes 1310720 | tf_op jit(solution)/shard_map/all_to_all | solution.py:152
  346.0 1.3 reshape.148
  (95 shorter events, 21.4 us)
Async XLA Ops:
  0.0 4.0 %copy-start = (bf16[40,8192]{1,0:T(8,128)(2,1)S(1)}, bf16[40,8192]{1,0:T(8,128)(2,1)}, u32[]{:S(2)}) copy-start(bf16[40,8192]{1,0:T(8,128)(2,1)} %param.8) | copy-start | bytes 1966084
  4.8 10.7 %copy-start.1 = (s32[64,4]{0,1:T(4,128)S(1)}, s32[64,4]{0,1:T(4,128)}, u32[]{:S(2)}) copy-start(s32[64,4]{0,1:T(4,128)} %param.12) | copy-start | bytes 3076
  4.8 10.8 %copy-start.3 = (s32[64]{0:T(128)S(1)}, s32[64]{0:T(128)}, u32[]{:S(2)}) copy-start(s32[64]{0:T(128)} %param.11) | copy-start | bytes 772
  4.8 11.6 %copy-start.2 = (s32[64,3]{0,1:T(4,128)S(1)}, s32[64,3]{0,1:T(4,128)}, u32[]{:S(2)}) copy-start(s32[64,3]{0,1:T(4,128)} %param.13) | copy-start | bytes 2308
  6.4 56.7 %all-to-all-start = ((bf16[40,64,384]{2,0,1:T(8,128)(2,1)}), bf16[40,64,384]{2,0,1:T(8,128)(2,1)S(1)}, u32[]{:S(2)}, u32[]{:S(2)}) async-start(bf16[40,64,384]{2,0,1:T(8,128)(2,1)} %pad_maximum_fusion.1), calls=%async_computation | async-start | bytes 3932160 | tf_op jit(solution)/shard_map/all_to_all | solution.py:18
  64.9 201.5 %collective-permute-start = (bf16[640,4,128]{2,0,1:T(8,128)(2,1)}, bf16[640,4,128]{2,0,1:T(8,128)(2,1)}, u32[]{:S(2)}, u32[]{:S(2)}) collective-permute-start(bf16[640,4,128]{2,0,1:T(8,128)(2,1)} %get-tuple-element.373), channel_id=1, source_target_pairs={{0,16},{16,32},{32,48},{48,64},{64,80},{80,96},{96,112},{112,128},... | collective-permute-start | bytes 1966088 | tf_op jit(solution)/shard_map/ppermute | solution.py:31
  66.8 199.5 %collective-permute-start.1 = (bf16[640,4,128]{2,0,1:T(8,128)(2,1)S(1)}, bf16[640,4,128]{2,0,1:T(8,128)(2,1)}, u32[]{:S(2)}, u32[]{:S(2)}) collective-permute-start(bf16[640,4,128]{2,0,1:T(8,128)(2,1)S(1)} %get-tuple-element.376), channel_id=1, source_target_pairs={{0,16},{16,32},{32,48},{48,64},{64,80},{80,96},{96,112},{112,128},... | collective-permute-start | bytes 1966088 | tf_op jit(solution)/shard_map/ppermute | solution.py:31
where the time goes:
time: 348 us; the launch traced here: 347 us
  blocking collectives  214 us (61%)
  waiting for transfers between devices  46 us (13%)
  local copies, waits for them, and re-layouts  25.1 us (7%)
  other arithmetic  23.2 us (7%)
  starting transfers between devices  15.4 us (4%)
  matrix products  15.3 us (4%)
  loops' own time  7.88 us (2%)
    psum x1, blocking collectives, packed_total(): total = lax.psum(ravelled, axis)  191 us
    all_to_all x1, waiting for transfers between devices, side_by_side(): lax.all_to_all(both, axis, split_axis=split_dim, concat_axis=concat_dim,...  46 us
    all_to_all x1, blocking collectives, per_device(): lax.all_to_all(arranged, 'head', split_axis=0, concat_axis=1, tiled=True)  23.2 us
    reduce_or x4, other arithmetic, attend_slot(): jnp.any(query_block[:, None, None] - window_block[None, :, None] == offse...  9.41 us
    all_to_all x1, starting transfers between devices, side_by_side(): lax.all_to_all(both, axis, split_axis=split_dim, concat_axis=concat_dim,...  9.12 us
    another operation x1, loops' own time, per_device(): attended_here = lax.map(attend_slot, jnp.arange(slot_count))  7.88 us
    dot_general x4, matrix products, attend_slot(): lax.dot_general(query_here[:, head_slot], all_keys, (((1,), (1,)), ((), (...  7.87 us
    dot_general x4, matrix products, attend_slot(): jnp.dot(weights.astype(jnp.bfloat16), all_values, preferred_element_type=...  7.47 us
  transfers between devices with their start and end apart: 3, of which 1 were waited for; matrix products, arithmetic and copies ran while one was open for 2% of the time, Pallas kernels for 0%

commit v1 on v0

v1 whole, which is shorter than its diff:
```python
import functools
import math

import jax
import jax.numpy as jnp
from jax import lax
from jax.experimental import pallas as pl
from jax.experimental.pallas import tpu as pltpu
from jax.sharding import Mesh, PartitionSpec as P

QUERY_HEADS = 64
KEY_VALUE_HEADS = 8
HD = 128
BT = 128
NV = 4
NS = 3
GROUPS = 16
SLOTS = QUERY_HEADS // GROUPS
ROWS = 40
SEQ_ROWS = 640
LB = SEQ_ROWS // BT
CH = 16
SUB = 16
ALL = ("xl", "za", "zb", "c", "xh", "y")
SEQ = ("xl", "za", "zb", "c")
HEAD = ("xh", "y")
PART = ("xl", "zb", "c")
SCALE = 1.0 / math.sqrt(HD)
NEG = float("-inf")


def attend(meta, q_ref, kv_ref, prev_ref, vert_ref, o_ref, win, kc, vc):
    seq_place = meta[0]
    win[0:SEQ_ROWS, :] = prev_ref[...]
    win[SEQ_ROWS:, :] = kv_ref[...]
    causal = lax.broadcasted_iota(jnp.int32, (BT, BT), 0) >= lax.broadcasted_iota(
        jnp.int32, (BT, BT), 1
    )

    def one_head(h, carry):
        lane = pl.ds(pl.multiple_of(h * HD, HD), HD)
        offs = [meta[17 + h * NS + n] for n in range(NS)]
        verts = [meta[1 + h * NV + n] for n in range(NV)]
        for n in range(NV):
            rows = slice((NS + n) * BT, (NS + n + 1) * BT)
            for i in range(LB):
                kc[i, rows, :] = vert_ref[0:8, h * NV + n].reshape(BT, HD)
                vc[i, rows, :] = vert_ref[8:16, h * NV + n].reshape(BT, HD)
        for i in range(LB):
            block = seq_place * LB + i
            good = []
            for n in range(NS):
                at = pl.ds(pl.multiple_of((LB + i - offs[n]) * BT, BT), BT)
                rows = slice(n * BT, (n + 1) * BT)
                kc[i, rows, :] = win[at, 0:HD]
                vc[i, rows, :] = win[at, HD : 2 * HD]
                good.append(block - offs[n] >= 0)
            for n in range(NV):
                ok = verts[n] <= block
                for o in offs:
                    ok = ok & (block - verts[n] != o)
                for e in range(n):
                    ok = ok & (verts[n] != verts[e])
                good.append(ok)
            q = q_ref[i * BT : (i + 1) * BT, lane]
            s = (
                lax.dot_general(
                    q, kc[i], (((1,), (1,)), ((), ())), preferred_element_type=jnp.float32
                )
                * SCALE
            )
            parts = [jnp.where(causal, s[:, 0:BT], NEG)]
            for n in range(1, NS + NV):
                bias = jnp.where(good[n], 0.0, NEG)
                parts.append(s[:, n * BT : (n + 1) * BT] + bias)
            top = parts[0]
            for x in parts[1:]:
                top = jnp.maximum(top, x)
            top = jnp.max(top, axis=1, keepdims=True)
            ws = [jnp.exp(x - top) for x in parts]
            total = ws[0]
            for x in ws[1:]:
                total = total + x
            total = jnp.sum(total, axis=1, keepdims=True)
            w = jnp.concatenate([x.astype(jnp.bfloat16) for x in ws], axis=1)
            acc = jnp.dot(w, vc[i], preferred_element_type=jnp.float32)
            o_ref[i * BT : (i + 1) * BT, lane] = (acc / total).astype(jnp.bfloat16)
        return carry

    lax.fori_loop(0, SLOTS, one_head, 0)


def attention(meta, q, kv, prev, vert):
    vm = pl.BlockSpec(memory_space=pltpu.VMEM)
    return pl.pallas_call(
        attend,
        out_shape=jax.ShapeDtypeStruct((SEQ_ROWS, SLOTS * HD), jnp.bfloat16),
        in_specs=[pl.BlockSpec(memory_space=pltpu.SMEM), vm, vm, vm, vm],
        out_specs=vm,
        scratch_shapes=[
            pltpu.VMEM((2 * SEQ_ROWS, 2 * HD), jnp.bfloat16),
            pltpu.VMEM((LB, (NS + NV) * BT, HD), jnp.bfloat16),
            pltpu.VMEM((LB, (NS + NV) * BT, HD), jnp.bfloat16),
        ],
        name="attend",
    )(meta, q, kv, prev, vert)


def to_slots(assign, x_ref, o_ref):
    for k in range(QUERY_HEADS):
        a = assign[k]
        lane = pl.ds(pl.multiple_of((a % SLOTS) * HD, HD), HD)
        o_ref[:, k * HD : (k + 1) * HD] = x_ref[a // SLOTS, :, lane]


def place_slots(assign, x):
    vm = pl.BlockSpec(memory_space=pltpu.VMEM)
    return pl.pallas_call(
        to_slots,
        out_shape=jax.ShapeDtypeStruct((ROWS, QUERY_HEADS * HD), jnp.bfloat16),
        in_specs=[pl.BlockSpec(memory_space=pltpu.SMEM), vm],
        out_specs=vm,
        name="to_slots",
    )(assign, x)


def per_device(q_rows, k_rows, v_rows, group_assign, vertical_blocks, slash_offsets):
    group = lax.axis_index(HEAD)
    seq_place = lax.axis_index(SEQ)
    za = lax.axis_index("za")
    verts = lax.dynamic_slice_in_dim(vertical_blocks, group * SLOTS, SLOTS).reshape(-1)
    offs = lax.dynamic_slice_in_dim(slash_offsets, group * SLOTS, SLOTS).reshape(-1)

    kv = jnp.stack(
        [k_rows.reshape(ROWS, KEY_VALUE_HEADS, HD), v_rows.reshape(ROWS, KEY_VALUE_HEADS, HD)],
        axis=2,
    ).reshape(ROWS, KEY_VALUE_HEADS, 2 * HD)
    kv = jnp.repeat(jnp.transpose(kv, (1, 0, 2)), GROUPS // KEY_VALUE_HEADS, axis=0)
    kv_here = lax.all_to_all(kv, HEAD, 0, 0, tiled=True).reshape(SEQ_ROWS, 2 * HD)

    q = jnp.transpose(q_rows.reshape(ROWS, GROUPS, SLOTS * HD), (1, 0, 2))
    q_here = lax.all_to_all(q, HEAD, 0, 0, tiled=True).reshape(SEQ_ROWS, SLOTS * HD)

    kv_before = lax.ppermute(kv_here, SEQ, [(i, i + 1) for i in range(47)])

    chunks = jnp.transpose(kv_here.reshape(LB, 8, CH, 2, HD), (3, 1, 0, 2, 4))
    held = lax.all_to_all(chunks.reshape(SUB, LB, CH, HD), PART, 0, 0, tiled=True)
    owner = verts // LB
    z = (owner % 24) // 2
    spot = ((owner // 24) * 8 + (z % 4) * 2 + owner % 2) * LB + verts % LB
    mine = (z // 4 == za)[:, None, None]
    chosen = jnp.where(mine, held.reshape(SUB * LB, CH, HD)[spot], jnp.bfloat16(0))
    one = lax.ppermute(chosen, "za", [(0, 1), (1, 2), (2, 0)])
    two = lax.ppermute(chosen, "za", [(0, 2), (1, 0), (2, 1)])
    chosen = chosen + one + two
    spread = jnp.broadcast_to(chosen[None], (SUB, SLOTS * NV, CH, HD))
    vert = lax.all_to_all(spread, PART, 0, 0, tiled=True)

    meta = jnp.concatenate([seq_place[None].astype(jnp.int32), verts, offs])
    out = attention(meta, q_here, kv_here, kv_before, vert)
    back = lax.all_to_all(out.reshape(GROUPS, ROWS, SLOTS * HD), HEAD, 0, 0, tiled=True)
    return place_slots(group_assign, back)


def solution(mesh):
    fine = Mesh(mesh.devices.reshape(2, 3, 4, 2, 2, 8), ALL)
    rows = P(ALL, None)
    return jax.shard_map(
        per_device,
        mesh=fine,
        in_specs=(rows, rows, rows, P(), P(), P()),
        out_specs=rows,
        check_vma=False,
    )
```

time: 348 us -> 149 us (0.43)
  the two profiles are of different devices: /device:TPU:10 before, /device:TPU:65 now
where the time goes in v1:
time: 149 us; the launch traced here: 148 us
  blocking collectives  50.2 us (34%)
  waiting for transfers between devices  39.6 us (27%)
  starting transfers between devices  37.4 us (25%)
  Pallas kernels  12.9 us (9%)
  local copies, waits for them, and re-layouts  7.28 us (5%)
    all_to_all x1, blocking collectives, per_device(): lax.all_to_all(out.reshape(GROUPS, ROWS, SLOTS * HD), HEAD, 0, 0, tiled=T...  29.6 us
    ppermute x1, waiting for transfers between devices, per_device(): kv_before = lax.ppermute(kv_here, SEQ, [(i, i + 1) for i in range(47)])  22.3 us
    all_to_all x1, blocking collectives, per_device(): lax.all_to_all(kv, HEAD, 0, 0, tiled=True).reshape(SEQ_ROWS, 2 * HD)  20.6 us
    pallas_call x1, Pallas kernels, attention(): pl.pallas_call(attend, out_shape=jax.ShapeDtypeStruct((SEQ_ROWS, SLOTS *...  10.5 us
    ppermute x1, starting transfers between devices, per_device(): one = lax.ppermute(chosen, 'za', [(0, 1), (1, 2), (2, 0)])  10.3 us
    all_to_all x1, starting transfers between devices, per_device(): lax.all_to_all(chunks.reshape(SUB, LB, CH, HD), PART, 0, 0, tiled=True)  9.07 us
    all_to_all x1, waiting for transfers between devices, per_device(): lax.all_to_all(chunks.reshape(SUB, LB, CH, HD), PART, 0, 0, tiled=True)  8.09 us
    ppermute x1, waiting for transfers between devices, per_device(): two = lax.ppermute(chosen, 'za', [(0, 2), (1, 0), (2, 1)])  7.08 us
  transfers between devices with their start and end apart: 6, of which 4 were waited for; matrix products, arithmetic and copies ran while one was open for 2% of the time, Pallas kernels for 0%

profile of v1, /device:TPU:65, one launch (start us, length us, event | category | flops | bytes accessed | tf_op | source)
XLA Modules:
  0.0 148.5 jit_solution(10399831764707222865)
XLA Ops:
  0.0 0.9 copy.29
  1.1 20.6 %all_to_all.25 = bf16[16,40,256]{2,1,0:T(8,128)(2,1)S(1)} all-to-all(bf16[16,40,256]{2,1,0:T(8,128)(2,1)S(1)} %bitcast.33), channel_id=1, replica_groups=mesh['xl'=2,'za'=3,'zb'=4,'c'=2,'xh'=2,'y'=8] {'xh','y'}, dimensions={0} | all-to-all | bytes 655360 | tf_op jit(solution)/shard_map/all_to_all | solution.py:139
  21.7 0.8 copy.24
  22.5 9.1 %all-to-all-start.2 = ((bf16[16,5,16,128]{3,2,1,0:T(8,128)(2,1)}), bf16[16,5,16,128]{3,2,1,0:T(8,128)(2,1)S(1)}, u32[]{:S(2)}, u32[]{:S(2)}) async-start(bf16[16,5,16,128]{3,2,1,0:T(8,128)(2,1)} %bitcast.8), calls=%async_computation.2 | async-start | bytes 655360 | tf_op jit(solution)/shard_map/all_to_all | solution.py:147
  31.6 0.7 copy-done.7
  32.3 0.1 copy.20
  32.4 0.9 copy.32
  33.3 8.1 %all-to-all-done.2 = bf16[16,5,16,128]{3,2,1,0:T(8,128)(2,1)S(1)} async-done(((bf16[16,5,16,128]{3,2,1,0:T(8,128)(2,1)}), bf16[16,5,16,128]{3,2,1,0:T(8,128)(2,1)S(1)}, u32[]{:S(2)}, u32[]{:S(2)}) %all-to-all-start.2) | async-done | bytes 327712 | tf_op jit(solution)/shard_map/all_to_all | solution.py:147
  41.4 4.9 %all-to-all-start = ((bf16[16,40,512]{2,1,0:T(8,128)(2,1)}), bf16[16,40,512]{2,1,0:T(8,128)(2,1)S(1)}, u32[]{:S(2)}, u32[]{:S(2)}) async-start(bf16[16,40,512]{2,1,0:T(8,128)(2,1)} %bitcast.28), calls=%async_computation | async-start | bytes 1310720 | tf_op jit(solution)/shard_map/all_to_all | solution.py:142
  46.4 0.1 copy.27
  46.5 0.1 div.66
  46.5 0.1 copy.26
  46.6 0.1 rem.154
  46.7 0.1 copy.25
  46.8 0.1 ne.197
  47.1 0.6 gather_fusion
  47.8 10.3 %collective-permute-start.1 = (bf16[16,16,128]{2,1,0:T(8,128)(2,1)S(1)}, bf16[16,16,128]{2,1,0:T(8,128)(2,1)S(1)}, u32[]{:S(2)}, u32[]{:S(2)}) collective-permute-start(bf16[16,16,128]{2,1,0:T(8,128)(2,1)S(1)} %broadcast_select_fusion), channel_id=1, source_target_pairs={{0,128},{128,256},{256,0},{1,129},{129,257},{257,1},{2,130},{130,2... | collective-permute-start | bytes 196616 | tf_op jit(solution)/shard_map/ppermute | solution.py:153
  58.1 3.2 %collective-permute-start.2 = (bf16[16,16,128]{2,1,0:T(8,128)(2,1)S(1)}, bf16[16,16,128]{2,1,0:T(8,128)(2,1)S(1)}, u32[]{:S(2)}, u32[]{:S(2)}) collective-permute-start(bf16[16,16,128]{2,1,0:T(8,128)(2,1)S(1)} %broadcast_select_fusion), channel_id=1, source_target_pairs={{0,256},{128,0},{256,128},{1,257},{129,1},{257,129},{2,258},{130,2... | collective-permute-start | bytes 196616 | tf_op jit(solution)/shard_map/ppermute | solution.py:154
  61.3 2.0 %collective-permute-done.1 = bf16[16,16,128]{2,1,0:T(8,128)(2,1)S(1)} collective-permute-done((bf16[16,16,128]{2,1,0:T(8,128)(2,1)S(1)}, bf16[16,16,128]{2,1,0:T(8,128)(2,1)S(1)}, u32[]{:S(2)}, u32[]{:S(2)}) %collective-permute-start.1) | collective-permute-done | bytes 65568 | tf_op jit(solution)/shard_map/ppermute | solution.py:153
  63.3 7.1 %collective-permute-done.2 = bf16[16,16,128]{2,1,0:T(8,128)(2,1)S(1)} collective-permute-done((bf16[16,16,128]{2,1,0:T(8,128)(2,1)S(1)}, bf16[16,16,128]{2,1,0:T(8,128)(2,1)S(1)}, u32[]{:S(2)}, u32[]{:S(2)}) %collective-permute-start.2) | collective-permute-done | bytes 65568 | tf_op jit(solution)/shard_map/ppermute | solution.py:154
  70.4 0.1 add_add_fusion
  70.5 1.2 broadcast_in_dim.30
  71.7 6.5 %all-to-all-start.3 = ((bf16[16,16,16,128]{3,2,1,0:T(8,128)(2,1)}), bf16[16,16,16,128]{3,2,1,0:T(8,128)(2,1)S(1)}, u32[]{:S(2)}, u32[]{:S(2)}) async-start(bf16[16,16,16,128]{3,2,1,0:T(8,128)(2,1)} %broadcast_in_dim.30), calls=%async_computation.3 | async-start | bytes 2097152 | tf_op jit(solution)/shard_map/all_to_all | solution.py:157
  78.2 3.4 %collective-permute-start = (bf16[640,256]{1,0:T(8,128)(2,1)S(1)}, bf16[640,256]{1,0:T(8,128)(2,1)S(1)}, u32[]{:S(2)}, u32[]{:S(2)}) collective-permute-start(bf16[640,256]{1,0:T(8,128)(2,1)S(1)} %bitcast.29), channel_id=1, source_target_pairs={{0,16},{16,32},{32,48},{48,64},{64,80},{80,96},{96,112},{112,128},... | collective-permute-start | bytes 983048 | tf_op jit(solution)/shard_map/ppermute | solution.py:144
  81.7 0.1 copy.21
  81.8 0.7 pad_add_fusion.meta
  82.5 22.3 %collective-permute-done.prev_ref = bf16[640,256]{1,0:T(8,128)(2,1)S(1)} collective-permute-done((bf16[640,256]{1,0:T(8,128)(2,1)S(1)}, bf16[640,256]{1,0:T(8,128)(2,1)S(1)}, u32[]{:S(2)}, u32[]{:S(2)}) %collective-permute-start) | collective-permute-done | bytes 327712 | tf_op jit(solution)/shard_map/ppermute | solution.py:144
  104.8 0.7 copy-done.5
  105.6 0.4 copy-done.1
  105.9 10.5 %attend.1 = bf16[640,512]{1,0:T(8,128)(2,1)} custom-call(s32[29]{0:T(128)} %pad_add_fusion.meta, bf16[640,512]{1,0:T(8,128)(2,1)} %bitcast.31, bf16[640,256]{1,0:T(8,128)(2,1)} %bitcast.30, bf16[640,256]{1,0:T(8,128)(2,1)} %copy-done.5, bf16[16,16,16,128]{3,2,1,0:T(8,128)(2,1)} %copy-done.1), custom_call_target="tpu_custom_call" | custom-call | tf_op jit(solution)/shard_map/attend/pallas_call | solution.py:95
  116.4 29.6 %all_to_all.26.x_ref = bf16[16,40,512]{2,1,0:T(8,128)(2,1)} all-to-all(bf16[16,40,512]{2,1,0:T(8,128)(2,1)} %bitcast.32), channel_id=1, replica_groups=mesh['xl'=2,'za'=3,'zb'=4,'c'=2,'xh'=2,'y'=8] {'xh','y'}, dimensions={0} | all-to-all | bytes 1310720 | tf_op jit(solution)/shard_map/all_to_all | solution.py:161
  146.1 2.4 %to_slots.1 = bf16[40,8192]{1,0:T(8,128)(2,1)} custom-call(s32[64]{0:T(128)} %assign.1, bf16[16,40,512]{2,1,0:T(8,128)(2,1)} %all_to_all.26.x_ref), custom_call_target="tpu_custom_call" | custom-call | tf_op jit(solution)/shard_map/to_slots/pallas_call | solution.py:118
  (29 shorter events, 0.7 us)
Async XLA Ops:
  0.0 81.6 %copy-start = (s32[64,3]{0,1:T(4,128)S(1)}, s32[64,3]{0,1:T(4,128)}, u32[]{:S(2)}) copy-start(s32[64,3]{0,1:T(4,128)} %param.11) | copy-start | bytes 2308
  0.0 0.9 copy-start.6
  21.6 56.5 %copy-start.2 = (bf16[16,40,256]{2,1,0:T(8,128)(2,1)}, bf16[16,40,256]{2,1,0:T(8,128)(2,1)S(1)}, u32[]{:S(2)}) copy-start(bf16[16,40,256]{2,1,0:T(8,128)(2,1)S(1)} %all_to_all.25) | copy-start | bytes 983044
  21.7 10.7 %copy-start.4 = (bf16[40,8192]{1,0:T(8,128)(2,1)S(1)}, bf16[40,8192]{1,0:T(8,128)(2,1)}, u32[]{:S(2)}) copy-start(bf16[40,8192]{1,0:T(8,128)(2,1)} %param.6) | copy-start | bytes 1966084
  22.5 18.9 %all-to-all-start.2 = ((bf16[16,5,16,128]{3,2,1,0:T(8,128)(2,1)}), bf16[16,5,16,128]{3,2,1,0:T(8,128)(2,1)S(1)}, u32[]{:S(2)}, u32[]{:S(2)}) async-start(bf16[16,5,16,128]{3,2,1,0:T(8,128)(2,1)} %bitcast.8), calls=%async_computation.2 | async-start | bytes 655360 | tf_op jit(solution)/shard_map/all_to_all | solution.py:147
  31.6 0.7 copy-start.7
  41.4 29.1 %all-to-all-start = ((bf16[16,40,512]{2,1,0:T(8,128)(2,1)}), bf16[16,40,512]{2,1,0:T(8,128)(2,1)S(1)}, u32[]{:S(2)}, u32[]{:S(2)}) async-start(bf16[16,40,512]{2,1,0:T(8,128)(2,1)} %bitcast.28), calls=%async_computation | async-start | bytes 1310720 | tf_op jit(solution)/shard_map/all_to_all | solution.py:142
  47.8 15.6 %collective-permute-start.1 = (bf16[16,16,128]{2,1,0:T(8,128)(2,1)S(1)}, bf16[16,16,128]{2,1,0:T(8,128)(2,1)S(1)}, u32[]{:S(2)}, u32[]{:S(2)}) collective-permute-start(bf16[16,16,128]{2,1,0:T(8,128)(2,1)S(1)} %broadcast_select_fusion), channel_id=1, source_target_pairs={{0,128},{128,256},{256,0},{1,129},{129,257},{257,1},{2,130},{130,2... | collective-permute-start | bytes 196616 | tf_op jit(solution)/shard_map/ppermute | solution.py:153
  58.1 12.3 %collective-permute-start.2 = (bf16[16,16,128]{2,1,0:T(8,128)(2,1)S(1)}, bf16[16,16,128]{2,1,0:T(8,128)(2,1)S(1)}, u32[]{:S(2)}, u32[]{:S(2)}) collective-permute-start(bf16[16,16,128]{2,1,0:T(8,128)(2,1)S(1)} %broadcast_select_fusion), channel_id=1, source_target_pairs={{0,256},{128,0},{256,128},{1,257},{129,1},{257,129},{2,258},{130,2... | collective-permute-start | bytes 196616 | tf_op jit(solution)/shard_map/ppermute | solution.py:154
  70.5 1.2 copy-start.3
  71.7 33.1 %all-to-all-start.3 = ((bf16[16,16,16,128]{3,2,1,0:T(8,128)(2,1)}), bf16[16,16,16,128]{3,2,1,0:T(8,128)(2,1)S(1)}, u32[]{:S(2)}, u32[]{:S(2)}) async-start(bf16[16,16,16,128]{3,2,1,0:T(8,128)(2,1)} %broadcast_in_dim.30), calls=%async_computation.3 | async-start | bytes 2097152 | tf_op jit(solution)/shard_map/all_to_all | solution.py:157
  78.2 26.6 %collective-permute-start = (bf16[640,256]{1,0:T(8,128)(2,1)S(1)}, bf16[640,256]{1,0:T(8,128)(2,1)S(1)}, u32[]{:S(2)}, u32[]{:S(2)}) collective-permute-start(bf16[640,256]{1,0:T(8,128)(2,1)S(1)} %bitcast.29), channel_id=1, source_target_pairs={{0,16},{16,32},{32,48},{48,64},{64,80},{80,96},{96,112},{112,128},... | collective-permute-start | bytes 983048 | tf_op jit(solution)/shard_map/ppermute | solution.py:144
  104.8 0.7 copy-start.5
  104.8 1.1 copy-start.1

commit v2 on v1

v2 whole, which is shorter than its diff:
```python
import math

import jax
import jax.numpy as jnp
from jax import lax
from jax.experimental import pallas as pl
from jax.experimental.pallas import tpu as pltpu
from jax.sharding import Mesh, PartitionSpec as P


QUERY_HEADS = 64
KEY_VALUE_HEADS = 8
HD = 128
BT = 128
NV = 4
NS = 3
GROUPS = 16
CORES = 2
SLOTS = QUERY_HEADS // GROUPS // CORES
ROWS = 40
SEQ_ROWS = 640
LB = SEQ_ROWS // BT
TOKENS = CORES * SEQ_ROWS
CHIP_WIDE = CORES * SLOTS * HD
WIDE = CHIP_WIDE + 2 * HD
CH = 16
SUB = 16
ALL = ("xl", "za", "zb", "c", "xh", "y")
HEAD = ("xh", "y")
SPLIT = ("c", "xh", "y")
PART = ("xl", "zb", "c")
SCALE = 1.0 / math.sqrt(HD)
NEG = float("-inf")


def attend(meta, here_ref, other_ref, prev_ref, vert_ref, o_ref, qs, win, vk, vv, kc, vc):
    first_block = meta[0]
    core = meta[1]
    wide = SLOTS * HD
    my_lanes = pl.ds(pl.multiple_of(core * wide, wide), wide)
    kv_lanes = slice(CORES * wide, CORES * wide + 2 * HD)
    mine = pl.multiple_of(core * SEQ_ROWS, SEQ_ROWS)
    theirs = pl.multiple_of((1 - core) * SEQ_ROWS, SEQ_ROWS)
    win[0:SEQ_ROWS, :] = prev_ref[...]
    win[pl.ds(SEQ_ROWS + mine, SEQ_ROWS), :] = here_ref[:, kv_lanes]
    win[pl.ds(SEQ_ROWS + theirs, SEQ_ROWS), :] = other_ref[:, kv_lanes]
    qs[pl.ds(mine, SEQ_ROWS), :] = here_ref[:, my_lanes]
    qs[pl.ds(theirs, SEQ_ROWS), :] = other_ref[:, my_lanes]
    causal = lax.broadcasted_iota(jnp.int32, (BT, BT), 0) >= lax.broadcasted_iota(
        jnp.int32, (BT, BT), 1
    )
    for j in range(SLOTS * NV):
        h, n = divmod(j, NV)
        vk[h, n * BT : (n + 1) * BT, :] = vert_ref[0:8, j].reshape(BT, HD)
        vv[h, n * BT : (n + 1) * BT, :] = vert_ref[8:16, j].reshape(BT, HD)

    def unit(step, carry):
        h = step // CORES
        half = step % CORES
        lane = pl.ds(pl.multiple_of(h * HD, HD), HD)
        offs = [meta[2 + SLOTS * NV + h * NS + n] for n in range(NS)]
        verts = [meta[2 + h * NV + n] for n in range(NV)]
        for i in range(LB):
            local = half * LB + i
            block = first_block + local
            good = []
            for n in range(NS):
                at = pl.ds(pl.multiple_of((LB + local - offs[n]) * BT, BT), BT)
                rows = slice(n * BT, (n + 1) * BT)
                kc[i, rows, :] = win[at, 0:HD]
                vc[i, rows, :] = win[at, HD : 2 * HD]
                good.append(block - offs[n] >= 0)
            for n in range(NV):
                ok = verts[n] <= block
                for o in offs:
                    ok = ok & (block - verts[n] != o)
                for e in range(n):
                    ok = ok & (verts[n] != verts[e])
                good.append(ok)
            rows = pl.ds(pl.multiple_of(local * BT, BT), BT)
            q = qs[rows, lane]
            dims = (((1,), (1,)), ((), ()))
            near = lax.dot_general(q, kc[i], dims, preferred_element_type=jnp.float32) * SCALE
            far = lax.dot_general(q, vk[h], dims, preferred_element_type=jnp.float32) * SCALE
            parts = [jnp.where(causal, near[:, 0:BT], NEG)]
            for n in range(1, NS):
                parts.append(near[:, n * BT : (n + 1) * BT] + jnp.where(good[n], 0.0, NEG))
            for n in range(NV):
                parts.append(far[:, n * BT : (n + 1) * BT] + jnp.where(good[NS + n], 0.0, NEG))
            top = parts[0]
            for x in parts[1:]:
                top = jnp.maximum(top, x)
            top = jnp.max(top, axis=1, keepdims=True)
            ws = [jnp.exp(x - top) for x in parts]
            total = ws[0]
            for x in ws[1:]:
                total = total + x
            total = jnp.sum(total, axis=1, keepdims=True)
            ws = [x.astype(jnp.bfloat16) for x in ws]
            acc = jnp.dot(
                jnp.concatenate(ws[:NS], axis=1), vc[i], preferred_element_type=jnp.float32
            ) + jnp.dot(jnp.concatenate(ws[NS:], axis=1), vv[h], preferred_element_type=jnp.float32)
            o_ref[rows, lane] = (acc / total).astype(jnp.bfloat16)
        return carry

    lax.fori_loop(0, SLOTS * CORES, unit, 0)


def attention(meta, here, other, prev, vert):
    vm = pl.BlockSpec(memory_space=pltpu.VMEM)
    return pl.pallas_call(
        attend,
        out_shape=jax.ShapeDtypeStruct((TOKENS, SLOTS * HD), jnp.bfloat16),
        in_specs=[pl.BlockSpec(memory_space=pltpu.SMEM), vm, vm, vm, vm],
        out_specs=vm,
        scratch_shapes=[
            pltpu.VMEM((TOKENS, SLOTS * HD), jnp.bfloat16),
            pltpu.VMEM((TOKENS + SEQ_ROWS, 2 * HD), jnp.bfloat16),
            pltpu.VMEM((SLOTS, NV * BT, HD), jnp.bfloat16),
            pltpu.VMEM((SLOTS, NV * BT, HD), jnp.bfloat16),
            pltpu.VMEM((LB, NS * BT, HD), jnp.bfloat16),
            pltpu.VMEM((LB, NS * BT, HD), jnp.bfloat16),
        ],
        name="attend",
    )(meta, here, other, prev, vert)


def lay_out(q_ref, k_ref, v_ref, o_ref):
    for g in range(GROUPS):
        m = g // (GROUPS // KEY_VALUE_HEADS)
        o_ref[g, :, 0:CHIP_WIDE] = q_ref[:, g * CHIP_WIDE : (g + 1) * CHIP_WIDE]
        o_ref[g, :, CHIP_WIDE : CHIP_WIDE + HD] = k_ref[:, m * HD : (m + 1) * HD]
        o_ref[g, :, CHIP_WIDE + HD : WIDE] = v_ref[:, m * HD : (m + 1) * HD]


def pack(q, k, v):
    vm = pl.BlockSpec(memory_space=pltpu.VMEM)
    return pl.pallas_call(
        lay_out,
        out_shape=jax.ShapeDtypeStruct((GROUPS, ROWS, WIDE), jnp.bfloat16),
        in_specs=[vm, vm, vm],
        out_specs=vm,
        name="lay_out",
    )(q, k, v)


def to_slots(assign, x_ref, o_ref):
    for k in range(QUERY_HEADS):
        a = assign[k]
        source = (a // SLOTS % CORES) * GROUPS + a // (SLOTS * CORES)
        lane = pl.ds(pl.multiple_of((a % SLOTS) * HD, HD), HD)
        o_ref[:, k * HD : (k + 1) * HD] = x_ref[source, :, lane]


def place_slots(assign, x):
    vm = pl.BlockSpec(memory_space=pltpu.VMEM)
    return pl.pallas_call(
        to_slots,
        out_shape=jax.ShapeDtypeStruct((ROWS, QUERY_HEADS * HD), jnp.bfloat16),
        in_specs=[pl.BlockSpec(memory_space=pltpu.SMEM), vm],
        out_specs=vm,
        name="to_slots",
    )(assign, x)


def per_device(q_rows, k_rows, v_rows, group_assign, vertical_blocks, slash_offsets):
    group = lax.axis_index(HEAD)
    core = lax.axis_index("c")
    chip = lax.axis_index(("xl", "za", "zb"))
    za = lax.axis_index("za")
    chip_heads = SLOTS * CORES
    verts = lax.dynamic_slice_in_dim(vertical_blocks, group * chip_heads, chip_heads).reshape(-1)
    my_head = group * chip_heads + core * SLOTS
    my_verts = lax.dynamic_slice_in_dim(vertical_blocks, my_head, SLOTS).reshape(-1)
    my_offs = lax.dynamic_slice_in_dim(slash_offsets, my_head, SLOTS).reshape(-1)

    sent = pack(q_rows, k_rows, v_rows)
    here = lax.all_to_all(sent, HEAD, 0, 0, tiled=True).reshape(SEQ_ROWS, WIDE)
    kv_here = here[:, CHIP_WIDE:]

    chunks = jnp.transpose(kv_here.reshape(LB, 8, CH, 2, HD), (3, 1, 0, 2, 4))
    held = lax.all_to_all(chunks.reshape(SUB, LB, CH, HD), PART, 0, 0, tiled=True)

    owner = verts // LB
    z = (owner % 24) // 2
    spot = ((owner // 24) * 8 + (z % 4) * 2 + owner % 2) * LB + verts % LB
    mine = (z // 4 == za)[:, None, None]
    chosen = jnp.where(mine, held.reshape(SUB * LB, CH, HD)[spot], jnp.bfloat16(0))
    slots = SLOTS * NV
    chosen = jnp.broadcast_to(
        chosen.reshape(1, CORES, slots, CH, HD), (3, CORES, slots, CH, HD)
    ).reshape(3 * CORES, slots, CH, HD)
    joined = lax.all_to_all(chosen, ("za", "c"), 0, 0, tiled=True)
    joined = joined.reshape(3, CORES, slots, CH, HD)
    joined = joined[0] + joined[1] + joined[2]
    spread = jnp.broadcast_to(joined[None], (8, CORES, slots, CH, HD))
    vert = lax.all_to_all(spread, ("xl", "zb"), 0, 0, tiled=True)

    other = lax.ppermute(here, "c", [(0, 1), (1, 0)])
    gated, _ = lax.optimization_barrier((other[:, CHIP_WIDE:], held))
    last = jnp.where(core == 1, kv_here, gated)
    kv_before = lax.ppermute(last, ("xl", "za", "zb"), [(i, i + 1) for i in range(23)])

    meta = jnp.concatenate(
        [jnp.stack([chip * CORES * LB, core]).astype(jnp.int32), my_verts, my_offs]
    )
    out = attention(meta, here, other, kv_before, vert.reshape(SUB, slots, CH, HD))
    back = lax.all_to_all(
        out.reshape(CORES * GROUPS, ROWS, SLOTS * HD), SPLIT, 0, 0, tiled=True
    )
    return place_slots(group_assign, back)


def solution(mesh):
    fine = Mesh(mesh.devices.reshape(2, 3, 4, 2, 2, 8), ALL)
    rows = P(ALL, None)
    return jax.shard_map(
        per_device,
        mesh=fine,
        in_specs=(rows, rows, rows, P(), P(), P()),
        out_specs=rows,
        check_vma=False,
    )
```

time: 149 us -> 148 us (level)
  the two profiles are of different devices: /device:TPU:65 before, /device:TPU:137 now
where the time goes in v2:
time: 148 us
  blocking collectives  61.6 us (42%)
  starting transfers between devices  33.9 us (23%)
  waiting for transfers between devices  29.5 us (20%)
  Pallas kernels  15.4 us (10%)
  local copies, waits for them, and re-layouts  6.14 us (4%)
    all_to_all x1, blocking collectives, per_device(): here = lax.all_to_all(sent, HEAD, 0, 0, tiled=True).reshape(SEQ_ROWS, WIDE)  34.1 us
    all_to_all x1, blocking collectives, per_device(): lax.all_to_all(out.reshape(CORES * GROUPS, ROWS, SLOTS * HD), SPLIT, 0, 0...  27.4 us
    ppermute x1, waiting for transfers between devices, per_device(): lax.ppermute(last, ('xl', 'za', 'zb'), [(i, i + 1) for i in range(23)])  15.4 us
    all_to_all x1, starting transfers between devices, per_device(): joined = lax.all_to_all(chosen, ('za', 'c'), 0, 0, tiled=True)  11.6 us
    pallas_call x1, Pallas kernels, attention(): pl.pallas_call(attend, out_shape=jax.ShapeDtypeStruct((TOKENS, SLOTS * HD...  10.4 us
    all_to_all x1, starting transfers between devices, per_device(): lax.all_to_all(chunks.reshape(SUB, LB, CH, HD), PART, 0, 0, tiled=True)  8.7 us
    all_to_all x1, starting transfers between devices, per_device(): vert = lax.all_to_all(spread, ('xl', 'zb'), 0, 0, tiled=True)  8.53 us
    all_to_all x1, waiting for transfers between devices, per_device(): joined = lax.all_to_all(chosen, ('za', 'c'), 0, 0, tiled=True)  7.31 us
  transfers between devices with their start and end apart: 5, of which 3 were waited for; matrix products, arithmetic and copies ran while one was open for 2% of the time, Pallas kernels for 0%

profile of v2, /device:TPU:137, one launch (start us, length us, event | category | flops | bytes accessed | tf_op | source)
XLA Modules:
  0.0 147.6 jit_solution(11858060841811074113)
XLA Ops:
  0.0 2.2 %lay_out.1 = bf16[16,40,768]{2,1,0:T(8,128)(2,1)} custom-call(bf16[40,8192]{1,0:T(8,128)(2,1)} %q_ref.1, bf16[40,1024]{1,0:T(8,128)(2,1)} %k_ref.1, bf16[40,1024]{1,0:T(8,128)(2,1)} %v_ref.1), custom_call_target="tpu_custom_call" | custom-call | tf_op jit(solution)/shard_map/lay_out/pallas_call | solution.py:138
  2.2 34.1 %all_to_all.25 = bf16[16,40,768]{2,1,0:T(8,128)(2,1)S(1)} all-to-all(bf16[16,40,768]{2,1,0:T(8,128)(2,1)} %lay_out.1), channel_id=1, replica_groups=mesh['xl'=2,'za'=3,'zb'=4,'c'=2,'xh'=2,'y'=8] {'xh','y'}, dimensions={0} | all-to-all | bytes 1966080 | tf_op jit(solution)/shard_map/all_to_all | solution.py:178
  36.4 0.9 copy.16
  37.3 8.7 %all-to-all-start.1 = ((bf16[16,5,16,128]{3,2,1,0:T(8,128)(2,1)}), bf16[16,5,16,128]{3,2,1,0:T(8,128)(2,1)S(1)}, u32[]{:S(2)}, u32[]{:S(2)}) async-start(bf16[16,5,16,128]{3,2,1,0:T(8,128)(2,1)} %bitcast.4), calls=%async_computation.1 | async-start | bytes 655360 | tf_op jit(solution)/shard_map/all_to_all | solution.py:182
  46.1 0.7 copy-done.5
  46.8 0.1 copy.18
  46.9 0.1 div.67
  47.2 0.1 copy.17
  47.3 0.1 and.137
  47.4 0.1 copy.19
  47.5 0.1 ne.196
  47.6 0.1 copy.20
  47.6 0.1 rem.149
  47.8 6.9 %all-to-all-done.1 = bf16[16,5,16,128]{3,2,1,0:T(8,128)(2,1)S(1)} async-done(((bf16[16,5,16,128]{3,2,1,0:T(8,128)(2,1)}), bf16[16,5,16,128]{3,2,1,0:T(8,128)(2,1)S(1)}, u32[]{:S(2)}, u32[]{:S(2)}) %all-to-all-start.1) | async-done | bytes 327712 | tf_op jit(solution)/shard_map/all_to_all | solution.py:182
  54.7 0.6 gather_fusion
  55.3 0.1 broadcast_select_fusion.1
  55.4 0.7 broadcast_in_dim.27
  56.1 11.6 %all-to-all-start.2 = ((bf16[6,8,16,128]{3,2,1,0:T(8,128)(2,1)}), bf16[6,8,16,128]{3,2,1,0:T(8,128)(2,1)S(1)}, u32[]{:S(2)}, u32[]{:S(2)}) async-start(bf16[6,8,16,128]{3,2,1,0:T(8,128)(2,1)} %bitcast.8), calls=%async_computation.2 | async-start | bytes 393216 | tf_op jit(solution)/shard_map/all_to_all | solution.py:193
  67.7 1.9 %collective-permute-start = (bf16[640,768]{1,0:T(8,128)(2,1)S(1)}, bf16[640,768]{1,0:T(8,128)(2,1)S(1)}, u32[]{:S(2)}, u32[]{:S(2)}) collective-permute-start(bf16[640,768]{1,0:T(8,128)(2,1)S(1)} %bitcast.14), channel_id=1, source_target_pairs={{0,16},{16,0},{1,17},{17,1},{2,18},{18,2},{3,19},{19,3},{4,20},{20... | collective-permute-start | bytes 2949128 | tf_op jit(solution)/shard_map/ppermute | solution.py:199
  69.6 7.3 %all-to-all-done.2 = bf16[6,8,16,128]{3,2,1,0:T(8,128)(2,1)S(1)} async-done(((bf16[6,8,16,128]{3,2,1,0:T(8,128)(2,1)}), bf16[6,8,16,128]{3,2,1,0:T(8,128)(2,1)S(1)}, u32[]{:S(2)}, u32[]{:S(2)}) %all-to-all-start.2) | async-done | bytes 196640 | tf_op jit(solution)/shard_map/all_to_all | solution.py:193
  76.9 0.9 broadcast_in_dim.28
  77.8 8.5 %all-to-all-start.3 = ((bf16[8,2,8,16,128]{4,3,2,1,0:T(8,128)(2,1)}), bf16[8,2,8,16,128]{4,3,2,1,0:T(8,128)(2,1)S(1)}, u32[]{:S(2)}, u32[]{:S(2)}) async-start(bf16[8,2,8,16,128]{4,3,2,1,0:T(8,128)(2,1)} %broadcast_in_dim.28), calls=%async_computation.3 | async-start | bytes 1048576 | tf_op jit(solution)/shard_map/all_to_all | solution.py:197
  86.4 3.1 %collective-permute-start.1 = (bf16[640,256]{1,0:T(8,128)(2,1)S(1)}, bf16[640,256]{1,0:T(8,128)(2,1)S(1)}, u32[]{:S(2)}, u32[]{:S(2)}) collective-permute-start(bf16[640,256]{1,0:T(8,128)(2,1)S(1)} %broadcast_select_fusion), channel_id=1, source_target_pairs={{0,32},{32,64},{64,96},{96,128},{128,160},{160,192},{192,224},{224... | collective-permute-start | bytes 983048 | tf_op jit(solution)/shard_map/ppermute | solution.py:202
  89.6 0.1 copy.15
  89.9 0.1 copy.14
  90.1 0.7 pad_add_fusion.meta
  90.7 15.4 %collective-permute-done.1.prev_ref = bf16[640,256]{1,0:T(8,128)(2,1)S(1)} collective-permute-done((bf16[640,256]{1,0:T(8,128)(2,1)S(1)}, bf16[640,256]{1,0:T(8,128)(2,1)S(1)}, u32[]{:S(2)}, u32[]{:S(2)}) %collective-permute-start.1) | collective-permute-done | bytes 327712 | tf_op jit(solution)/shard_map/ppermute | solution.py:202
  106.1 0.7 copy-done.4
  106.8 0.2 copy-done.2
  107.0 10.4 %attend.1 = bf16[1280,256]{1,0:T(8,128)(2,1)} custom-call(s32[16]{0:T(128)} %pad_add_fusion.meta, bf16[640,768]{1,0:T(8,128)(2,1)} %bitcast.16, bf16[640,768]{1,0:T(8,128)(2,1)} %copy-done.3, bf16[640,256]{1,0:T(8,128)(2,1)} %copy-done.4, bf16[16,8,16,128]{3,2,1,0:T(8,128)(2,1)} %bitcast.18), custom_call_target="tpu_custom_call" | custom-call | tf_op jit(solution)/shard_map/attend/pallas_call | solution.py:111
  117.4 27.4 %all_to_all.26.x_ref = bf16[32,40,256]{2,1,0:T(8,128)(2,1)} all-to-all(bf16[32,40,256]{2,1,0:T(8,128)(2,1)} %bitcast.17), channel_id=1, replica_groups=mesh['xl'=2,'za'=3,'zb'=4,'c'=2,'xh'=2,'y'=8] {'c','xh','y'}, dimensions={0} | all-to-all | bytes 1310720 | tf_op jit(solution)/shard_map/all_to_all | solution.py:208
  144.8 2.8 %to_slots.1 = bf16[40,8192]{1,0:T(8,128)(2,1)} custom-call(s32[64]{0:T(128)} %assign.1, bf16[32,40,256]{2,1,0:T(8,128)(2,1)} %all_to_all.26.x_ref), custom_call_target="tpu_custom_call" | custom-call | tf_op jit(solution)/shard_map/to_slots/pallas_call | solution.py:157
  (26 shorter events, 0.8 us)
Async XLA Ops:
  0.0 89.5 %copy-start = (s32[64,3]{0,1:T(4,128)S(1)}, s32[64,3]{0,1:T(4,128)}, u32[]{:S(2)}) copy-start(s32[64,3]{0,1:T(4,128)} %param.11) | copy-start | bytes 2308
  36.3 50.1 %copy-start.1 = (bf16[16,40,768]{2,1,0:T(8,128)(2,1)}, bf16[16,40,768]{2,1,0:T(8,128)(2,1)S(1)}, u32[]{:S(2)}) copy-start(bf16[16,40,768]{2,1,0:T(8,128)(2,1)S(1)} %all_to_all.25) | copy-start | bytes 2949124
  37.3 17.3 %all-to-all-start.1 = ((bf16[16,5,16,128]{3,2,1,0:T(8,128)(2,1)}), bf16[16,5,16,128]{3,2,1,0:T(8,128)(2,1)S(1)}, u32[]{:S(2)}, u32[]{:S(2)}) async-start(bf16[16,5,16,128]{3,2,1,0:T(8,128)(2,1)} %bitcast.4), calls=%async_computation.1 | async-start | bytes 655360 | tf_op jit(solution)/shard_map/all_to_all | solution.py:182
  46.0 0.7 copy-start.5
  56.1 20.8 %all-to-all-start.2 = ((bf16[6,8,16,128]{3,2,1,0:T(8,128)(2,1)}), bf16[6,8,16,128]{3,2,1,0:T(8,128)(2,1)S(1)}, u32[]{:S(2)}, u32[]{:S(2)}) async-start(bf16[6,8,16,128]{3,2,1,0:T(8,128)(2,1)} %bitcast.8), calls=%async_computation.2 | async-start | bytes 393216 | tf_op jit(solution)/shard_map/all_to_all | solution.py:193
  67.7 18.7 %collective-permute-start = (bf16[640,768]{1,0:T(8,128)(2,1)S(1)}, bf16[640,768]{1,0:T(8,128)(2,1)S(1)}, u32[]{:S(2)}, u32[]{:S(2)}) collective-permute-start(bf16[640,768]{1,0:T(8,128)(2,1)S(1)} %bitcast.14), channel_id=1, source_target_pairs={{0,16},{16,0},{1,17},{17,1},{2,18},{18,2},{3,19},{19,3},{4,20},{20... | collective-permute-start | bytes 2949128 | tf_op jit(solution)/shard_map/ppermute | solution.py:199
  77.8 28.3 %all-to-all-start.3 = ((bf16[8,2,8,16,128]{4,3,2,1,0:T(8,128)(2,1)}), bf16[8,2,8,16,128]{4,3,2,1,0:T(8,128)(2,1)S(1)}, u32[]{:S(2)}, u32[]{:S(2)}) async-start(bf16[8,2,8,16,128]{4,3,2,1,0:T(8,128)(2,1)} %broadcast_in_dim.28), calls=%async_computation.3 | async-start | bytes 1048576 | tf_op jit(solution)/shard_map/all_to_all | solution.py:197
  86.3 19.8 %copy-start.3 = (bf16[640,768]{1,0:T(8,128)(2,1)}, bf16[640,768]{1,0:T(8,128)(2,1)S(1)}, u32[]{:S(2)}) copy-start(bf16[640,768]{1,0:T(8,128)(2,1)S(1)} %collective-permute-done.other_ref) | copy-start | bytes 2949124
  86.4 19.7 %collective-permute-start.1 = (bf16[640,256]{1,0:T(8,128)(2,1)S(1)}, bf16[640,256]{1,0:T(8,128)(2,1)S(1)}, u32[]{:S(2)}, u32[]{:S(2)}) collective-permute-start(bf16[640,256]{1,0:T(8,128)(2,1)S(1)} %broadcast_select_fusion), channel_id=1, source_target_pairs={{0,32},{32,64},{64,96},{96,128},{128,160},{160,192},{192,224},{224... | collective-permute-start | bytes 983048 | tf_op jit(solution)/shard_map/ppermute | solution.py:202
  106.1 0.7 copy-start.4
  106.1 0.9 copy-start.2

commit v3 on v2

v3 whole, which is shorter than its diff:
```python
import math

import jax
import jax.numpy as jnp
from jax import lax
from jax.experimental import pallas as pl
from jax.experimental.pallas import tpu as pltpu
from jax.sharding import Mesh, PartitionSpec as P


QUERY_HEADS = 64
KEY_VALUE_HEADS = 8
HD = 128
BT = 128
NV = 4
NS = 3
GROUPS = 16
CORES = 2
SLOTS = QUERY_HEADS // GROUPS // CORES
ROWS = 40
SEQ_ROWS = 640
LB = SEQ_ROWS // BT
TOKENS = CORES * SEQ_ROWS
CHIP_WIDE = CORES * SLOTS * HD
WIDE = CHIP_WIDE + 2 * HD
CHIP_SLOTS = CORES * SLOTS * NV
CH = 16
SUB = 16
ALL = ("xl", "za", "zb", "c", "xh", "y")
HEAD = ("xh", "y")
SPLIT = ("c", "xh", "y")
PART = ("xl", "zb", "c")
SCALE = 1.0 / math.sqrt(HD)
NEG = float("-inf")
SMALL = 4 * 1024 * 1024
PAIR = 2
LARGE = 12 * 1024 * 1024


LOG2E_SCALE = SCALE * math.log2(math.e)
DIMS = (((1,), (1,)), ((), ()))


def in_vmem(x):
    return pltpu.with_memory_space_constraint(x, pltpu.VMEM)


def in_hbm(x):
    return pltpu.with_memory_space_constraint(x, pltpu.HBM)


def near_part(meta, here_ref, other_ref, prev_ref, acc_ref, stat_ref, q_ref, win, kc, vc):
    first_block = meta[0]
    core = meta[1]
    wide = SLOTS * HD
    my_lanes = pl.ds(pl.multiple_of(core * wide, wide), wide)
    kv_lanes = slice(CORES * wide, CORES * wide + 2 * HD)
    mine = pl.multiple_of(core * SEQ_ROWS, SEQ_ROWS)
    theirs = pl.multiple_of((1 - core) * SEQ_ROWS, SEQ_ROWS)
    win[0:SEQ_ROWS, :] = prev_ref[...]
    win[pl.ds(SEQ_ROWS + mine, SEQ_ROWS), :] = here_ref[:, kv_lanes]
    win[pl.ds(SEQ_ROWS + theirs, SEQ_ROWS), :] = other_ref[:, kv_lanes]
    q_ref[pl.ds(mine, SEQ_ROWS), :] = here_ref[:, my_lanes]
    q_ref[pl.ds(theirs, SEQ_ROWS), :] = other_ref[:, my_lanes]
    causal = lax.broadcasted_iota(jnp.int32, (BT, BT), 0) >= lax.broadcasted_iota(
        jnp.int32, (BT, BT), 1
    )

    def unit(step, carry):
        for i in range(PAIR * SLOTS):
            h = i % SLOTS
            local = step * PAIR + i // SLOTS
            lane = slice(h * HD, (h + 1) * HD)
            offs = [meta[2 + SLOTS * NV + h * NS + n] for n in range(NS)]
            good = []
            for n in range(NS):
                at = pl.ds(pl.multiple_of((LB + local - offs[n]) * BT, BT), BT)
                rows = slice(n * BT, (n + 1) * BT)
                kc[i, rows, :] = win[at, 0:HD]
                vc[i, rows, :] = win[at, HD : 2 * HD]
                good.append(first_block + local - offs[n] >= 0)
            rows = pl.ds(pl.multiple_of(local * BT, BT), BT)
            s = lax.dot_general(q_ref[rows, lane], kc[i], DIMS, preferred_element_type=jnp.float32)
            parts = [jnp.where(causal, s[:, 0:BT], NEG)]
            for n in range(1, NS):
                parts.append(s[:, n * BT : (n + 1) * BT] + jnp.where(good[n], 0.0, NEG))
            top = jnp.maximum(jnp.maximum(parts[0], parts[1]), parts[2])
            top = jnp.max(top, axis=1, keepdims=True)
            ws = [jnp.exp2((x - top) * LOG2E_SCALE) for x in parts]
            total = jnp.sum(ws[0] + ws[1] + ws[2], axis=1, keepdims=True)
            w = jnp.concatenate([x.astype(jnp.bfloat16) for x in ws], axis=1)
            acc_ref[rows, lane] = jnp.dot(w, vc[i], preferred_element_type=jnp.float32)
            stat_ref[rows, 2 * h : 2 * h + 1] = top
            stat_ref[rows, 2 * h + 1 : 2 * h + 2] = total
        return carry

    lax.fori_loop(0, TOKENS // BT // PAIR, unit, 0)


def near(meta, here, other, prev):
    vm = pl.BlockSpec(memory_space=pltpu.VMEM)
    return pl.pallas_call(
        near_part,
        out_shape=(
            jax.ShapeDtypeStruct((TOKENS, SLOTS * HD), jnp.float32),
            pltpu.VMEM((TOKENS, HD), jnp.float32),
            pltpu.VMEM((TOKENS, SLOTS * HD), jnp.bfloat16),
        ),
        in_specs=[pl.BlockSpec(memory_space=pltpu.SMEM), vm, vm, vm],
        out_specs=(vm, vm, vm),
        scratch_shapes=[
            pltpu.VMEM((TOKENS + SEQ_ROWS, 2 * HD), jnp.bfloat16),
            pltpu.VMEM((PAIR * SLOTS, NS * BT, HD), jnp.bfloat16),
            pltpu.VMEM((PAIR * SLOTS, NS * BT, HD), jnp.bfloat16),
        ],
        name="near",
        compiler_params=pltpu.CompilerParams(vmem_limit_bytes=LARGE),
    )(meta, in_vmem(here), in_vmem(other), in_vmem(prev))


def far_part(meta, q_ref, acc_hbm, stat_ref, vert_ref, o_ref, acc_ref, vk, vv, sems):
    first_block = meta[0]
    steps = TOKENS // BT // PAIR

    def fetch(step):
        rows = pl.ds(pl.multiple_of(step * PAIR * BT, PAIR * BT), PAIR * BT)
        return pltpu.make_async_copy(acc_hbm.at[rows], acc_ref.at[rows], sems.at[step])

    for step in range(steps):
        fetch(step).start()
    for j in range(SLOTS * NV):
        h, n = divmod(j, NV)
        vk[h, n * BT : (n + 1) * BT, :] = vert_ref[0:8, j].reshape(BT, HD)
        vv[h, n * BT : (n + 1) * BT, :] = vert_ref[8:16, j].reshape(BT, HD)

    def unit(step, carry):
        fetch(step).wait()
        for i in range(PAIR * SLOTS):
            h = i % SLOTS
            local = step * PAIR + i // SLOTS
            lane = slice(h * HD, (h + 1) * HD)
            offs = [meta[2 + SLOTS * NV + h * NS + n] for n in range(NS)]
            verts = [meta[2 + h * NV + n] for n in range(NV)]
            block = first_block + local
            rows = pl.ds(pl.multiple_of(local * BT, BT), BT)
            s = lax.dot_general(q_ref[rows, lane], vk[h], DIMS, preferred_element_type=jnp.float32)
            parts = []
            for n in range(NV):
                ok = verts[n] <= block
                for o in offs:
                    ok = ok & (block - verts[n] != o)
                for e in range(n):
                    ok = ok & (verts[n] != verts[e])
                parts.append(s[:, n * BT : (n + 1) * BT] + jnp.where(ok, 0.0, NEG))
            old = stat_ref[rows, 2 * h : 2 * h + 1]
            top = jnp.maximum(
                jnp.maximum(parts[0], parts[1]), jnp.maximum(parts[2], parts[3])
            )
            top = jnp.maximum(jnp.max(top, axis=1, keepdims=True), old)
            keep = jnp.exp2((old - top) * LOG2E_SCALE)
            ws = [jnp.exp2((x - top) * LOG2E_SCALE) for x in parts]
            total = jnp.sum((ws[0] + ws[1]) + (ws[2] + ws[3]), axis=1, keepdims=True)
            total = total + stat_ref[rows, 2 * h + 1 : 2 * h + 2] * keep
            w = jnp.concatenate([x.astype(jnp.bfloat16) for x in ws], axis=1)
            acc = acc_ref[rows, lane] * keep + jnp.dot(
                w, vv[h], preferred_element_type=jnp.float32
            )
            o_ref[rows, lane] = (acc / total).astype(jnp.bfloat16)
        return carry

    lax.fori_loop(0, steps, unit, 0)


def far(meta, q, acc, stat, vert):
    vm = pl.BlockSpec(memory_space=pltpu.VMEM)
    return pl.pallas_call(
        far_part,
        out_shape=pltpu.VMEM((TOKENS, SLOTS * HD), jnp.bfloat16),
        in_specs=[
            pl.BlockSpec(memory_space=pltpu.SMEM),
            vm,
            pl.BlockSpec(memory_space=pltpu.HBM),
            vm,
            vm,
        ],
        out_specs=vm,
        scratch_shapes=[
            pltpu.VMEM((TOKENS, SLOTS * HD), jnp.float32),
            pltpu.VMEM((SLOTS, NV * BT, HD), jnp.bfloat16),
            pltpu.VMEM((SLOTS, NV * BT, HD), jnp.bfloat16),
            pltpu.SemaphoreType.DMA((TOKENS // BT // PAIR,)),
        ],
        name="far",
        compiler_params=pltpu.CompilerParams(vmem_limit_bytes=LARGE),
    )(meta, in_vmem(q), in_hbm(acc), in_vmem(stat), in_vmem(vert))


def cut(here_ref, o_ref):
    for j in range(LB):
        for r in range(BT // CH):
            rows = slice(j * BT + r * CH, j * BT + (r + 1) * CH)
            o_ref[r, j] = here_ref[rows, CHIP_WIDE : CHIP_WIDE + HD]
            o_ref[BT // CH + r, j] = here_ref[rows, CHIP_WIDE + HD : WIDE]


def in_chunks(here):
    vm = pl.BlockSpec(memory_space=pltpu.VMEM)
    return pl.pallas_call(
        cut,
        out_shape=pltpu.VMEM((SUB, LB, CH, HD), jnp.bfloat16),
        in_specs=[vm],
        out_specs=vm,
        name="cut",
        compiler_params=pltpu.CompilerParams(vmem_limit_bytes=SMALL),
    )(in_vmem(here))


def newest(core, here_ref, other_ref, o_ref):
    @pl.when(core[0] == 1)
    def _():
        o_ref[...] = here_ref[:, CHIP_WIDE:WIDE]

    @pl.when(core[0] != 1)
    def _():
        o_ref[...] = other_ref[:, CHIP_WIDE:WIDE]


def last_window(core, here, other):
    vm = pl.BlockSpec(memory_space=pltpu.VMEM)
    return pl.pallas_call(
        newest,
        out_shape=pltpu.VMEM((SEQ_ROWS, 2 * HD), jnp.bfloat16),
        in_specs=[pl.BlockSpec(memory_space=pltpu.SMEM), vm, vm],
        out_specs=vm,
        name="newest",
        compiler_params=pltpu.CompilerParams(vmem_limit_bytes=SMALL),
    )(core, in_vmem(here), in_vmem(other))


def choose(spots, held_ref, o_ref):
    for c in range(CORES):
        for j in range(SLOTS * NV):
            at = c * SLOTS * NV + j
            x = held_ref[spots[at]] * jnp.where(spots[CHIP_SLOTS + at] == 1, 1.0, 0.0).astype(
                jnp.bfloat16
            )
            for part in range(3):
                o_ref[part * CORES + c, j] = x


def chosen_chunks(spots, held):
    vm = pl.BlockSpec(memory_space=pltpu.VMEM)
    return pl.pallas_call(
        choose,
        out_shape=pltpu.VMEM((3 * CORES, SLOTS * NV, CH, HD), jnp.bfloat16),
        in_specs=[pl.BlockSpec(memory_space=pltpu.SMEM), vm],
        out_specs=vm,
        name="choose",
        compiler_params=pltpu.CompilerParams(vmem_limit_bytes=SMALL),
    )(spots, in_vmem(held))


def add_up(x_ref, o_ref):
    for c in range(CORES):
        total = x_ref[c] + x_ref[CORES + c] + x_ref[2 * CORES + c]
        for part in range(8):
            o_ref[part, c] = total


def copies_of_sum(x):
    vm = pl.BlockSpec(memory_space=pltpu.VMEM)
    return pl.pallas_call(
        add_up,
        out_shape=jax.ShapeDtypeStruct((8, CORES, SLOTS * NV, CH, HD), jnp.bfloat16),
        in_specs=[vm],
        out_specs=vm,
        name="add_up",
        compiler_params=pltpu.CompilerParams(vmem_limit_bytes=SMALL),
    )(in_vmem(x))


def lay_out(q_ref, k_ref, v_ref, o_ref, sems):
    copies = []
    for g in range(GROUPS):
        m = g // (GROUPS // KEY_VALUE_HEADS) * HD
        for n, (ref, start, at, size) in enumerate(
            (
                (q_ref, g * CHIP_WIDE, 0, CHIP_WIDE),
                (k_ref, m, CHIP_WIDE, HD),
                (v_ref, m, CHIP_WIDE + HD, HD),
            )
        ):
            copies.append(
                pltpu.make_async_copy(
                    ref.at[:, pl.ds(start, size)], o_ref.at[g, :, pl.ds(at, size)], sems.at[n, g]
                )
            )
    for copy in copies:
        copy.start()
    for copy in copies:
        copy.wait()


def pack(q, k, v):
    anywhere = pl.BlockSpec(memory_space=pltpu.HBM)
    return pl.pallas_call(
        lay_out,
        out_shape=pltpu.VMEM((GROUPS, ROWS, WIDE), jnp.bfloat16),
        in_specs=[anywhere] * 3,
        out_specs=pl.BlockSpec(memory_space=pltpu.VMEM),
        scratch_shapes=[pltpu.SemaphoreType.DMA((3, GROUPS))],
        name="lay_out",
        compiler_params=pltpu.CompilerParams(vmem_limit_bytes=SMALL),
    )(in_hbm(q), in_hbm(k), in_hbm(v))


def to_slots(assign, x_ref, o_ref, sems):
    copies = []
    for k in range(QUERY_HEADS):
        a = assign[k]
        source = (a >> 1 & 1) * GROUPS + (a >> 2)
        lane = pl.ds(pl.multiple_of((a & 1) * HD, HD), HD)
        copies.append(
            pltpu.make_async_copy(
                x_ref.at[source, :, lane], o_ref.at[:, pl.ds(k * HD, HD)], sems.at[k]
            )
        )
        copies[-1].start()
    for copy in copies:
        copy.wait()


def place_slots(assign, x):
    return pl.pallas_call(
        to_slots,
        out_shape=jax.ShapeDtypeStruct((ROWS, QUERY_HEADS * HD), jnp.bfloat16),
        in_specs=[
            pl.BlockSpec(memory_space=pltpu.SMEM),
            pl.BlockSpec(memory_space=pltpu.VMEM),
        ],
        out_specs=pl.BlockSpec(memory_space=pl.ANY),
        scratch_shapes=[pltpu.SemaphoreType.DMA((QUERY_HEADS,))],
        name="to_slots",
        compiler_params=pltpu.CompilerParams(vmem_limit_bytes=SMALL),
    )(assign, in_vmem(x))


def per_device(q_rows, k_rows, v_rows, group_assign, vertical_blocks, slash_offsets):
    group = lax.axis_index(HEAD)
    core = lax.axis_index("c")
    chip = lax.axis_index(("xl", "za", "zb"))
    za = lax.axis_index("za")
    chip_heads = SLOTS * CORES
    verts = lax.dynamic_slice_in_dim(vertical_blocks, group * chip_heads, chip_heads).reshape(-1)
    my_head = group * chip_heads + core * SLOTS
    my_verts = lax.dynamic_slice_in_dim(vertical_blocks, my_head, SLOTS).reshape(-1)
    my_offs = lax.dynamic_slice_in_dim(slash_offsets, my_head, SLOTS).reshape(-1)

    sent = pack(q_rows, k_rows, v_rows)
    here = lax.all_to_all(sent, HEAD, 0, 0, tiled=True).reshape(SEQ_ROWS, WIDE)
    held = lax.all_to_all(in_chunks(here), PART, 0, 0, tiled=True)

    other = lax.ppermute(here, "c", [(0, 1), (1, 0)])
    last = last_window(core.reshape(1), here, other)
    kv_before = lax.ppermute(last, ("xl", "za", "zb"), [(i, i + 1) for i in range(23)])
    meta = jnp.concatenate(
        [jnp.stack([chip * CORES * LB, core]).astype(jnp.int32), my_verts, my_offs]
    )

    owner = verts // LB
    z = (owner % 24) // 2
    spot = ((owner // 24) * 8 + (z % 4) * 2 + owner % 2) * LB + verts % LB
    spots = jnp.concatenate([spot, (z // 4 == za).astype(jnp.int32)])
    chosen = chosen_chunks(spots, held.reshape(SUB * LB, CH, HD))
    joined = lax.all_to_all(chosen, ("za", "c"), 0, 0, tiled=True)
    spread = copies_of_sum(joined)
    vert = lax.all_to_all(spread, ("xl", "zb"), 0, 0, tiled=True)
    slots = SLOTS * NV
    acc, stat, q_here = near(meta, here, other, kv_before)
    out = far(meta, q_here, acc, stat, vert.reshape(SUB, slots, CH, HD))
    back = lax.all_to_all(
        out.reshape(CORES * GROUPS, ROWS, SLOTS * HD), SPLIT, 0, 0, tiled=True
    )
    return place_slots(group_assign, back)


def solution(mesh):
    fine = Mesh(mesh.devices.reshape(2, 3, 4, 2, 2, 8), ALL)
    rows = P(ALL, None)
    return jax.shard_map(
        per_device,
        mesh=fine,
        in_specs=(rows, rows, rows, P(), P(), P()),
        out_specs=rows,
        check_vma=False,
    )
```

time: 148 us -> 155 us (1.047)
  the two profiles are of different devices: /device:TPU:137 before, /device:TPU:10 now
where the time goes in v3:
time: 155 us; the launch traced here: 154 us
  blocking collectives  85.5 us (55%)
  waiting for transfers between devices  23.3 us (15%)
  Pallas kernels  22.2 us (14%)
  starting transfers between devices  19 us (12%)
  local copies, waits for them, and re-layouts  4.07 us (3%)
    all_to_all x1, blocking collectives, per_device(): here = lax.all_to_all(sent, HEAD, 0, 0, tiled=True).reshape(SEQ_ROWS, WIDE)  35.4 us
    all_to_all x1, blocking collectives, per_device(): lax.all_to_all(out.reshape(CORES * GROUPS, ROWS, SLOTS * HD), SPLIT, 0, 0...  26.6 us
    all_to_all x1, blocking collectives, per_device(): joined = lax.all_to_all(chosen, ('za', 'c'), 0, 0, tiled=True)  23.5 us
    ppermute x1, waiting for transfers between devices, per_device(): lax.ppermute(last, ('xl', 'za', 'zb'), [(i, i + 1) for i in range(23)])  12 us
    pallas_call x1, Pallas kernels, far(): pl.pallas_call(far_part, out_shape=pltpu.VMEM((TOKENS, SLOTS * HD), jnp.b...  9.54 us
    all_to_all x1, waiting for transfers between devices, per_device(): held = lax.all_to_all(in_chunks(here), PART, 0, 0, tiled=True)  8.84 us
    all_to_all x1, starting transfers between devices, per_device(): held = lax.all_to_all(in_chunks(here), PART, 0, 0, tiled=True)  8.74 us
    pallas_call x1, Pallas kernels, near(): pl.pallas_call(near_part, out_shape=(jax.ShapeDtypeStruct((TOKENS, SLOTS...  6.72 us
  transfers between devices with their start and end apart: 4, of which 3 were waited for; matrix products, arithmetic and copies ran while one was open for 1% of the time, Pallas kernels for 4%

profile of v3, /device:TPU:10, one launch (start us, length us, event | category | flops | bytes accessed | tf_op | source)
XLA Modules:
  0.0 154.5 jit_solution(11078106933219980102)
XLA Ops:
  0.0 1.6 %lay_out.1 = bf16[16,40,768]{2,1,0:T(8,128)(2,1)S(1)} custom-call(bf16[40,8192]{1,0:T(8,128)(2,1)} %q_ref.1, bf16[40,1024]{1,0:T(8,128)(2,1)} %k_ref.1, bf16[40,1024]{1,0:T(8,128)(2,1)} %v_ref.1), custom_call_target="tpu_custom_call" | custom-call | tf_op jit(solution)/shard_map/lay_out/pallas_call | solution.py:306
  1.7 35.4 %all_to_all.25 = bf16[16,40,768]{2,1,0:T(8,128)(2,1)S(1)} all-to-all(bf16[16,40,768]{2,1,0:T(8,128)(2,1)S(1)} %lay_out.1), channel_id=1, replica_groups=mesh['xl'=2,'za'=3,'zb'=4,'c'=2,'xh'=2,'y'=8] {'xh','y'}, dimensions={0} | all-to-all | bytes 1966080 | tf_op jit(solution)/shard_map/all_to_all | solution.py:360
  37.1 0.8 cut.1
  37.8 8.7 %all-to-all-start.1 = ((bf16[16,5,16,128]{3,2,1,0:T(8,128)(2,1)}), bf16[16,5,16,128]{3,2,1,0:T(8,128)(2,1)S(1)}, u32[]{:S(2)}, u32[]{:S(2)}) async-start(bf16[16,5,16,128]{3,2,1,0:T(8,128)(2,1)} %cut.1), calls=%async_computation.1 | async-start | bytes 655360 | tf_op jit(solution)/shard_map/all_to_all | solution.py:361
  46.6 0.1 dynamic-slice_divide_fusion
  46.7 0.1 copy.11
  46.8 0.1 div.30
  46.9 0.1 copy.10
  47.0 0.1 rem.77
  47.1 0.1 copy.9
  47.2 0.1 ne.57
  47.4 8.8 %all-to-all-done.1 = bf16[16,5,16,128]{3,2,1,0:T(8,128)(2,1)S(1)} async-done(((bf16[16,5,16,128]{3,2,1,0:T(8,128)(2,1)}), bf16[16,5,16,128]{3,2,1,0:T(8,128)(2,1)S(1)}, u32[]{:S(2)}, u32[]{:S(2)}) %all-to-all-start.1) | async-done | bytes 327712 | tf_op jit(solution)/shard_map/all_to_all | solution.py:361
  56.3 0.6 choose.1
  56.9 23.5 %all_to_all.26.x_ref = bf16[6,8,16,128]{3,2,1,0:T(8,128)(2,1)S(1)} all-to-all(bf16[6,8,16,128]{3,2,1,0:T(8,128)(2,1)S(1)} %choose.1), channel_id=1, replica_groups=mesh['xl'=2,'za'=3,'zb'=4,'c'=2,'xh'=2,'y'=8] {'za','c'}, dimensions={0} | all-to-all | bytes 393216 | tf_op jit(solution)/shard_map/all_to_all | solution.py:375
  80.4 0.9 add_up.1
  81.3 4.9 %all-to-all-start.3 = ((bf16[8,2,8,16,128]{4,3,2,1,0:T(8,128)(2,1)}), bf16[8,2,8,16,128]{4,3,2,1,0:T(8,128)(2,1)S(1)}, u32[]{:S(2)}, u32[]{:S(2)}) async-start(bf16[8,2,8,16,128]{4,3,2,1,0:T(8,128)(2,1)} %add_up.1), calls=%async_computation.3 | async-start | bytes 1048576 | tf_op jit(solution)/shard_map/all_to_all | solution.py:377
  86.2 1.9 %collective-permute-start = (bf16[640,768]{1,0:T(8,128)(2,1)S(1)}, bf16[640,768]{1,0:T(8,128)(2,1)S(1)}, u32[]{:S(2)}, u32[]{:S(2)}) collective-permute-start(bf16[640,768]{1,0:T(8,128)(2,1)S(1)} %bitcast.7), channel_id=1, source_target_pairs={{0,16},{16,0},{1,17},{17,1},{2,18},{18,2},{3,19},{19,3},{4,20},{20... | collective-permute-start | bytes 2949128 | tf_op jit(solution)/shard_map/ppermute | solution.py:363
  88.1 2.5 %collective-permute-done.other_ref = bf16[640,768]{1,0:T(8,128)(2,1)S(1)} collective-permute-done((bf16[640,768]{1,0:T(8,128)(2,1)S(1)}, bf16[640,768]{1,0:T(8,128)(2,1)S(1)}, u32[]{:S(2)}, u32[]{:S(2)}) %collective-permute-start) | collective-permute-done | bytes 983072 | tf_op jit(solution)/shard_map/ppermute | solution.py:363
  90.7 3.4 %collective-permute-start.1 = (bf16[640,256]{1,0:T(8,128)(2,1)S(1)}, bf16[640,256]{1,0:T(8,128)(2,1)S(1)}, u32[]{:S(2)}, u32[]{:S(2)}) collective-permute-start(bf16[640,256]{1,0:T(8,128)(2,1)S(1)} %newest.1), channel_id=1, source_target_pairs={{0,32},{32,64},{64,96},{96,128},{128,160},{160,192},{192,224},{224... | collective-permute-start | bytes 983048 | tf_op jit(solution)/shard_map/ppermute | solution.py:365
  94.1 0.1 copy.7
  94.2 0.1 reshape.27
  94.4 0.1 copy.8
  94.5 0.1 reshape.28
  94.6 0.1 pad_add_fusion.meta
  94.6 12.0 %collective-permute-done.1.prev_ref = bf16[640,256]{1,0:T(8,128)(2,1)S(1)} collective-permute-done((bf16[640,256]{1,0:T(8,128)(2,1)S(1)}, bf16[640,256]{1,0:T(8,128)(2,1)S(1)}, u32[]{:S(2)}, u32[]{:S(2)}) %collective-permute-start.1) | collective-permute-done | bytes 327712 | tf_op jit(solution)/shard_map/ppermute | solution.py:365
  106.6 6.7 %near.1 = (f32[1280,256]{1,0:T(8,128)S(1)}, f32[1280,128]{1,0:T(8,128)S(1)}, bf16[1280,256]{1,0:T(8,128)(2,1)S(1)}) custom-call(s32[16]{0:T(128)S(1)} %pad_add_fusion.meta, bf16[640,768]{1,0:T(8,128)(2,1)S(1)} %bitcast.9, bf16[640,768]{1,0:T(8,128)(2,1)S(1)} %collective-permute-done.other_ref, bf16[640,256]{1,0:T(8,128)(2,1)S(1)} %collective-permute-done.1.prev_ref), custom_call_target="tpu_custom_call" | custom-call | tf_op jit(solution)/shard_map/near/pallas_call | solution.py:102
  113.3 1.1 copy-done.1
  114.4 0.8 copy-done.2
  115.2 1.1 copy-done.3
  116.3 9.5 %far.1 = bf16[1280,256]{1,0:T(8,128)(2,1)S(1)} custom-call(s32[16]{0:T(128)S(1)} %pad_add_fusion.meta, bf16[1280,256]{1,0:T(8,128)(2,1)S(1)} %copy-done.3, f32[1280,256]{1,0:T(8,128)} %copy-done.1, f32[1280,128]{1,0:T(8,128)S(1)} %get-tuple-element.10.stat_ref, bf16[16,8,16,128]{3,2,1,0:T(8,128)(2,1)S(1)} %bitcast.11), custom_call_target="tpu_custom_call" | custom-call | tf_op jit(solution)/shard_map/far/pallas_call | solution.py:176
  125.9 26.6 %all_to_all.27.x_ref = bf16[32,40,256]{2,1,0:T(8,128)(2,1)S(1)} all-to-all(bf16[32,40,256]{2,1,0:T(8,128)(2,1)S(1)} %bitcast.10), channel_id=1, replica_groups=mesh['xl'=2,'za'=3,'zb'=4,'c'=2,'xh'=2,'y'=8] {'c','xh','y'}, dimensions={0} | all-to-all | bytes 1310720 | tf_op jit(solution)/shard_map/all_to_all | solution.py:381
  152.5 2.0 %to_slots.1 = bf16[40,8192]{1,0:T(8,128)(2,1)} custom-call(s32[64]{0:T(128)S(1)} %copy-done.4, bf16[32,40,256]{2,1,0:T(8,128)(2,1)S(1)} %all_to_all.27.x_ref), custom_call_target="tpu_custom_call" | custom-call | tf_op jit(solution)/shard_map/to_slots/pallas_call | solution.py:334
  (17 shorter events, 0.4 us)
Async XLA Ops:
  0.0 94.3 %copy-start = (s32[64,3]{0,1:T(4,128)S(1)}, s32[64,3]{0,1:T(4,128)}, u32[]{:S(2)}) copy-start(s32[64,3]{0,1:T(4,128)} %param.11) | copy-start | bytes 2308
  37.1 9.5 %copy-start.5 = (s32[64,4]{0,1:T(4,128)S(1)}, s32[64,4]{0,1:T(4,128)}, u32[]{:S(2)}) copy-start(s32[64,4]{0,1:T(4,128)} %param.10) | copy-start | bytes 3076
  37.8 18.4 %all-to-all-start.1 = ((bf16[16,5,16,128]{3,2,1,0:T(8,128)(2,1)}), bf16[16,5,16,128]{3,2,1,0:T(8,128)(2,1)S(1)}, u32[]{:S(2)}, u32[]{:S(2)}) async-start(bf16[16,5,16,128]{3,2,1,0:T(8,128)(2,1)} %cut.1), calls=%async_computation.1 | async-start | bytes 655360 | tf_op jit(solution)/shard_map/all_to_all | solution.py:361
  81.3 34.0 %all-to-all-start.3 = ((bf16[8,2,8,16,128]{4,3,2,1,0:T(8,128)(2,1)}), bf16[8,2,8,16,128]{4,3,2,1,0:T(8,128)(2,1)S(1)}, u32[]{:S(2)}, u32[]{:S(2)}) async-start(bf16[8,2,8,16,128]{4,3,2,1,0:T(8,128)(2,1)} %add_up.1), calls=%async_computation.3 | async-start | bytes 1048576 | tf_op jit(solution)/shard_map/all_to_all | solution.py:377
  86.2 4.4 %collective-permute-start = (bf16[640,768]{1,0:T(8,128)(2,1)S(1)}, bf16[640,768]{1,0:T(8,128)(2,1)S(1)}, u32[]{:S(2)}, u32[]{:S(2)}) collective-permute-start(bf16[640,768]{1,0:T(8,128)(2,1)S(1)} %bitcast.7), channel_id=1, source_target_pairs={{0,16},{16,0},{1,17},{17,1},{2,18},{18,2},{3,19},{19,3},{4,20},{20... | collective-permute-start | bytes 2949128 | tf_op jit(solution)/shard_map/ppermute | solution.py:363
  90.7 15.9 %collective-permute-start.1 = (bf16[640,256]{1,0:T(8,128)(2,1)S(1)}, bf16[640,256]{1,0:T(8,128)(2,1)S(1)}, u32[]{:S(2)}, u32[]{:S(2)}) collective-permute-start(bf16[640,256]{1,0:T(8,128)(2,1)S(1)} %newest.1), channel_id=1, source_target_pairs={{0,32},{32,64},{64,96},{96,128},{128,160},{160,192},{192,224},{224... | collective-permute-start | bytes 983048 | tf_op jit(solution)/shard_map/ppermute | solution.py:365
  113.3 1.1 copy-start.1
  114.4 0.8 copy-start.2
  115.2 1.1 copy-start.3
  125.9 26.6 %copy-start.4 = (s32[64]{0:T(128)S(1)}, s32[64]{0:T(128)}, u32[]{:S(2)}) copy-start(s32[64]{0:T(128)} %assign.1) | copy-start | bytes 772

commit v4 on v3

v4 whole, which is shorter than its diff:
```python
import math

import jax
import jax.numpy as jnp
from jax import lax
from jax.experimental import pallas as pl
from jax.experimental.pallas import tpu as pltpu
from jax.sharding import Mesh, PartitionSpec as P


QUERY_HEADS = 64
HD = 128
BT = 128
NV = 4
NS = 3
GROUPS = 16
CORES = 2
SLOTS = QUERY_HEADS // GROUPS // CORES
ROWS = 40
SEQ_ROWS = 640
LB = SEQ_ROWS // BT
TOKENS = CORES * SEQ_ROWS
CHIP_WIDE = CORES * SLOTS * HD
WIDE = CHIP_WIDE + HD
MINE = SLOTS * NV
PAIR_SLOTS = 2 * CORES * MINE
CH = 8
SUB = 16
ALL = ("xl", "za", "zb", "c", "xh", "ya", "yb")
HEAD = ("xh", "ya", "yb")
SPLIT = ("c", "xh", "ya", "yb")
PART = ("xl", "zb", "c")
SCALE = 1.0 / math.sqrt(HD)
NEG = float("-inf")
SMALL = 4 * 1024 * 1024
PAIR = 5
LARGE = 12 * 1024 * 1024


LOG2E_SCALE = SCALE * math.log2(math.e)
DIMS = (((1,), (1,)), ((), ()))


def in_vmem(x):
    return pltpu.with_memory_space_constraint(x, pltpu.VMEM)


def in_hbm(x):
    return pltpu.with_memory_space_constraint(x, pltpu.HBM)


def both_kinds(meta, here_ref, other_ref, pair_ref, diag_ref):
    own = pl.ds(pl.multiple_of(meta[2] * HD, HD), HD)
    rest = pl.ds(pl.multiple_of((1 - meta[2]) * HD, HD), HD)
    x = slice(CHIP_WIDE, WIDE)
    return ((own, here_ref.at[:, x], other_ref.at[:, x]), (rest, pair_ref, diag_ref))


def near_part(
    meta,
    here_ref,
    other_ref,
    pair_ref,
    diag_ref,
    prev_ref,
    acc_ref,
    top_ref,
    q_ref,
    win,
    kc,
    vc,
):
    first_block = meta[0]
    core = meta[1]
    wide = SLOTS * HD
    my_lanes = pl.ds(pl.multiple_of(core * wide, wide), wide)
    mine = pl.multiple_of(core * SEQ_ROWS, SEQ_ROWS)
    theirs = pl.multiple_of((1 - core) * SEQ_ROWS, SEQ_ROWS)
    win[0:SEQ_ROWS, :] = prev_ref[...]
    for lanes, inner, outer in both_kinds(meta, here_ref, other_ref, pair_ref, diag_ref):
        win[pl.ds(SEQ_ROWS + mine, SEQ_ROWS), lanes] = inner[...]
        win[pl.ds(SEQ_ROWS + theirs, SEQ_ROWS), lanes] = outer[...]
    q_ref[pl.ds(mine, SEQ_ROWS), :] = here_ref[:, my_lanes]
    q_ref[pl.ds(theirs, SEQ_ROWS), :] = other_ref[:, my_lanes]
    for i in range(PAIR * SLOTS):
        vc[i, :, HD : 2 * HD] = jnp.ones((NS * BT, HD), jnp.bfloat16)
    causal = lax.broadcasted_iota(jnp.int32, (BT, BT), 0) >= lax.broadcasted_iota(
        jnp.int32, (BT, BT), 1
    )

    def unit(step, carry):
        for i in range(PAIR * SLOTS):
            h = i % SLOTS
            local = step * PAIR + i // SLOTS
            offs = [meta[3 + MINE + h * NS + n] for n in range(NS)]
            good = []
            for n in range(NS):
                at = pl.ds(pl.multiple_of((LB + local - offs[n]) * BT, BT), BT)
                rows = slice(n * BT, (n + 1) * BT)
                kc[i, rows, :] = win[at, 0:HD]
                vc[i, rows, 0:HD] = win[at, HD : 2 * HD]
                good.append(first_block + local - offs[n] >= 0)
            rows = pl.ds(pl.multiple_of(local * BT, BT), BT)
            q = q_ref[rows, h * HD : (h + 1) * HD]
            s = lax.dot_general(q, kc[i], DIMS, preferred_element_type=jnp.float32)
            parts = [jnp.where(causal, s[:, 0:BT], NEG)]
            for n in range(1, NS):
                parts.append(s[:, n * BT : (n + 1) * BT] + jnp.where(good[n], 0.0, NEG))
            top = jnp.maximum(jnp.maximum(parts[0], parts[1]), parts[2])
            top = jnp.broadcast_to(jnp.max(top, axis=1, keepdims=True), (BT, HD))
            w = jnp.concatenate(
                [jnp.exp2((x - top) * LOG2E_SCALE).astype(jnp.bfloat16) for x in parts], axis=1
            )
            acc_ref[rows, 2 * h * HD : 2 * (h + 1) * HD] = jnp.dot(
                w, vc[i], preferred_element_type=jnp.float32
            )
            top_ref[rows, h * HD : (h + 1) * HD] = top
        return carry

    lax.fori_loop(0, TOKENS // BT // PAIR, unit, 0)


def near(meta, here, other, pair, diag, prev):
    vm = pl.BlockSpec(memory_space=pltpu.VMEM)
    return pl.pallas_call(
        near_part,
        out_shape=(
            jax.ShapeDtypeStruct((TOKENS, 2 * SLOTS * HD), jnp.float32),
            jax.ShapeDtypeStruct((TOKENS, SLOTS * HD), jnp.float32),
            jax.ShapeDtypeStruct((TOKENS, SLOTS * HD), jnp.bfloat16),
        ),
        in_specs=[pl.BlockSpec(memory_space=pltpu.SMEM), vm, vm, vm, vm, vm],
        out_specs=(vm, vm, vm),
        scratch_shapes=[
            pltpu.VMEM((TOKENS + SEQ_ROWS, 2 * HD), jnp.bfloat16),
            pltpu.VMEM((PAIR * SLOTS, NS * BT, HD), jnp.bfloat16),
            pltpu.VMEM((PAIR * SLOTS, NS * BT, 2 * HD), jnp.bfloat16),
        ],
        name="near",
        compiler_params=pltpu.CompilerParams(vmem_limit_bytes=LARGE),
    )(meta, *(in_vmem(x) for x in (here, other, pair, diag, prev)))


def far_part(
    meta, q_hbm, acc_hbm, top_hbm, vert_ref, o_ref, q_ref, acc_ref, top_ref, vk, vv, sems
):
    first_block = meta[0]
    steps = TOKENS // BT // PAIR
    moves = ((q_hbm, q_ref), (top_hbm, top_ref), (acc_hbm, acc_ref))

    def fetch(step):
        rows = pl.ds(pl.multiple_of(step * PAIR * BT, PAIR * BT), PAIR * BT)
        return [
            pltpu.make_async_copy(source.at[rows], target.at[rows], sems.at[n, step])
            for n, (source, target) in enumerate(moves)
        ]

    for step in range(steps):
        for copy in fetch(step):
            copy.start()
    for h in range(SLOTS):
        vv[h, :, HD : 2 * HD] = jnp.ones((NV * BT, HD), jnp.bfloat16)
        for n in range(NV):
            rows = slice(n * BT, (n + 1) * BT)
            for kind, target in ((0, vk), (1, vv)):
                x = vert_ref[:, kind, h * NV + n].astype(jnp.float32).reshape(BT, HD)
                target[h, rows, 0:HD] = x.astype(jnp.bfloat16)

    def unit(step, carry):
        moving = fetch(step)
        moving[0].wait()
        moving[1].wait()
        later = []
        both = pl.ds(pl.multiple_of(step * PAIR * BT, PAIR * BT), PAIR * BT)
        for h in range(SLOTS):
            offs = [meta[3 + MINE + h * NS + n] for n in range(NS)]
            verts = [meta[3 + h * NV + n] for n in range(NV)]
            lane = slice(h * HD, (h + 1) * HD)
            s = lax.dot_general(q_ref[both, lane], vk[h], DIMS, preferred_element_type=jnp.float32)
            ws = []
            keeps = []
            for p in range(PAIR):
                local = step * PAIR + p
                block = first_block + local
                parts = []
                for n in range(NV):
                    ok = verts[n] <= block
                    for o in offs:
                        ok = ok & (block - verts[n] != o)
                    for e in range(n):
                        ok = ok & (verts[n] != verts[e])
                    x = s[p * BT : (p + 1) * BT, n * BT : (n + 1) * BT]
                    parts.append(x + jnp.where(ok, 0.0, NEG))
                rows = pl.ds(pl.multiple_of(local * BT, BT), BT)
                old = top_ref[rows, lane]
                top = jnp.maximum(
                    jnp.maximum(parts[0], parts[1]), jnp.maximum(parts[2], parts[3])
                )
                top = jnp.maximum(
                    jnp.broadcast_to(jnp.max(top, axis=1, keepdims=True), (BT, HD)), old
                )
                keeps.append(jnp.exp2((old - top) * LOG2E_SCALE))
                ws.append(
                    jnp.concatenate(
                        [jnp.exp2((x - top) * LOG2E_SCALE).astype(jnp.bfloat16) for x in parts],
                        axis=1,
                    )
                )
            gain = jnp.dot(
                jnp.concatenate(ws, axis=0), vv[h], preferred_element_type=jnp.float32
            )
            later.append((keeps, gain))
        moving[2].wait()
        for h, (keeps, gain) in enumerate(later):
            lane = slice(h * HD, (h + 1) * HD)
            for p in range(PAIR):
                rows = pl.ds(pl.multiple_of((step * PAIR + p) * BT, BT), BT)
                here = slice(p * BT, (p + 1) * BT)
                acc = acc_ref[rows, 2 * h * HD : (2 * h + 1) * HD] * keeps[p] + gain[here, 0:HD]
                total = (
                    acc_ref[rows, (2 * h + 1) * HD : (2 * h + 2) * HD] * keeps[p]
                    + gain[here, HD : 2 * HD]
                )
                o_ref[rows, lane] = (acc / total).astype(jnp.bfloat16)
        return carry

    lax.fori_loop(0, steps, unit, 0)


def far(meta, q, acc, top, vert):
    vm = pl.BlockSpec(memory_space=pltpu.VMEM)
    hbm = pl.BlockSpec(memory_space=pltpu.HBM)
    return pl.pallas_call(
        far_part,
        out_shape=pltpu.VMEM((TOKENS, SLOTS * HD), jnp.bfloat16),
        in_specs=[pl.BlockSpec(memory_space=pltpu.SMEM), hbm, hbm, hbm, vm],
        out_specs=vm,
        scratch_shapes=[
            pltpu.VMEM((TOKENS, SLOTS * HD), jnp.bfloat16),
            pltpu.VMEM((TOKENS, 2 * SLOTS * HD), jnp.float32),
            pltpu.VMEM((TOKENS, SLOTS * HD), jnp.float32),
            pltpu.VMEM((SLOTS, NV * BT, HD), jnp.bfloat16),
            pltpu.VMEM((SLOTS, NV * BT, 2 * HD), jnp.bfloat16),
            pltpu.SemaphoreType.DMA((3, TOKENS // BT // PAIR)),
        ],
        name="far",
        compiler_params=pltpu.CompilerParams(vmem_limit_bytes=LARGE),
    )(meta, in_hbm(q), in_hbm(acc), in_hbm(top), in_vmem(vert))


def cut(here_ref, o_ref, x_ref):
    x_ref[...] = here_ref[:, CHIP_WIDE:WIDE]
    for j in range(LB):
        x = here_ref[j * BT : (j + 1) * BT, CHIP_WIDE:WIDE].astype(jnp.float32)
        for r in range(SUB):
            o_ref[r, j] = x[r * CH : (r + 1) * CH].astype(jnp.bfloat16)


def in_chunks(here):
    vm = pl.BlockSpec(memory_space=pltpu.VMEM)
    return pl.pallas_call(
        cut,
        out_shape=(
            pltpu.VMEM((SUB, LB, CH, HD), jnp.bfloat16),
            pltpu.VMEM((SEQ_ROWS, HD), jnp.bfloat16),
        ),
        in_specs=[vm],
        out_specs=(vm, vm),
        name="cut",
        compiler_params=pltpu.CompilerParams(vmem_limit_bytes=SMALL),
    )(in_vmem(here))


def newest(meta, here_ref, other_ref, pair_ref, diag_ref, o_ref):
    for lanes, inner, outer in both_kinds(meta, here_ref, other_ref, pair_ref, diag_ref):

        @pl.when(meta[1] == 1)
        def _():
            o_ref[:, lanes] = inner[...]

        @pl.when(meta[1] != 1)
        def _():
            o_ref[:, lanes] = outer[...]


def last_window(meta, here, other, pair, diag):
    vm = pl.BlockSpec(memory_space=pltpu.VMEM)
    return pl.pallas_call(
        newest,
        out_shape=pltpu.VMEM((SEQ_ROWS, 2 * HD), jnp.bfloat16),
        in_specs=[pl.BlockSpec(memory_space=pltpu.SMEM), vm, vm, vm, vm],
        out_specs=vm,
        name="newest",
        compiler_params=pltpu.CompilerParams(vmem_limit_bytes=SMALL),
    )(meta, *(in_vmem(x) for x in (here, other, pair, diag)))


def choose(spots, held_ref, o_ref):
    for pair in range(2):
        for c in range(CORES):
            for j in range(MINE):
                at = (pair * CORES + c) * MINE + j
                mine = jnp.where(spots[PAIR_SLOTS + at] == 1, 1.0, 0.0).astype(jnp.bfloat16)
                x = held_ref[spots[at]] * mine
                for part in range(3):
                    o_ref[(part * CORES + c) * 2 + pair, j] = x


def chosen_chunks(spots, held):
    vm = pl.BlockSpec(memory_space=pltpu.VMEM)
    return pl.pallas_call(
        choose,
        out_shape=pltpu.VMEM((3 * CORES * 2, MINE, CH, HD), jnp.bfloat16),
        in_specs=[pl.BlockSpec(memory_space=pltpu.SMEM), vm],
        out_specs=vm,
        name="choose",
        compiler_params=pltpu.CompilerParams(vmem_limit_bytes=SMALL),
    )(spots, in_vmem(held))


def add_up(x_ref, o_ref):
    kinds = CORES * 2
    for c in range(kinds):
        total = x_ref[c] + x_ref[kinds + c] + x_ref[2 * kinds + c]
        for part in range(8):
            o_ref[part, c] = total


def copies_of_sum(x):
    vm = pl.BlockSpec(memory_space=pltpu.VMEM)
    return pl.pallas_call(
        add_up,
        out_shape=jax.ShapeDtypeStruct((8, CORES * 2, MINE, CH, HD), jnp.bfloat16),
        in_specs=[vm],
        out_specs=vm,
        name="add_up",
        compiler_params=pltpu.CompilerParams(vmem_limit_bytes=SMALL),
    )(in_vmem(x))


def lay_out(q_ref, k_ref, v_ref, o_ref, sems):
    copies = []
    for g in range(GROUPS):
        m = g // 2 * HD
        for n, (ref, start, at, size) in enumerate(
            (
                (q_ref, g * CHIP_WIDE, 0, CHIP_WIDE),
                (v_ref if g % 2 else k_ref, m, CHIP_WIDE, HD),
            )
        ):
            copies.append(
                pltpu.make_async_copy(
                    ref.at[:, pl.ds(start, size)], o_ref.at[g, :, pl.ds(at, size)], sems.at[n, g]
                )
            )
    for copy in copies:
        copy.start()
    for copy in copies:
        copy.wait()


def pack(q, k, v):
    anywhere = pl.BlockSpec(memory_space=pltpu.HBM)
    return pl.pallas_call(
        lay_out,
        out_shape=pltpu.VMEM((GROUPS, ROWS, WIDE), jnp.bfloat16),
        in_specs=[anywhere] * 3,
        out_specs=pl.BlockSpec(memory_space=pltpu.VMEM),
        scratch_shapes=[pltpu.SemaphoreType.DMA((2, GROUPS))],
        name="lay_out",
        compiler_params=pltpu.CompilerParams(vmem_limit_bytes=SMALL),
    )(in_hbm(q), in_hbm(k), in_hbm(v))


def to_slots(assign, x_ref, o_ref, sems):
    copies = []
    for k in range(QUERY_HEADS):
        a = assign[k]
        source = (a >> 1 & 1) * GROUPS + (a >> 2)
        lane = pl.ds(pl.multiple_of((a & 1) * HD, HD), HD)
        copies.append(
            pltpu.make_async_copy(
                x_ref.at[source, :, lane], o_ref.at[:, pl.ds(k * HD, HD)], sems.at[k]
            )
        )
        copies[-1].start()
    for copy in copies:
        copy.wait()


def place_slots(assign, x):
    return pl.pallas_call(
        to_slots,
        out_shape=jax.ShapeDtypeStruct((ROWS, QUERY_HEADS * HD), jnp.bfloat16),
        in_specs=[
            pl.BlockSpec(memory_space=pltpu.SMEM),
            pl.BlockSpec(memory_space=pltpu.VMEM),
        ],
        out_specs=pl.BlockSpec(memory_space=pl.ANY),
        scratch_shapes=[pltpu.SemaphoreType.DMA((QUERY_HEADS,))],
        name="to_slots",
        compiler_params=pltpu.CompilerParams(vmem_limit_bytes=SMALL),
    )(assign, in_vmem(x))


def per_device(q_rows, k_rows, v_rows, group_assign, vertical_blocks, slash_offsets):
    group = lax.axis_index(HEAD)
    core = lax.axis_index("c")
    odd = lax.axis_index("yb")
    chip = lax.axis_index(("xl", "za", "zb"))
    za = lax.axis_index("za")
    pair_heads = 2 * CORES * SLOTS
    verts = lax.dynamic_slice_in_dim(vertical_blocks, group // 2 * pair_heads, pair_heads)
    verts = verts.reshape(-1)
    my_head = (group * CORES + core) * SLOTS
    my_verts = lax.dynamic_slice_in_dim(vertical_blocks, my_head, SLOTS).reshape(-1)
    my_offs = lax.dynamic_slice_in_dim(slash_offsets, my_head, SLOTS).reshape(-1)
    place = jnp.stack([chip * CORES * LB, core, odd]).astype(jnp.int32)
    meta = jnp.concatenate([place, my_verts, my_offs])

    sent = pack(q_rows, k_rows, v_rows)
    here = lax.all_to_all(sent, HEAD, 0, 0, tiled=True).reshape(SEQ_ROWS, WIDE)
    chunks, x_here = in_chunks(here)
    held = lax.all_to_all(chunks, PART, 0, 0, tiled=True)

    other = lax.ppermute(here, "c", [(0, 1), (1, 0)])
    pair = lax.ppermute(x_here, "yb", [(0, 1), (1, 0)])
    diag = lax.ppermute(x_here, ("c", "yb"), [(0, 3), (1, 2), (2, 1), (3, 0)])
    last = last_window(place, here, other, pair, diag)
    kv_before = lax.ppermute(last, ("xl", "za", "zb"), [(i, i + 1) for i in range(23)])

    owner = verts // LB
    z = (owner % 24) // 2
    spot = ((owner // 24) * 8 + (z % 4) * 2 + owner % 2) * LB + verts % LB
    spots = jnp.concatenate([spot, (z // 4 == za).astype(jnp.int32)])
    chosen = chosen_chunks(spots, held.reshape(SUB * LB, CH, HD))
    joined = lax.all_to_all(chosen, ("za", "c", "yb"), 0, 0, tiled=True)
    spread = copies_of_sum(joined)
    vert = lax.all_to_all(spread, ("xl", "zb"), 0, 0, tiled=True)
    acc, top, q_here = near(meta, here, other, pair, diag, kv_before)
    out = far(meta, q_here, acc, top, vert.reshape(SUB, 2, MINE, CH, HD))
    back = lax.all_to_all(
        out.reshape(CORES * GROUPS, ROWS, SLOTS * HD), SPLIT, 0, 0, tiled=True
    )
    return place_slots(group_assign, back)


def solution(mesh):
    fine = Mesh(mesh.devices.reshape(2, 3, 4, 2, 2, 4, 2), ALL)
    rows = P(ALL, None)
    return jax.shard_map(
        per_device,
        mesh=fine,
        in_specs=(rows, rows, rows, P(), P(), P()),
        out_specs=rows,
        check_vma=False,
    )
```

time: 155 us -> 150 us (0.968)
  blocking collectives: 85.5 us -> 51 us
  waiting for transfers between devices: 23.3 us -> 45.2 us
  starting transfers between devices: 19 us -> 33.3 us
  Pallas kernels: 22.2 us -> 15.1 us
    all_to_all x2 -> x1, blocking collectives: 58.9 us -> 23.9 us  [per_device(): joined = lax.all_to_all(chosen, ('za', 'c', 'yb'), 0, 0, tiled=True)]
    all_to_all x1 -> x2, waiting for transfers between devices: 8.84 us -> 29.2 us  [the longest x1 22.3 us: per_device(): here = lax.all_to_all(sent, HEAD, 0, 0, tiled=True).reshape(SEQ_ROWS, WIDE)]
    all_to_all x1 -> x2, starting transfers between devices: 8.74 us -> 17.9 us  [the longest x1 9.14 us: per_device(): here = lax.all_to_all(sent, HEAD, 0, 0, tiled=True).reshape(SEQ_ROWS, WIDE)]
    ppermute x0 -> x2, waiting for transfers between devices: none -> 5.75 us  [the longest x1 3.19 us: per_device(): pair = lax.ppermute(x_here, 'yb', [(0, 1), (1, 0)])]
    ppermute x0 -> x2, starting transfers between devices: none -> 5.67 us  [the longest x1 3.02 us: per_device(): pair = lax.ppermute(x_here, 'yb', [(0, 1), (1, 0)])]
    pallas_call x1, Pallas kernels: 9.54 us -> 4.65 us  [far(): pl.pallas_call(far_part, out_shape=pltpu.VMEM((TOKENS, SLOTS * HD), jnp.b...]
    pallas_call x4, Pallas kernels: 8.99 us -> 5.46 us  [the longest x1 3.21 us: near(): pl.pallas_call(near_part, out_shape=(jax.ShapeDtypeStruct((TOKENS, 2 * SL...]
    ppermute x1, waiting for transfers between devices: 2.52 us -> 0.01 us  [per_device(): other = lax.ppermute(here, 'c', [(0, 1), (1, 0)])]
  transfers between devices with their start and end apart: 4 -> 7, of which waited for: 3 -> 5; matrix products, arithmetic and copies ran while one was open for 1% -> 1% of each run, Pallas kernels for 4% -> 3%
where the time goes in v4:
time: 150 us
  blocking collectives  51 us (34%)
  waiting for transfers between devices  45.2 us (30%)
  starting transfers between devices  33.3 us (22%)
  Pallas kernels  15.1 us (10%)
  local copies, waits for them, and re-layouts  4.5 us (3%)
    all_to_all x1, blocking collectives, per_device(): lax.all_to_all(out.reshape(CORES * GROUPS, ROWS, SLOTS * HD), SPLIT, 0, 0...  27.1 us
    all_to_all x1, blocking collectives, per_device(): joined = lax.all_to_all(chosen, ('za', 'c', 'yb'), 0, 0, tiled=True)  23.9 us
    all_to_all x1, waiting for transfers between devices, per_device(): here = lax.all_to_all(sent, HEAD, 0, 0, tiled=True).reshape(SEQ_ROWS, WIDE)  22.3 us
    ppermute x1, waiting for transfers between devices, per_device(): lax.ppermute(last, ('xl', 'za', 'zb'), [(i, i + 1) for i in range(23)])  10.2 us
    all_to_all x1, starting transfers between devices, per_device(): here = lax.all_to_all(sent, HEAD, 0, 0, tiled=True).reshape(SEQ_ROWS, WIDE)  9.14 us
    all_to_all x1, starting transfers between devices, per_device(): held = lax.all_to_all(chunks, PART, 0, 0, tiled=True)  8.74 us
    all_to_all x1, waiting for transfers between devices, per_device(): held = lax.all_to_all(chunks, PART, 0, 0, tiled=True)  6.93 us
    pallas_call x1, Pallas kernels, far(): pl.pallas_call(far_part, out_shape=pltpu.VMEM((TOKENS, SLOTS * HD), jnp.b...  4.65 us
  transfers between devices with their start and end apart: 7, of which 5 were waited for; matrix products, arithmetic and copies ran while one was open for 1% of the time, Pallas kernels for 3%

profile of v4, /device:TPU:10, one launch (start us, length us, event | category | flops | bytes accessed | tf_op | source)
XLA Modules:
  0.0 149.6 jit_solution(4992407471120560374)
XLA Ops:
  0.0 2.3 %lay_out.1 = bf16[16,40,640]{2,1,0:T(8,128)(2,1)} custom-call(bf16[40,8192]{1,0:T(8,128)(2,1)} %q_ref.1, bf16[40,1024]{1,0:T(8,128)(2,1)} %k_ref.1, bf16[40,1024]{1,0:T(8,128)(2,1)} %v_ref.1), custom_call_target="tpu_custom_call" | custom-call | tf_op jit(solution)/shard_map/lay_out/pallas_call | solution.py:364
  2.4 9.1 %all-to-all-start = ((bf16[16,40,640]{2,1,0:T(8,128)(2,1)}), bf16[16,40,640]{2,1,0:T(8,128)(2,1)S(1)}, u32[]{:S(2)}, u32[]{:S(2)}) async-start(bf16[16,40,640]{2,1,0:T(8,128)(2,1)} %lay_out.1), calls=%async_computation | async-start | bytes 1638400 | tf_op jit(solution)/shard_map/all_to_all | solution.py:422
  11.5 0.1 dynamic-slice_divide_fusion
  12.0 0.1 copy.14
  12.1 0.1 ne.74
  12.2 22.3 %all-to-all-done = bf16[16,40,640]{2,1,0:T(8,128)(2,1)S(1)} async-done(((bf16[16,40,640]{2,1,0:T(8,128)(2,1)}), bf16[16,40,640]{2,1,0:T(8,128)(2,1)S(1)}, u32[]{:S(2)}, u32[]{:S(2)}) %all-to-all-start) | async-done | bytes 819232 | tf_op jit(solution)/shard_map/all_to_all | solution.py:422
  34.5 0.7 cut.1
  35.2 8.7 %all-to-all-start.1 = ((bf16[16,5,8,128]{3,2,1,0:T(8,128)(2,1)}), bf16[16,5,8,128]{3,2,1,0:T(8,128)(2,1)S(1)}, u32[]{:S(2)}, u32[]{:S(2)}) async-start(bf16[16,5,8,128]{3,2,1,0:T(8,128)(2,1)} %get-tuple-element.14), calls=%async_computation.1 | async-start | bytes 327680 | tf_op jit(solution)/shard_map/all_to_all | solution.py:424
  44.0 6.9 %all-to-all-done.1 = bf16[16,5,8,128]{3,2,1,0:T(8,128)(2,1)S(1)} async-done(((bf16[16,5,8,128]{3,2,1,0:T(8,128)(2,1)}), bf16[16,5,8,128]{3,2,1,0:T(8,128)(2,1)S(1)}, u32[]{:S(2)}, u32[]{:S(2)}) %all-to-all-start.1) | async-done | bytes 163872 | tf_op jit(solution)/shard_map/all_to_all | solution.py:424
  51.0 0.7 choose.1
  51.7 23.9 %all_to_all.25.x_ref = bf16[12,8,8,128]{3,2,1,0:T(8,128)(2,1)S(1)} all-to-all(bf16[12,8,8,128]{3,2,1,0:T(8,128)(2,1)S(1)} %choose.1), channel_id=1, replica_groups=mesh['xl'=2,'za'=3,'zb'=4,'c'=2,'xh'=2,'ya'=4,'yb'=2] {'za','c','yb'}, dimensions={0} | all-to-all | bytes 393216 | tf_op jit(solution)/shard_map/all_to_all | solution.py:437
  75.6 0.8 add_up.1
  76.4 4.5 %all-to-all-start.3 = ((bf16[8,4,8,8,128]{4,3,2,1,0:T(8,128)(2,1)}), bf16[8,4,8,8,128]{4,3,2,1,0:T(8,128)(2,1)S(1)}, u32[]{:S(2)}, u32[]{:S(2)}) async-start(bf16[8,4,8,8,128]{4,3,2,1,0:T(8,128)(2,1)} %add_up.1), calls=%async_computation.3 | async-start | bytes 1048576 | tf_op jit(solution)/shard_map/all_to_all | solution.py:439
  80.9 1.9 %collective-permute-start = (bf16[640,640]{1,0:T(8,128)(2,1)S(1)}, bf16[640,640]{1,0:T(8,128)(2,1)S(1)}, u32[]{:S(2)}, u32[]{:S(2)}) collective-permute-start(bf16[640,640]{1,0:T(8,128)(2,1)S(1)} %bitcast.8), channel_id=1, source_target_pairs={{0,16},{16,0},{1,17},{17,1},{2,18},{18,2},{3,19},{19,3},{4,20},{20... | collective-permute-start | bytes 2457608 | tf_op jit(solution)/shard_map/ppermute | solution.py:426
  82.8 3.0 %collective-permute-start.1 = (bf16[640,128]{1,0:T(8,128)(2,1)S(1)}, bf16[640,128]{1,0:T(8,128)(2,1)S(1)}, u32[]{:S(2)}, u32[]{:S(2)}) collective-permute-start(bf16[640,128]{1,0:T(8,128)(2,1)S(1)} %get-tuple-element.10), channel_id=1, source_target_pairs={{0,1},{1,0},{2,3},{3,2},{4,5},{5,4},{6,7},{7,6},{8,9},{9,8},{10,11... | collective-permute-start | bytes 491528 | tf_op jit(solution)/shard_map/ppermute | solution.py:427
  85.8 2.6 %collective-permute-start.2 = (bf16[640,128]{1,0:T(8,128)(2,1)S(1)}, bf16[640,128]{1,0:T(8,128)(2,1)S(1)}, u32[]{:S(2)}, u32[]{:S(2)}) collective-permute-start(bf16[640,128]{1,0:T(8,128)(2,1)S(1)} %get-tuple-element.10), channel_id=1, source_target_pairs={{0,17},{1,16},{16,1},{17,0},{2,19},{3,18},{18,3},{19,2},{4,21},{5,... | collective-permute-start | bytes 491528 | tf_op jit(solution)/shard_map/ppermute | solution.py:428
  88.6 3.2 %collective-permute-done.1.pair_ref = bf16[640,128]{1,0:T(8,128)(2,1)S(1)} collective-permute-done((bf16[640,128]{1,0:T(8,128)(2,1)S(1)}, bf16[640,128]{1,0:T(8,128)(2,1)S(1)}, u32[]{:S(2)}, u32[]{:S(2)}) %collective-permute-start.1) | collective-permute-done | bytes 163872 | tf_op jit(solution)/shard_map/ppermute | solution.py:427
  91.8 2.6 %collective-permute-done.2.diag_ref = bf16[640,128]{1,0:T(8,128)(2,1)S(1)} collective-permute-done((bf16[640,128]{1,0:T(8,128)(2,1)S(1)}, bf16[640,128]{1,0:T(8,128)(2,1)S(1)}, u32[]{:S(2)}, u32[]{:S(2)}) %collective-permute-start.2) | collective-permute-done | bytes 163872 | tf_op jit(solution)/shard_map/ppermute | solution.py:428
  94.3 0.6 newest.1
  95.0 3.4 %collective-permute-start.3 = (bf16[640,256]{1,0:T(8,128)(2,1)S(1)}, bf16[640,256]{1,0:T(8,128)(2,1)S(1)}, u32[]{:S(2)}, u32[]{:S(2)}) collective-permute-start(bf16[640,256]{1,0:T(8,128)(2,1)S(1)} %newest.1), channel_id=1, source_target_pairs={{0,32},{32,64},{64,96},{96,128},{128,160},{160,192},{192,224},{224... | collective-permute-start | bytes 983048 | tf_op jit(solution)/shard_map/ppermute | solution.py:430
  98.4 0.1 copy.12
  98.5 0.1 reshape.26
  98.7 0.1 copy.13
  98.8 0.1 reshape.27
  98.9 10.2 %collective-permute-done.3.prev_ref = bf16[640,256]{1,0:T(8,128)(2,1)S(1)} collective-permute-done((bf16[640,256]{1,0:T(8,128)(2,1)S(1)}, bf16[640,256]{1,0:T(8,128)(2,1)S(1)}, u32[]{:S(2)}, u32[]{:S(2)}) %collective-permute-start.3) | collective-permute-done | bytes 327712 | tf_op jit(solution)/shard_map/ppermute | solution.py:430
  109.2 3.2 %near.1 = (f32[1280,512]{1,0:T(8,128)S(1)}, f32[1280,256]{1,0:T(8,128)S(1)}, bf16[1280,256]{1,0:T(8,128)(2,1)S(1)}) custom-call(s32[17]{0:T(128)S(1)} %concatenate.7.meta, bf16[640,640]{1,0:T(8,128)(2,1)S(1)} %bitcast.10, bf16[640,640]{1,0:T(8,128)(2,1)S(1)} %collective-permute-done.other_ref, bf16[640,128]{1,0:T(8,128)(2,1)S(1)} %collective-permute-done.1.pair_ref, ...), custom_call_target="tpu_custom_call" | custom-call | tf_op jit(solution)/shard_map/near/pallas_call | solution.py:125
  112.4 1.5 copy-done.1
  113.9 1.1 copy-done.2
  114.9 0.8 copy-done.3
  115.8 4.7 %far.1 = bf16[1280,256]{1,0:T(8,128)(2,1)S(1)} custom-call(s32[17]{0:T(128)S(1)} %concatenate.7.meta, bf16[1280,256]{1,0:T(8,128)(2,1)} %copy-done.3, f32[1280,512]{1,0:T(8,128)} %copy-done.1, f32[1280,256]{1,0:T(8,128)} %copy-done.2, bf16[16,2,8,8,128]{4,3,2,1,0:T(8,128)(2,1)S(1)} %bitcast.12), custom_call_target="tpu_custom_call" | custom-call | tf_op jit(solution)/shard_map/far/pallas_call | solution.py:233
  120.4 27.1 %all_to_all.26.x_ref = bf16[32,40,256]{2,1,0:T(8,128)(2,1)S(1)} all-to-all(bf16[32,40,256]{2,1,0:T(8,128)(2,1)S(1)} %bitcast.11), channel_id=1, replica_groups=mesh['xl'=2,'za'=3,'zb'=4,'c'=2,'xh'=2,'ya'=4,'yb'=2] {'c','xh','ya','yb'}, dimensions={0} | all-to-all | bytes 1310720 | tf_op jit(solution)/shard_map/all_to_all | solution.py:442
  147.6 2.0 %to_slots.1 = bf16[40,8192]{1,0:T(8,128)(2,1)} custom-call(s32[64]{0:T(128)S(1)} %copy-done.4, bf16[32,40,256]{2,1,0:T(8,128)(2,1)S(1)} %all_to_all.26.x_ref), custom_call_target="tpu_custom_call" | custom-call | tf_op jit(solution)/shard_map/to_slots/pallas_call | solution.py:392
  (23 shorter events, 0.8 us)
Async XLA Ops:
  0.0 98.6 %copy-start = (s32[64,3]{0,1:T(4,128)S(1)}, s32[64,3]{0,1:T(4,128)}, u32[]{:S(2)}) copy-start(s32[64,3]{0,1:T(4,128)} %param.11) | copy-start | bytes 2308
  0.0 11.5 %copy-start.5 = (s32[64,4]{0,1:T(4,128)S(1)}, s32[64,4]{0,1:T(4,128)}, u32[]{:S(2)}) copy-start(s32[64,4]{0,1:T(4,128)} %param.10) | copy-start | bytes 3076
  2.4 32.1 %all-to-all-start = ((bf16[16,40,640]{2,1,0:T(8,128)(2,1)}), bf16[16,40,640]{2,1,0:T(8,128)(2,1)S(1)}, u32[]{:S(2)}, u32[]{:S(2)}) async-start(bf16[16,40,640]{2,1,0:T(8,128)(2,1)} %lay_out.1), calls=%async_computation | async-start | bytes 1638400 | tf_op jit(solution)/shard_map/all_to_all | solution.py:422
  35.2 15.8 %all-to-all-start.1 = ((bf16[16,5,8,128]{3,2,1,0:T(8,128)(2,1)}), bf16[16,5,8,128]{3,2,1,0:T(8,128)(2,1)S(1)}, u32[]{:S(2)}, u32[]{:S(2)}) async-start(bf16[16,5,8,128]{3,2,1,0:T(8,128)(2,1)} %get-tuple-element.14), calls=%async_computation.1 | async-start | bytes 327680 | tf_op jit(solution)/shard_map/all_to_all | solution.py:424
  76.4 39.4 %all-to-all-start.3 = ((bf16[8,4,8,8,128]{4,3,2,1,0:T(8,128)(2,1)}), bf16[8,4,8,8,128]{4,3,2,1,0:T(8,128)(2,1)S(1)}, u32[]{:S(2)}, u32[]{:S(2)}) async-start(bf16[8,4,8,8,128]{4,3,2,1,0:T(8,128)(2,1)} %add_up.1), calls=%async_computation.3 | async-start | bytes 1048576 | tf_op jit(solution)/shard_map/all_to_all | solution.py:439
  80.9 13.4 %collective-permute-start = (bf16[640,640]{1,0:T(8,128)(2,1)S(1)}, bf16[640,640]{1,0:T(8,128)(2,1)S(1)}, u32[]{:S(2)}, u32[]{:S(2)}) collective-permute-start(bf16[640,640]{1,0:T(8,128)(2,1)S(1)} %bitcast.8), channel_id=1, source_target_pairs={{0,16},{16,0},{1,17},{17,1},{2,18},{18,2},{3,19},{19,3},{4,20},{20... | collective-permute-start | bytes 2457608 | tf_op jit(solution)/shard_map/ppermute | solution.py:426
  82.8 9.0 %collective-permute-start.1 = (bf16[640,128]{1,0:T(8,128)(2,1)S(1)}, bf16[640,128]{1,0:T(8,128)(2,1)S(1)}, u32[]{:S(2)}, u32[]{:S(2)}) collective-permute-start(bf16[640,128]{1,0:T(8,128)(2,1)S(1)} %get-tuple-element.10), channel_id=1, source_target_pairs={{0,1},{1,0},{2,3},{3,2},{4,5},{5,4},{6,7},{7,6},{8,9},{9,8},{10,11... | collective-permute-start | bytes 491528 | tf_op jit(solution)/shard_map/ppermute | solution.py:427
  85.8 8.5 %collective-permute-start.2 = (bf16[640,128]{1,0:T(8,128)(2,1)S(1)}, bf16[640,128]{1,0:T(8,128)(2,1)S(1)}, u32[]{:S(2)}, u32[]{:S(2)}) collective-permute-start(bf16[640,128]{1,0:T(8,128)(2,1)S(1)} %get-tuple-element.10), channel_id=1, source_target_pairs={{0,17},{1,16},{16,1},{17,0},{2,19},{3,18},{18,3},{19,2},{4,21},{5,... | collective-permute-start | bytes 491528 | tf_op jit(solution)/shard_map/ppermute | solution.py:428
  95.0 14.2 %collective-permute-start.3 = (bf16[640,256]{1,0:T(8,128)(2,1)S(1)}, bf16[640,256]{1,0:T(8,128)(2,1)S(1)}, u32[]{:S(2)}, u32[]{:S(2)}) collective-permute-start(bf16[640,256]{1,0:T(8,128)(2,1)S(1)} %newest.1), channel_id=1, source_target_pairs={{0,32},{32,64},{64,96},{96,128},{128,160},{160,192},{192,224},{224... | collective-permute-start | bytes 983048 | tf_op jit(solution)/shard_map/ppermute | solution.py:430
  112.4 1.5 %copy-start.1 = (f32[1280,512]{1,0:T(8,128)}, f32[1280,512]{1,0:T(8,128)S(1)}, u32[]{:S(2)}) copy-start(f32[1280,512]{1,0:T(8,128)S(1)} %get-tuple-element.12.acc_hbm) | copy-start | bytes 7864324
  113.9 1.1 copy-start.2
  114.9 0.8 copy-start.3
  115.8 31.8 %copy-start.4 = (s32[64]{0:T(128)S(1)}, s32[64]{0:T(128)}, u32[]{:S(2)}) copy-start(s32[64]{0:T(128)} %assign.1) | copy-start | bytes 772

commit v5 on v4

--- a/solution.py
+++ b/solution.py
@@ -43,6 +43,10 @@
 
 def in_vmem(x):
     return pltpu.with_memory_space_constraint(x, pltpu.VMEM)
+
+
+def in_smem(x):
+    return pltpu.with_memory_space_constraint(x, pltpu.SMEM)
 
 
 def in_hbm(x):
@@ -138,7 +142,7 @@
         ],
         name="near",
         compiler_params=pltpu.CompilerParams(vmem_limit_bytes=LARGE),
-    )(meta, *(in_vmem(x) for x in (here, other, pair, diag, prev)))
+    )(in_smem(meta), *(in_vmem(x) for x in (here, other, pair, diag, prev)))
 
 
 def far_part(
@@ -245,7 +249,7 @@
         ],
         name="far",
         compiler_params=pltpu.CompilerParams(vmem_limit_bytes=LARGE),
-    )(meta, in_hbm(q), in_hbm(acc), in_hbm(top), in_vmem(vert))
+    )(in_smem(meta), in_hbm(q), in_hbm(acc), in_hbm(top), in_vmem(vert))
 
 
 def cut(here_ref, o_ref, x_ref):
@@ -292,7 +296,7 @@
         out_specs=vm,
         name="newest",
         compiler_params=pltpu.CompilerParams(vmem_limit_bytes=SMALL),
-    )(meta, *(in_vmem(x) for x in (here, other, pair, diag)))
+    )(in_smem(meta), *(in_vmem(x) for x in (here, other, pair, diag)))
 
 
 def choose(spots, held_ref, o_ref):
@@ -301,41 +305,40 @@
             for j in range(MINE):
                 at = (pair * CORES + c) * MINE + j
                 mine = jnp.where(spots[PAIR_SLOTS + at] == 1, 1.0, 0.0).astype(jnp.bfloat16)
-                x = held_ref[spots[at]] * mine
-                for part in range(3):
-                    o_ref[(part * CORES + c) * 2 + pair, j] = x
+                o_ref[at] = held_ref[spots[at]] * mine
 
 
 def chosen_chunks(spots, held):
     vm = pl.BlockSpec(memory_space=pltpu.VMEM)
     return pl.pallas_call(
         choose,
-        out_shape=pltpu.VMEM((3 * CORES * 2, MINE, CH, HD), jnp.bfloat16),
+        out_shape=pltpu.VMEM((PAIR_SLOTS, CH, HD), jnp.bfloat16),
         in_specs=[pl.BlockSpec(memory_space=pltpu.SMEM), vm],
         out_specs=vm,
         name="choose",
         compiler_params=pltpu.CompilerParams(vmem_limit_bytes=SMALL),
-    )(spots, in_vmem(held))
-
-
-def add_up(x_ref, o_ref):
-    kinds = CORES * 2
-    for c in range(kinds):
-        total = x_ref[c] + x_ref[kinds + c] + x_ref[2 * kinds + c]
-        for part in range(8):
-            o_ref[part, c] = total
-
-
-def copies_of_sum(x):
+    )(in_smem(spots), in_vmem(held))
+
+
+def add_up(x_ref, one_ref, two_ref, o_ref):
+    for pair in range(2):
+        for c in range(CORES):
+            slots = slice((pair * CORES + c) * MINE, (pair * CORES + c + 1) * MINE)
+            total = x_ref[slots] + one_ref[slots] + two_ref[slots]
+            for part in range(8):
+                o_ref[(part * CORES + c) * 2 + pair] = total
+
+
+def copies_of_sum(x, one, two):
     vm = pl.BlockSpec(memory_space=pltpu.VMEM)
     return pl.pallas_call(
         add_up,
-        out_shape=jax.ShapeDtypeStruct((8, CORES * 2, MINE, CH, HD), jnp.bfloat16),
-        in_specs=[vm],
+        out_shape=pltpu.VMEM((8 * CORES * 2, MINE, CH, HD), jnp.bfloat16),
+        in_specs=[vm, vm, vm],
         out_specs=vm,
         name="add_up",
         compiler_params=pltpu.CompilerParams(vmem_limit_bytes=SMALL),
-    )(in_vmem(x))
+    )(in_vmem(x), in_vmem(one), in_vmem(two))
 
 
 def lay_out(q_ref, k_ref, v_ref, o_ref, sems):
@@ -400,7 +403,7 @@
         scratch_shapes=[pltpu.SemaphoreType.DMA((QUERY_HEADS,))],
         name="to_slots",
         compiler_params=pltpu.CompilerParams(vmem_limit_bytes=SMALL),
-    )(assign, in_vmem(x))
+    )(in_smem(assign), in_vmem(x))
 
 
 def per_device(q_rows, k_rows, v_rows, group_assign, vertical_blocks, slash_offsets):
@@ -426,7 +429,7 @@
     other = lax.ppermute(here, "c", [(0, 1), (1, 0)])
     pair = lax.ppermute(x_here, "yb", [(0, 1), (1, 0)])
     diag = lax.ppermute(x_here, ("c", "yb"), [(0, 3), (1, 2), (2, 1), (3, 0)])
-    last = last_window(place, here, other, pair, diag)
+    last = last_window(meta, here, other, pair, diag)
     kv_before = lax.ppermute(last, ("xl", "za", "zb"), [(i, i + 1) for i in range(23)])
 
     owner = verts // LB
@@ -434,9 +437,10 @@
     spot = ((owner // 24) * 8 + (z % 4) * 2 + owner % 2) * LB + verts % LB
     spots = jnp.concatenate([spot, (z // 4 == za).astype(jnp.int32)])
     chosen = chosen_chunks(spots, held.reshape(SUB * LB, CH, HD))
-    joined = lax.all_to_all(chosen, ("za", "c", "yb"), 0, 0, tiled=True)
-    spread = copies_of_sum(joined)
-    vert = lax.all_to_all(spread, ("xl", "zb"), 0, 0, tiled=True)
+    one = lax.ppermute(chosen, "za", [(0, 1), (1, 2), (2, 0)])
+    two = lax.ppermute(chosen, "za", [(0, 2), (1, 0), (2, 1)])
+    spread = copies_of_sum(chosen, one, two)
+    vert = lax.all_to_all(spread, ("xl", "zb", "c", "yb"), 0, 0, tiled=True)
     acc, top, q_here = near(meta, here, other, pair, diag, kv_before)
     out = far(meta, q_here, acc, top, vert.reshape(SUB, 2, MINE, CH, HD))
     back = lax.all_to_all(

time: 150 us -> 153 us (1.020)
  blocking collectives: 51 us -> 27 us
  starting transfers between devices: 33.3 us -> 47.4 us
  waiting for transfers between devices: 45.2 us -> 57.3 us
    all_to_all x1 -> x0, blocking collectives: 23.9 us -> none  [per_device(): joined = lax.all_to_all(chosen, ('za', 'c', 'yb'), 0, 0, tiled=True)]
    ppermute x0 -> x2, starting transfers between devices: none -> 13.8 us  [the longest x1 10.6 us: per_device(): one = lax.ppermute(chosen, 'za', [(0, 1), (1, 2), (2, 0)])]
    ppermute x0 -> x2, waiting for transfers between devices: none -> 10.3 us  [the longest x1 9.84 us: per_device(): two = lax.ppermute(chosen, 'za', [(0, 2), (1, 0), (2, 1)])]
    ppermute x1, waiting for transfers between devices: 3.19 us -> 5.09 us  [per_device(): pair = lax.ppermute(x_here, 'yb', [(0, 1), (1, 0)])]
  transfers between devices with their start and end apart: 7 -> 9, of which waited for: 5 -> 7; matrix products, arithmetic and copies ran while one was open for 1% -> 1% of each run, Pallas kernels for 3% -> 3%
where the time goes in v5:
time: 153 us; the launch traced here: 152 us
  waiting for transfers between devices  57.3 us (37%)
  starting transfers between devices  47.4 us (31%)
  blocking collectives  27 us (18%)
  Pallas kernels  15.1 us (10%)
  local copies, waits for them, and re-layouts  4.5 us (3%)
    all_to_all x1, blocking collectives, per_device(): lax.all_to_all(out.reshape(CORES * GROUPS, ROWS, SLOTS * HD), SPLIT, 0, 0...  27 us
    all_to_all x1, waiting for transfers between devices, per_device(): here = lax.all_to_all(sent, HEAD, 0, 0, tiled=True).reshape(SEQ_ROWS, WIDE)  22.3 us
    ppermute x1, starting transfers between devices, per_device(): one = lax.ppermute(chosen, 'za', [(0, 1), (1, 2), (2, 0)])  10.6 us
    ppermute x1, waiting for transfers between devices, per_device(): lax.ppermute(last, ('xl', 'za', 'zb'), [(i, i + 1) for i in range(23)])  10.4 us
    ppermute x1, waiting for transfers between devices, per_device(): two = lax.ppermute(chosen, 'za', [(0, 2), (1, 0), (2, 1)])  9.84 us
    all_to_all x1, starting transfers between devices, per_device(): here = lax.all_to_all(sent, HEAD, 0, 0, tiled=True).reshape(SEQ_ROWS, WIDE)  9.14 us
    all_to_all x1, starting transfers between devices, per_device(): held = lax.all_to_all(chunks, PART, 0, 0, tiled=True)  8.74 us
    all_to_all x1, waiting for transfers between devices, per_device(): held = lax.all_to_all(chunks, PART, 0, 0, tiled=True)  6.93 us
  transfers between devices with their start and end apart: 9, of which 7 were waited for; matrix products, arithmetic and copies ran while one was open for 1% of the time, Pallas kernels for 3%

profile of v5, /device:TPU:10, one launch (start us, length us, event | category | flops | bytes accessed | tf_op | source)
XLA Modules:
  0.0 151.8 jit_solution(12661971444839821607)
XLA Ops:
  0.0 2.4 %lay_out.1 = bf16[16,40,640]{2,1,0:T(8,128)(2,1)} custom-call(bf16[40,8192]{1,0:T(8,128)(2,1)} %q_ref.1, bf16[40,1024]{1,0:T(8,128)(2,1)} %k_ref.1, bf16[40,1024]{1,0:T(8,128)(2,1)} %v_ref.1), custom_call_target="tpu_custom_call" | custom-call | tf_op jit(solution)/shard_map/lay_out/pallas_call | solution.py:367
  2.4 9.1 %all-to-all-start = ((bf16[16,40,640]{2,1,0:T(8,128)(2,1)}), bf16[16,40,640]{2,1,0:T(8,128)(2,1)S(1)}, u32[]{:S(2)}, u32[]{:S(2)}) async-start(bf16[16,40,640]{2,1,0:T(8,128)(2,1)} %lay_out.1), calls=%async_computation | async-start | bytes 1638400 | tf_op jit(solution)/shard_map/all_to_all | solution.py:425
  12.0 0.1 copy.14
  12.1 0.1 ne.74
  12.2 22.3 %all-to-all-done = bf16[16,40,640]{2,1,0:T(8,128)(2,1)S(1)} async-done(((bf16[16,40,640]{2,1,0:T(8,128)(2,1)}), bf16[16,40,640]{2,1,0:T(8,128)(2,1)S(1)}, u32[]{:S(2)}, u32[]{:S(2)}) %all-to-all-start) | async-done | bytes 819232 | tf_op jit(solution)/shard_map/all_to_all | solution.py:425
  34.5 0.7 cut.1
  35.2 8.7 %all-to-all-start.1 = ((bf16[16,5,8,128]{3,2,1,0:T(8,128)(2,1)}), bf16[16,5,8,128]{3,2,1,0:T(8,128)(2,1)S(1)}, u32[]{:S(2)}, u32[]{:S(2)}) async-start(bf16[16,5,8,128]{3,2,1,0:T(8,128)(2,1)} %get-tuple-element.14), calls=%async_computation.1 | async-start | bytes 327680 | tf_op jit(solution)/shard_map/all_to_all | solution.py:427
  44.0 6.9 %all-to-all-done.1 = bf16[16,5,8,128]{3,2,1,0:T(8,128)(2,1)S(1)} async-done(((bf16[16,5,8,128]{3,2,1,0:T(8,128)(2,1)}), bf16[16,5,8,128]{3,2,1,0:T(8,128)(2,1)S(1)}, u32[]{:S(2)}, u32[]{:S(2)}) %all-to-all-start.1) | async-done | bytes 163872 | tf_op jit(solution)/shard_map/all_to_all | solution.py:427
  51.0 0.7 choose.1.x_ref
  51.7 10.6 %collective-permute-start.4 = (bf16[32,8,128]{2,1,0:T(8,128)(2,1)S(1)}, bf16[32,8,128]{2,1,0:T(8,128)(2,1)S(1)}, u32[]{:S(2)}, u32[]{:S(2)}) collective-permute-start(bf16[32,8,128]{2,1,0:T(8,128)(2,1)S(1)} %choose.1.x_ref), channel_id=1, source_target_pairs={{0,128},{128,256},{256,0},{1,129},{129,257},{257,1},{2,130},{130,2... | collective-permute-start | bytes 196616 | tf_op jit(solution)/shard_map/ppermute | solution.py:440
  62.3 3.2 %collective-permute-start.5 = (bf16[32,8,128]{2,1,0:T(8,128)(2,1)S(1)}, bf16[32,8,128]{2,1,0:T(8,128)(2,1)S(1)}, u32[]{:S(2)}, u32[]{:S(2)}) collective-permute-start(bf16[32,8,128]{2,1,0:T(8,128)(2,1)S(1)} %choose.1.x_ref), channel_id=1, source_target_pairs={{0,256},{128,0},{256,128},{1,257},{129,1},{257,129},{2,258},{130,2... | collective-permute-start | bytes 196616 | tf_op jit(solution)/shard_map/ppermute | solution.py:441
  65.5 0.4 collective-permute-done.4.one_ref
  65.9 9.8 %collective-permute-done.5.two_ref = bf16[32,8,128]{2,1,0:T(8,128)(2,1)S(1)} collective-permute-done((bf16[32,8,128]{2,1,0:T(8,128)(2,1)S(1)}, bf16[32,8,128]{2,1,0:T(8,128)(2,1)S(1)}, u32[]{:S(2)}, u32[]{:S(2)}) %collective-permute-start.5) | collective-permute-done | bytes 65568 | tf_op jit(solution)/shard_map/ppermute | solution.py:441
  75.7 0.8 add_up.1
  76.6 4.6 %all-to-all-start.2 = ((bf16[32,8,8,128]{3,2,1,0:T(8,128)(2,1)}), bf16[32,8,8,128]{3,2,1,0:T(8,128)(2,1)S(1)}, u32[]{:S(2)}, u32[]{:S(2)}) async-start(bf16[32,8,8,128]{3,2,1,0:T(8,128)(2,1)} %add_up.1), calls=%async_computation.2 | async-start | bytes 1048576 | tf_op jit(solution)/shard_map/all_to_all | solution.py:443
  81.2 2.0 %collective-permute-start = (bf16[640,640]{1,0:T(8,128)(2,1)S(1)}, bf16[640,640]{1,0:T(8,128)(2,1)S(1)}, u32[]{:S(2)}, u32[]{:S(2)}) collective-permute-start(bf16[640,640]{1,0:T(8,128)(2,1)S(1)} %bitcast.8), channel_id=1, source_target_pairs={{0,16},{16,0},{1,17},{17,1},{2,18},{18,2},{3,19},{19,3},{4,20},{20... | collective-permute-start | bytes 2457608 | tf_op jit(solution)/shard_map/ppermute | solution.py:429
  83.2 2.5 %collective-permute-start.1 = (bf16[640,128]{1,0:T(8,128)(2,1)S(1)}, bf16[640,128]{1,0:T(8,128)(2,1)S(1)}, u32[]{:S(2)}, u32[]{:S(2)}) collective-permute-start(bf16[640,128]{1,0:T(8,128)(2,1)S(1)} %get-tuple-element.10), channel_id=1, source_target_pairs={{0,1},{1,0},{2,3},{3,2},{4,5},{5,4},{6,7},{7,6},{8,9},{9,8},{10,11... | collective-permute-start | bytes 491528 | tf_op jit(solution)/shard_map/ppermute | solution.py:430
  85.7 3.1 %collective-permute-start.2 = (bf16[640,128]{1,0:T(8,128)(2,1)S(1)}, bf16[640,128]{1,0:T(8,128)(2,1)S(1)}, u32[]{:S(2)}, u32[]{:S(2)}) collective-permute-start(bf16[640,128]{1,0:T(8,128)(2,1)S(1)} %get-tuple-element.10), channel_id=1, source_target_pairs={{0,17},{1,16},{16,1},{17,0},{2,19},{3,18},{18,3},{19,2},{4,21},{5,... | collective-permute-start | bytes 491528 | tf_op jit(solution)/shard_map/ppermute | solution.py:431
  88.9 0.1 copy.12
  89.1 0.1 copy.13
  89.4 5.1 %collective-permute-done.1.pair_ref = bf16[640,128]{1,0:T(8,128)(2,1)S(1)} collective-permute-done((bf16[640,128]{1,0:T(8,128)(2,1)S(1)}, bf16[640,128]{1,0:T(8,128)(2,1)S(1)}, u32[]{:S(2)}, u32[]{:S(2)}) %collective-permute-start.1) | collective-permute-done | bytes 163872 | tf_op jit(solution)/shard_map/ppermute | solution.py:430
  94.5 2.3 %collective-permute-done.2.diag_ref = bf16[640,128]{1,0:T(8,128)(2,1)S(1)} collective-permute-done((bf16[640,128]{1,0:T(8,128)(2,1)S(1)}, bf16[640,128]{1,0:T(8,128)(2,1)S(1)}, u32[]{:S(2)}, u32[]{:S(2)}) %collective-permute-start.2) | collective-permute-done | bytes 163872 | tf_op jit(solution)/shard_map/ppermute | solution.py:431
  96.8 0.6 newest.1
  97.5 3.6 %collective-permute-start.3 = (bf16[640,256]{1,0:T(8,128)(2,1)S(1)}, bf16[640,256]{1,0:T(8,128)(2,1)S(1)}, u32[]{:S(2)}, u32[]{:S(2)}) collective-permute-start(bf16[640,256]{1,0:T(8,128)(2,1)S(1)} %newest.1), channel_id=1, source_target_pairs={{0,32},{32,64},{64,96},{96,128},{128,160},{160,192},{192,224},{224... | collective-permute-start | bytes 983048 | tf_op jit(solution)/shard_map/ppermute | solution.py:433
  101.1 10.4 %collective-permute-done.3.prev_ref = bf16[640,256]{1,0:T(8,128)(2,1)S(1)} collective-permute-done((bf16[640,256]{1,0:T(8,128)(2,1)S(1)}, bf16[640,256]{1,0:T(8,128)(2,1)S(1)}, u32[]{:S(2)}, u32[]{:S(2)}) %collective-permute-start.3) | collective-permute-done | bytes 327712 | tf_op jit(solution)/shard_map/ppermute | solution.py:433
  111.5 3.2 %near.1 = (f32[1280,512]{1,0:T(8,128)S(1)}, f32[1280,256]{1,0:T(8,128)S(1)}, bf16[1280,256]{1,0:T(8,128)(2,1)S(1)}) custom-call(s32[17]{0:T(128)S(1)} %concatenate.6.meta, bf16[640,640]{1,0:T(8,128)(2,1)S(1)} %bitcast.10, bf16[640,640]{1,0:T(8,128)(2,1)S(1)} %collective-permute-done.other_ref, bf16[640,128]{1,0:T(8,128)(2,1)S(1)} %collective-permute-done.1.pair_ref, ...), custom_call_target="tpu_custom_call" | custom-call | tf_op jit(solution)/shard_map/near/pallas_call | solution.py:129
  114.7 1.5 copy-done.1
  116.2 1.1 copy-done.2
  117.3 0.8 copy-done.3
  118.1 4.7 %far.1 = bf16[1280,256]{1,0:T(8,128)(2,1)S(1)} custom-call(s32[17]{0:T(128)S(1)} %concatenate.6.meta, bf16[1280,256]{1,0:T(8,128)(2,1)} %copy-done.3, f32[1280,512]{1,0:T(8,128)} %copy-done.1, f32[1280,256]{1,0:T(8,128)} %copy-done.2, bf16[16,2,8,8,128]{4,3,2,1,0:T(8,128)(2,1)S(1)} %bitcast.12), custom_call_target="tpu_custom_call" | custom-call | tf_op jit(solution)/shard_map/far/pallas_call | solution.py:237
  122.8 27.0 %all_to_all.20.x_ref = bf16[32,40,256]{2,1,0:T(8,128)(2,1)S(1)} all-to-all(bf16[32,40,256]{2,1,0:T(8,128)(2,1)S(1)} %bitcast.11), channel_id=1, replica_groups=mesh['xl'=2,'za'=3,'zb'=4,'c'=2,'xh'=2,'ya'=4,'yb'=2] {'c','xh','ya','yb'}, dimensions={0} | all-to-all | bytes 1310720 | tf_op jit(solution)/shard_map/all_to_all | solution.py:446
  149.8 2.0 %to_slots.1 = bf16[40,8192]{1,0:T(8,128)(2,1)} custom-call(s32[64]{0:T(128)S(1)} %copy-done.4, bf16[32,40,256]{2,1,0:T(8,128)(2,1)S(1)} %all_to_all.20.x_ref), custom_call_target="tpu_custom_call" | custom-call | tf_op jit(solution)/shard_map/to_slots/pallas_call | solution.py:395
  (25 shorter events, 1.0 us)
Async XLA Ops:
  0.0 89.1 %copy-start = (s32[64,3]{0,1:T(4,128)S(1)}, s32[64,3]{0,1:T(4,128)}, u32[]{:S(2)}) copy-start(s32[64,3]{0,1:T(4,128)} %param.11) | copy-start | bytes 2308
  0.0 11.5 %copy-start.5 = (s32[64,4]{0,1:T(4,128)S(1)}, s32[64,4]{0,1:T(4,128)}, u32[]{:S(2)}) copy-start(s32[64,4]{0,1:T(4,128)} %param.10) | copy-start | bytes 3076
  2.4 32.1 %all-to-all-start = ((bf16[16,40,640]{2,1,0:T(8,128)(2,1)}), bf16[16,40,640]{2,1,0:T(8,128)(2,1)S(1)}, u32[]{:S(2)}, u32[]{:S(2)}) async-start(bf16[16,40,640]{2,1,0:T(8,128)(2,1)} %lay_out.1), calls=%async_computation | async-start | bytes 1638400 | tf_op jit(solution)/shard_map/all_to_all | solution.py:425
  35.2 15.8 %all-to-all-start.1 = ((bf16[16,5,8,128]{3,2,1,0:T(8,128)(2,1)}), bf16[16,5,8,128]{3,2,1,0:T(8,128)(2,1)S(1)}, u32[]{:S(2)}, u32[]{:S(2)}) async-start(bf16[16,5,8,128]{3,2,1,0:T(8,128)(2,1)} %get-tuple-element.14), calls=%async_computation.1 | async-start | bytes 327680 | tf_op jit(solution)/shard_map/all_to_all | solution.py:427
  51.7 14.2 %collective-permute-start.4 = (bf16[32,8,128]{2,1,0:T(8,128)(2,1)S(1)}, bf16[32,8,128]{2,1,0:T(8,128)(2,1)S(1)}, u32[]{:S(2)}, u32[]{:S(2)}) collective-permute-start(bf16[32,8,128]{2,1,0:T(8,128)(2,1)S(1)} %choose.1.x_ref), channel_id=1, source_target_pairs={{0,128},{128,256},{256,0},{1,129},{129,257},{257,1},{2,130},{130,2... | collective-permute-start | bytes 196616 | tf_op jit(solution)/shard_map/ppermute | solution.py:440
  62.3 13.4 %collective-permute-start.5 = (bf16[32,8,128]{2,1,0:T(8,128)(2,1)S(1)}, bf16[32,8,128]{2,1,0:T(8,128)(2,1)S(1)}, u32[]{:S(2)}, u32[]{:S(2)}) collective-permute-start(bf16[32,8,128]{2,1,0:T(8,128)(2,1)S(1)} %choose.1.x_ref), channel_id=1, source_target_pairs={{0,256},{128,0},{256,128},{1,257},{129,1},{257,129},{2,258},{130,2... | collective-permute-start | bytes 196616 | tf_op jit(solution)/shard_map/ppermute | solution.py:441
  76.6 41.5 %all-to-all-start.2 = ((bf16[32,8,8,128]{3,2,1,0:T(8,128)(2,1)}), bf16[32,8,8,128]{3,2,1,0:T(8,128)(2,1)S(1)}, u32[]{:S(2)}, u32[]{:S(2)}) async-start(bf16[32,8,8,128]{3,2,1,0:T(8,128)(2,1)} %add_up.1), calls=%async_computation.2 | async-start | bytes 1048576 | tf_op jit(solution)/shard_map/all_to_all | solution.py:443
  81.2 15.6 %collective-permute-start = (bf16[640,640]{1,0:T(8,128)(2,1)S(1)}, bf16[640,640]{1,0:T(8,128)(2,1)S(1)}, u32[]{:S(2)}, u32[]{:S(2)}) collective-permute-start(bf16[640,640]{1,0:T(8,128)(2,1)S(1)} %bitcast.8), channel_id=1, source_target_pairs={{0,16},{16,0},{1,17},{17,1},{2,18},{18,2},{3,19},{19,3},{4,20},{20... | collective-permute-start | bytes 2457608 | tf_op jit(solution)/shard_map/ppermute | solution.py:429
  83.2 11.2 %collective-permute-start.1 = (bf16[640,128]{1,0:T(8,128)(2,1)S(1)}, bf16[640,128]{1,0:T(8,128)(2,1)S(1)}, u32[]{:S(2)}, u32[]{:S(2)}) collective-permute-start(bf16[640,128]{1,0:T(8,128)(2,1)S(1)} %get-tuple-element.10), channel_id=1, source_target_pairs={{0,1},{1,0},{2,3},{3,2},{4,5},{5,4},{6,7},{7,6},{8,9},{9,8},{10,11... | collective-permute-start | bytes 491528 | tf_op jit(solution)/shard_map/ppermute | solution.py:430
  85.7 11.1 %collective-permute-start.2 = (bf16[640,128]{1,0:T(8,128)(2,1)S(1)}, bf16[640,128]{1,0:T(8,128)(2,1)S(1)}, u32[]{:S(2)}, u32[]{:S(2)}) collective-permute-start(bf16[640,128]{1,0:T(8,128)(2,1)S(1)} %get-tuple-element.10), channel_id=1, source_target_pairs={{0,17},{1,16},{16,1},{17,0},{2,19},{3,18},{18,3},{19,2},{4,21},{5,... | collective-permute-start | bytes 491528 | tf_op jit(solution)/shard_map/ppermute | solution.py:431
  97.5 14.0 %collective-permute-start.3 = (bf16[640,256]{1,0:T(8,128)(2,1)S(1)}, bf16[640,256]{1,0:T(8,128)(2,1)S(1)}, u32[]{:S(2)}, u32[]{:S(2)}) collective-permute-start(bf16[640,256]{1,0:T(8,128)(2,1)S(1)} %newest.1), channel_id=1, source_target_pairs={{0,32},{32,64},{64,96},{96,128},{128,160},{160,192},{192,224},{224... | collective-permute-start | bytes 983048 | tf_op jit(solution)/shard_map/ppermute | solution.py:433
  114.7 1.5 copy-start.1
  116.2 1.1 copy-start.2
  117.3 0.8 copy-start.3
  118.1 31.7 %copy-start.4 = (s32[64]{0:T(128)S(1)}, s32[64]{0:T(128)}, u32[]{:S(2)}) copy-start(s32[64]{0:T(128)} %assign.1) | copy-start | bytes 772

commit v6 on v5

--- a/solution.py
+++ b/solution.py
@@ -9,6 +9,7 @@
 
 
 QUERY_HEADS = 64
+KEY_VALUE_HEADS = 8
 HD = 128
 BT = 128
 NV = 4
@@ -53,11 +54,14 @@
     return pltpu.with_memory_space_constraint(x, pltpu.HBM)
 
 
-def both_kinds(meta, here_ref, other_ref, pair_ref, diag_ref):
+def both_kinds(meta, here_ref, other_ref, pair_ref):
     own = pl.ds(pl.multiple_of(meta[2] * HD, HD), HD)
     rest = pl.ds(pl.multiple_of((1 - meta[2]) * HD, HD), HD)
     x = slice(CHIP_WIDE, WIDE)
-    return ((own, here_ref.at[:, x], other_ref.at[:, x]), (rest, pair_ref, diag_ref))
+    return (
+        (own, here_ref.at[:, x], other_ref.at[:, x]),
+        (rest, pair_ref.at[0:SEQ_ROWS], pair_ref.at[SEQ_ROWS:TOKENS]),
+    )
 
 
 def near_part(
@@ -65,14 +69,17 @@
     here_ref,
     other_ref,
     pair_ref,
-    diag_ref,
     prev_ref,
+    acc_hbm,
+    top_hbm,
+    q_hbm,
     acc_ref,
     top_ref,
     q_ref,
     win,
     kc,
     vc,
+    sems,
 ):
     first_block = meta[0]
     core = meta[1]
@@ -81,11 +88,22 @@
     mine = pl.multiple_of(core * SEQ_ROWS, SEQ_ROWS)
     theirs = pl.multiple_of((1 - core) * SEQ_ROWS, SEQ_ROWS)
     win[0:SEQ_ROWS, :] = prev_ref[...]
-    for lanes, inner, outer in both_kinds(meta, here_ref, other_ref, pair_ref, diag_ref):
+    for lanes, inner, outer in both_kinds(meta, here_ref, other_ref, pair_ref):
         win[pl.ds(SEQ_ROWS + mine, SEQ_ROWS), lanes] = inner[...]
         win[pl.ds(SEQ_ROWS + theirs, SEQ_ROWS), lanes] = outer[...]
     q_ref[pl.ds(mine, SEQ_ROWS), :] = here_ref[:, my_lanes]
     q_ref[pl.ds(theirs, SEQ_ROWS), :] = other_ref[:, my_lanes]
+    steps = TOKENS // BT // PAIR
+    whole = pltpu.make_async_copy(q_ref, q_hbm, sems.at[2, 0])
+    whole.start()
+
+    def put(step):
+        rows = pl.ds(pl.multiple_of(step * PAIR * BT, PAIR * BT), PAIR * BT)
+        return [
+            pltpu.make_async_copy(source.at[rows], target.at[rows], sems.at[n, step])
+            for n, (source, target) in enumerate(((acc_ref, acc_hbm), (top_ref, top_hbm)))
+        ]
+
     for i in range(PAIR * SLOTS):
         vc[i, :, HD : 2 * HD] = jnp.ones((NS * BT, HD), jnp.bfloat16)
     causal = lax.broadcasted_iota(jnp.int32, (BT, BT), 0) >= lax.broadcasted_iota(
@@ -119,30 +137,40 @@
                 w, vc[i], preferred_element_type=jnp.float32
             )
             top_ref[rows, h * HD : (h + 1) * HD] = top
+        for copy in put(step):
+            copy.start()
         return carry
 
-    lax.fori_loop(0, TOKENS // BT // PAIR, unit, 0)
-
-
-def near(meta, here, other, pair, diag, prev):
+    lax.fori_loop(0, steps, unit, 0)
+    whole.wait()
+    for step in range(steps):
+        for copy in put(step):
+            copy.wait()
+
+
+def near(meta, here, other, pair, prev):
     vm = pl.BlockSpec(memory_space=pltpu.VMEM)
     return pl.pallas_call(
         near_part,
         out_shape=(
-            jax.ShapeDtypeStruct((TOKENS, 2 * SLOTS * HD), jnp.float32),
-            jax.ShapeDtypeStruct((TOKENS, SLOTS * HD), jnp.float32),
-            jax.ShapeDtypeStruct((TOKENS, SLOTS * HD), jnp.bfloat16),
+            pltpu.HBM((TOKENS, 2 * SLOTS * HD), jnp.float32),
+            pltpu.HBM((TOKENS, SLOTS * HD), jnp.float32),
+            pltpu.HBM((TOKENS, SLOTS * HD), jnp.bfloat16),
         ),
-        in_specs=[pl.BlockSpec(memory_space=pltpu.SMEM), vm, vm, vm, vm, vm],
-        out_specs=(vm, vm, vm),
+        in_specs=[pl.BlockSpec(memory_space=pltpu.SMEM), vm, vm, vm, vm],
+        out_specs=tuple(pl.BlockSpec(memory_space=pltpu.HBM) for _ in range(3)),
         scratch_shapes=[
+            pltpu.VMEM((TOKENS, 2 * SLOTS * HD), jnp.float32),
+            pltpu.VMEM((TOKENS, SLOTS * HD), jnp.float32),
+            pltpu.VMEM((TOKENS, SLOTS * HD), jnp.bfloat16),
             pltpu.VMEM((TOKENS + SEQ_ROWS, 2 * HD), jnp.bfloat16),
             pltpu.VMEM((PAIR * SLOTS, NS * BT, HD), jnp.bfloat16),
             pltpu.VMEM((PAIR * SLOTS, NS * BT, 2 * HD), jnp.bfloat16),
+            pltpu.SemaphoreType.DMA((3, TOKENS // BT // PAIR)),
         ],
         name="near",
         compiler_params=pltpu.CompilerParams(vmem_limit_bytes=LARGE),
-    )(in_smem(meta), *(in_vmem(x) for x in (here, other, pair, diag, prev)))
+    )(in_smem(meta), *(in_vmem(x) for x in (here, other, pair, prev)))
 
 
 def far_part(
@@ -252,8 +280,7 @@
     )(in_smem(meta), in_hbm(q), in_hbm(acc), in_hbm(top), in_vmem(vert))
 
 
-def cut(here_ref, o_ref, x_ref):
-    x_ref[...] = here_ref[:, CHIP_WIDE:WIDE]
+def cut(here_ref, o_ref):
     for j in range(LB):
         x = here_ref[j * BT : (j + 1) * BT, CHIP_WIDE:WIDE].astype(jnp.float32)
         for r in range(SUB):
@@ -264,19 +291,33 @@
     vm = pl.BlockSpec(memory_space=pltpu.VMEM)
     return pl.pallas_call(
         cut,
-        out_shape=(
-            pltpu.VMEM((SUB, LB, CH, HD), jnp.bfloat16),
-            pltpu.VMEM((SEQ_ROWS, HD), jnp.bfloat16),
-        ),
+        out_shape=pltpu.VMEM((SUB, LB, CH, HD), jnp.bfloat16),
         in_specs=[vm],
-        out_specs=(vm, vm),
+        out_specs=vm,
         name="cut",
         compiler_params=pltpu.CompilerParams(vmem_limit_bytes=SMALL),
     )(in_vmem(here))
 
 
-def newest(meta, here_ref, other_ref, pair_ref, diag_ref, o_ref):
-    for lanes, inner, outer in both_kinds(meta, here_ref, other_ref, pair_ref, diag_ref):
+def stack(here_ref, other_ref, o_ref):
+    o_ref[0:SEQ_ROWS, :] = here_ref[:, CHIP_WIDE:WIDE]
+    o_ref[SEQ_ROWS:TOKENS, :] = other_ref[:, CHIP_WIDE:WIDE]
+
+
+def both_windows(here, other):
+    vm = pl.BlockSpec(memory_space=pltpu.VMEM)
+    return pl.pallas_call(
+        stack,
+        out_shape=pltpu.VMEM((TOKENS, HD), jnp.bfloat16),
+        in_specs=[vm, vm],
+        out_specs=vm,
+        name="stack",
+        compiler_params=pltpu.CompilerParams(vmem_limit_bytes=SMALL),
+    )(in_vmem(here), in_vmem(other))
+
+
+def newest(meta, here_ref, other_ref, pair_ref, o_ref):
+    for lanes, inner, outer in both_kinds(meta, here_ref, other_ref, pair_ref):
 
         @pl.when(meta[1] == 1)
         def _():
@@ -287,16 +328,16 @@
             o_ref[:, lanes] = outer[...]
 
 
-def last_window(meta, here, other, pair, diag):
+def last_window(meta, here, other, pair):
     vm = pl.BlockSpec(memory_space=pltpu.VMEM)
     return pl.pallas_call(
         newest,
         out_shape=pltpu.VMEM((SEQ_ROWS, 2 * HD), jnp.bfloat16),
-        in_specs=[pl.BlockSpec(memory_space=pltpu.SMEM), vm, vm, vm, vm],
+        in_specs=[pl.BlockSpec(memory_space=pltpu.SMEM), vm, vm, vm],
         out_specs=vm,
         name="newest",
         compiler_params=pltpu.CompilerParams(vmem_limit_bytes=SMALL),
-    )(in_smem(meta), *(in_vmem(x) for x in (here, other, pair, diag)))
+    )(in_smem(meta), *(in_vmem(x) for x in (here, other, pair)))
 
 
 def choose(spots, held_ref, o_ref):
@@ -341,35 +382,42 @@
     )(in_vmem(x), in_vmem(one), in_vmem(two))
 
 
-def lay_out(q_ref, k_ref, v_ref, o_ref, sems):
-    copies = []
+def lay_out(q_hbm, k_hbm, v_hbm, o_ref, q_ref, k_ref, v_ref, sems):
+    step = 8
+    copies = [
+        pltpu.make_async_copy(k_hbm, k_ref, sems.at[0]),
+        pltpu.make_async_copy(v_hbm, v_ref, sems.at[1]),
+    ]
+    for n, row in enumerate(range(0, ROWS, step)):
+        rows = pl.ds(row, step)
+        copies.append(pltpu.make_async_copy(q_hbm.at[rows], q_ref.at[rows], sems.at[2 + n]))
+    for copy in copies:
+        copy.start()
+    copies[0].wait()
+    copies[1].wait()
     for g in range(GROUPS):
         m = g // 2 * HD
-        for n, (ref, start, at, size) in enumerate(
-            (
-                (q_ref, g * CHIP_WIDE, 0, CHIP_WIDE),
-                (v_ref if g % 2 else k_ref, m, CHIP_WIDE, HD),
-            )
-        ):
-            copies.append(
-                pltpu.make_async_copy(
-                    ref.at[:, pl.ds(start, size)], o_ref.at[g, :, pl.ds(at, size)], sems.at[n, g]
-                )
-            )
-    for copy in copies:
-        copy.start()
-    for copy in copies:
-        copy.wait()
+        o_ref[g, :, CHIP_WIDE:WIDE] = (v_ref if g % 2 else k_ref)[:, m : m + HD]
+    for n, row in enumerate(range(0, ROWS, step)):
+        copies[2 + n].wait()
+        for g in range(GROUPS):
+            o_ref[g, row : row + step, 0:CHIP_WIDE] = q_ref[
+                row : row + step, g * CHIP_WIDE : (g + 1) * CHIP_WIDE
+            ]
 
 
 def pack(q, k, v):
-    anywhere = pl.BlockSpec(memory_space=pltpu.HBM)
     return pl.pallas_call(
         lay_out,
         out_shape=pltpu.VMEM((GROUPS, ROWS, WIDE), jnp.bfloat16),
-        in_specs=[anywhere] * 3,
+        in_specs=[pl.BlockSpec(memory_space=pltpu.HBM)] * 3,
         out_specs=pl.BlockSpec(memory_space=pltpu.VMEM),
-        scratch_shapes=[pltpu.SemaphoreType.DMA((2, GROUPS))],
+        scratch_shapes=[
+            pltpu.VMEM((ROWS, QUERY_HEADS * HD), jnp.bfloat16),
+            pltpu.VMEM((ROWS, KEY_VALUE_HEADS * HD), jnp.bfloat16),
+            pltpu.VMEM((ROWS, KEY_VALUE_HEADS * HD), jnp.bfloat16),
+            pltpu.SemaphoreType.DMA((2 + ROWS // 8,)),
+        ],
         name="lay_out",
         compiler_params=pltpu.CompilerParams(vmem_limit_bytes=SMALL),
     )(in_hbm(q), in_hbm(k), in_hbm(v))
@@ -423,13 +471,12 @@
 
     sent = pack(q_rows, k_rows, v_rows)
     here = lax.all_to_all(sent, HEAD, 0, 0, tiled=True).reshape(SEQ_ROWS, WIDE)
-    chunks, x_here = in_chunks(here)
-    held = lax.all_to_all(chunks, PART, 0, 0, tiled=True)
+    held = lax.all_to_all(in_chunks(here), PART, 0, 0, tiled=True)
 
     other = lax.ppermute(here, "c", [(0, 1), (1, 0)])
-    pair = lax.ppermute(x_here, "yb", [(0, 1), (1, 0)])
-    diag = lax.ppermute(x_here, ("c", "yb"), [(0, 3), (1, 2), (2, 1), (3, 0)])
-    last = last_window(meta, here, other, pair, diag)
+    windows = both_windows(here, other)
+    pair = lax.ppermute(windows, "yb", [(0, 1), (1, 0)])
+    last = last_window(meta, here, other, pair)
     kv_before = lax.ppermute(last, ("xl", "za", "zb"), [(i, i + 1) for i in range(23)])
 
     owner = verts // LB
@@ -441,7 +488,7 @@
     two = lax.ppermute(chosen, "za", [(0, 2), (1, 0), (2, 1)])
     spread = copies_of_sum(chosen, one, two)
     vert = lax.all_to_all(spread, ("xl", "zb", "c", "yb"), 0, 0, tiled=True)
-    acc, top, q_here = near(meta, here, other, pair, diag, kv_before)
+    acc, top, q_here = near(meta, here, other, pair, kv_before)
     out = far(meta, q_here, acc, top, vert.reshape(SUB, 2, MINE, CH, HD))
     back = lax.all_to_all(
         out.reshape(CORES * GROUPS, ROWS, SLOTS * HD), SPLIT, 0, 0, tiled=True

time: 153 us -> 151 us (0.987)
  waiting for transfers between devices: 57.3 us -> 63 us
  starting transfers between devices: 47.4 us -> 43.4 us
  local copies, waits for them, and re-layouts: 4.5 us -> 1.11 us
    unnamed x12 -> x6, local copies, waits for them, and re-layouts: 3.39 us -> 0.01 us
    ppermute x2 -> x1, waiting for transfers between devices: 7.43 us -> 10.6 us  [per_device(): pair = lax.ppermute(windows, 'yb', [(0, 1), (1, 0)])]
    ppermute x2 -> x1, starting transfers between devices: 5.55 us -> 2.46 us  [per_device(): pair = lax.ppermute(windows, 'yb', [(0, 1), (1, 0)])]
    ppermute x1, waiting for transfers between devices: 0.01 us -> 2.18 us  [per_device(): other = lax.ppermute(here, 'c', [(0, 1), (1, 0)])]
    pallas_call x2 -> x3, Pallas kernels: 3.92 us -> 5.25 us  [the longest x1 4.5 us: near(): pl.pallas_call(near_part, out_shape=(pltpu.HBM((TOKENS, 2 * SLOTS * HD),...]
  transfers between devices with their start and end apart: 9 -> 8, of which waited for: 7 -> 7; matrix products, arithmetic and copies ran while one was open for 1% -> 1% of each run, Pallas kernels for 3% -> 3%
where the time goes in v6:
time: 151 us
  waiting for transfers between devices  63 us (42%)
  starting transfers between devices  43.4 us (29%)
  blocking collectives  26.7 us (18%)
  Pallas kernels  16.3 us (11%)
    all_to_all x1, blocking collectives, per_device(): lax.all_to_all(out.reshape(CORES * GROUPS, ROWS, SLOTS * HD), SPLIT, 0, 0...  26.7 us
    all_to_all x1, waiting for transfers between devices, per_device(): here = lax.all_to_all(sent, HEAD, 0, 0, tiled=True).reshape(SEQ_ROWS, WIDE)  22.3 us
    ppermute x1, waiting for transfers between devices, per_device(): lax.ppermute(last, ('xl', 'za', 'zb'), [(i, i + 1) for i in range(23)])  10.7 us
    ppermute x1, starting transfers between devices, per_device(): one = lax.ppermute(chosen, 'za', [(0, 1), (1, 2), (2, 0)])  10.6 us
    ppermute x1, waiting for transfers between devices, per_device(): pair = lax.ppermute(windows, 'yb', [(0, 1), (1, 0)])  10.6 us
    ppermute x1, waiting for transfers between devices, per_device(): two = lax.ppermute(chosen, 'za', [(0, 2), (1, 0), (2, 1)])  9.84 us
    all_to_all x1, starting transfers between devices, per_device(): here = lax.all_to_all(sent, HEAD, 0, 0, tiled=True).reshape(SEQ_ROWS, WIDE)  9.14 us
    all_to_all x1, starting transfers between devices, per_device(): held = lax.all_to_all(in_chunks(here), PART, 0, 0, tiled=True)  8.74 us
  transfers between devices with their start and end apart: 8, of which 7 were waited for; matrix products, arithmetic and copies ran while one was open for 1% of the time, Pallas kernels for 3%

profile of v6, /device:TPU:10, one launch (start us, length us, event | category | flops | bytes accessed | tf_op | source)
XLA Modules:
  0.0 150.8 jit_solution(17314383608034560454)
XLA Ops:
  0.0 2.2 %lay_out.1 = bf16[16,40,640]{2,1,0:T(8,128)(2,1)} custom-call(bf16[40,8192]{1,0:T(8,128)(2,1)} %q_hbm.1, bf16[40,1024]{1,0:T(8,128)(2,1)} %k_hbm.1, bf16[40,1024]{1,0:T(8,128)(2,1)} %v_hbm.1), custom_call_target="tpu_custom_call" | custom-call | tf_op jit(solution)/shard_map/lay_out/pallas_call | solution.py:410
  2.2 9.1 %all-to-all-start = ((bf16[16,40,640]{2,1,0:T(8,128)(2,1)}), bf16[16,40,640]{2,1,0:T(8,128)(2,1)S(1)}, u32[]{:S(2)}, u32[]{:S(2)}) async-start(bf16[16,40,640]{2,1,0:T(8,128)(2,1)} %lay_out.1), calls=%async_computation | async-start | bytes 1638400 | tf_op jit(solution)/shard_map/all_to_all | solution.py:473
  11.4 0.1 dynamic-slice_divide_fusion
  11.4 0.1 copy.15
  11.9 0.1 copy.14
  11.9 0.1 ne.74
  12.0 22.3 %all-to-all-done = bf16[16,40,640]{2,1,0:T(8,128)(2,1)S(1)} async-done(((bf16[16,40,640]{2,1,0:T(8,128)(2,1)}), bf16[16,40,640]{2,1,0:T(8,128)(2,1)S(1)}, u32[]{:S(2)}, u32[]{:S(2)}) %all-to-all-start) | async-done | bytes 819232 | tf_op jit(solution)/shard_map/all_to_all | solution.py:473
  34.3 0.7 cut.1
  35.0 8.7 %all-to-all-start.1 = ((bf16[16,5,8,128]{3,2,1,0:T(8,128)(2,1)}), bf16[16,5,8,128]{3,2,1,0:T(8,128)(2,1)S(1)}, u32[]{:S(2)}, u32[]{:S(2)}) async-start(bf16[16,5,8,128]{3,2,1,0:T(8,128)(2,1)} %cut.1), calls=%async_computation.1 | async-start | bytes 327680 | tf_op jit(solution)/shard_map/all_to_all | solution.py:474
  43.9 6.9 %all-to-all-done.1 = bf16[16,5,8,128]{3,2,1,0:T(8,128)(2,1)S(1)} async-done(((bf16[16,5,8,128]{3,2,1,0:T(8,128)(2,1)}), bf16[16,5,8,128]{3,2,1,0:T(8,128)(2,1)S(1)}, u32[]{:S(2)}, u32[]{:S(2)}) %all-to-all-start.1) | async-done | bytes 163872 | tf_op jit(solution)/shard_map/all_to_all | solution.py:474
  50.8 0.7 choose.1.x_ref
  51.5 10.6 %collective-permute-start.3 = (bf16[32,8,128]{2,1,0:T(8,128)(2,1)S(1)}, bf16[32,8,128]{2,1,0:T(8,128)(2,1)S(1)}, u32[]{:S(2)}, u32[]{:S(2)}) collective-permute-start(bf16[32,8,128]{2,1,0:T(8,128)(2,1)S(1)} %choose.1.x_ref), channel_id=1, source_target_pairs={{0,128},{128,256},{256,0},{1,129},{129,257},{257,1},{2,130},{130,2... | collective-permute-start | bytes 196616 | tf_op jit(solution)/shard_map/ppermute | solution.py:487
  62.2 3.2 %collective-permute-start.4 = (bf16[32,8,128]{2,1,0:T(8,128)(2,1)S(1)}, bf16[32,8,128]{2,1,0:T(8,128)(2,1)S(1)}, u32[]{:S(2)}, u32[]{:S(2)}) collective-permute-start(bf16[32,8,128]{2,1,0:T(8,128)(2,1)S(1)} %choose.1.x_ref), channel_id=1, source_target_pairs={{0,256},{128,0},{256,128},{1,257},{129,1},{257,129},{2,258},{130,2... | collective-permute-start | bytes 196616 | tf_op jit(solution)/shard_map/ppermute | solution.py:488
  65.3 0.4 collective-permute-done.3.one_ref
  65.7 9.8 %collective-permute-done.4.two_ref = bf16[32,8,128]{2,1,0:T(8,128)(2,1)S(1)} collective-permute-done((bf16[32,8,128]{2,1,0:T(8,128)(2,1)S(1)}, bf16[32,8,128]{2,1,0:T(8,128)(2,1)S(1)}, u32[]{:S(2)}, u32[]{:S(2)}) %collective-permute-start.4) | collective-permute-done | bytes 65568 | tf_op jit(solution)/shard_map/ppermute | solution.py:488
  75.6 0.8 add_up.1
  76.4 4.6 %all-to-all-start.2 = ((bf16[32,8,8,128]{3,2,1,0:T(8,128)(2,1)}), bf16[32,8,8,128]{3,2,1,0:T(8,128)(2,1)S(1)}, u32[]{:S(2)}, u32[]{:S(2)}) async-start(bf16[32,8,8,128]{3,2,1,0:T(8,128)(2,1)} %add_up.1), calls=%async_computation.2 | async-start | bytes 1048576 | tf_op jit(solution)/shard_map/all_to_all | solution.py:490
  81.0 2.0 %collective-permute-start = (bf16[640,640]{1,0:T(8,128)(2,1)S(1)}, bf16[640,640]{1,0:T(8,128)(2,1)S(1)}, u32[]{:S(2)}, u32[]{:S(2)}) collective-permute-start(bf16[640,640]{1,0:T(8,128)(2,1)S(1)} %bitcast.8), channel_id=1, source_target_pairs={{0,16},{16,0},{1,17},{17,1},{2,18},{18,2},{3,19},{19,3},{4,20},{20... | collective-permute-start | bytes 2457608 | tf_op jit(solution)/shard_map/ppermute | solution.py:476
  83.1 2.2 %collective-permute-done.other_ref = bf16[640,640]{1,0:T(8,128)(2,1)S(1)} collective-permute-done((bf16[640,640]{1,0:T(8,128)(2,1)S(1)}, bf16[640,640]{1,0:T(8,128)(2,1)S(1)}, u32[]{:S(2)}, u32[]{:S(2)}) %collective-permute-start) | collective-permute-done | bytes 819232 | tf_op jit(solution)/shard_map/ppermute | solution.py:476
  85.3 2.5 %collective-permute-start.1 = (bf16[1280,128]{1,0:T(8,128)(2,1)S(1)}, bf16[1280,128]{1,0:T(8,128)(2,1)S(1)}, u32[]{:S(2)}, u32[]{:S(2)}) collective-permute-start(bf16[1280,128]{1,0:T(8,128)(2,1)S(1)} %stack.13), channel_id=1, source_target_pairs={{0,1},{1,0},{2,3},{3,2},{4,5},{5,4},{6,7},{7,6},{8,9},{9,8},{10,11... | collective-permute-start | bytes 983048 | tf_op jit(solution)/shard_map/ppermute | solution.py:478
  87.9 0.1 copy.12
  88.0 0.1 reshape.26
  88.1 0.1 copy.13
  88.2 0.1 reshape.27
  88.4 10.6 %collective-permute-done.1.pair_ref = bf16[1280,128]{1,0:T(8,128)(2,1)S(1)} collective-permute-done((bf16[1280,128]{1,0:T(8,128)(2,1)S(1)}, bf16[1280,128]{1,0:T(8,128)(2,1)S(1)}, u32[]{:S(2)}, u32[]{:S(2)}) %collective-permute-start.1) | collective-permute-done | bytes 327712 | tf_op jit(solution)/shard_map/ppermute | solution.py:478
  98.9 0.6 newest.1
  99.6 2.6 %collective-permute-start.2 = (bf16[640,256]{1,0:T(8,128)(2,1)S(1)}, bf16[640,256]{1,0:T(8,128)(2,1)S(1)}, u32[]{:S(2)}, u32[]{:S(2)}) collective-permute-start(bf16[640,256]{1,0:T(8,128)(2,1)S(1)} %newest.1), channel_id=1, source_target_pairs={{0,32},{32,64},{64,96},{96,128},{128,160},{160,192},{192,224},{224... | collective-permute-start | bytes 983048 | tf_op jit(solution)/shard_map/ppermute | solution.py:480
  102.2 10.7 %collective-permute-done.2.prev_ref = bf16[640,256]{1,0:T(8,128)(2,1)S(1)} collective-permute-done((bf16[640,256]{1,0:T(8,128)(2,1)S(1)}, bf16[640,256]{1,0:T(8,128)(2,1)S(1)}, u32[]{:S(2)}, u32[]{:S(2)}) %collective-permute-start.2) | collective-permute-done | bytes 327712 | tf_op jit(solution)/shard_map/ppermute | solution.py:480
  112.9 4.5 %near.1 = (f32[1280,512]{1,0:T(8,128)}, f32[1280,256]{1,0:T(8,128)}, bf16[1280,256]{1,0:T(8,128)(2,1)}) custom-call(s32[17]{0:T(128)S(1)} %concatenate.6.meta, bf16[640,640]{1,0:T(8,128)(2,1)S(1)} %bitcast.11, bf16[640,640]{1,0:T(8,128)(2,1)S(1)} %collective-permute-done.other_ref, bf16[1280,128]{1,0:T(8,128)(2,1)S(1)} %collective-permute-done.1.pair_ref, ...), custom_call_target="tpu_custom_call" | custom-call | tf_op jit(solution)/shard_map/near/pallas_call | solution.py:153
  117.4 4.7 %far.1 = bf16[1280,256]{1,0:T(8,128)(2,1)S(1)} custom-call(s32[17]{0:T(128)S(1)} %concatenate.6.meta, bf16[1280,256]{1,0:T(8,128)(2,1)} %get-tuple-element.8.q_hbm, f32[1280,512]{1,0:T(8,128)} %get-tuple-element.9.acc_hbm, f32[1280,256]{1,0:T(8,128)} %get-tuple-element.10.top_hbm, bf16[16,2,8,8,128]{4,3,2,1,0:T(8,128)(2,1)S(1)} %bitcast.13), custom_call_target="tpu_custom_call" | custom-call | tf_op jit(solution)/shard_map/far/pallas_call | solution.py:265
  122.1 26.7 %all_to_all.20.x_ref = bf16[32,40,256]{2,1,0:T(8,128)(2,1)S(1)} all-to-all(bf16[32,40,256]{2,1,0:T(8,128)(2,1)S(1)} %bitcast.12), channel_id=1, replica_groups=mesh['xl'=2,'za'=3,'zb'=4,'c'=2,'xh'=2,'ya'=4,'yb'=2] {'c','xh','ya','yb'}, dimensions={0} | all-to-all | bytes 1310720 | tf_op jit(solution)/shard_map/all_to_all | solution.py:493
  148.8 2.0 %to_slots.1 = bf16[40,8192]{1,0:T(8,128)(2,1)} custom-call(s32[64]{0:T(128)S(1)} %copy-done.1, bf16[32,40,256]{2,1,0:T(8,128)(2,1)S(1)} %all_to_all.20.x_ref), custom_call_target="tpu_custom_call" | custom-call | tf_op jit(solution)/shard_map/to_slots/pallas_call | solution.py:443
  (18 shorter events, 0.7 us)
Async XLA Ops:
  0.0 88.0 %copy-start = (s32[64,3]{0,1:T(4,128)S(1)}, s32[64,3]{0,1:T(4,128)}, u32[]{:S(2)}) copy-start(s32[64,3]{0,1:T(4,128)} %param.11) | copy-start | bytes 2308
  0.0 11.4 %copy-start.2 = (s32[64,4]{0,1:T(4,128)S(1)}, s32[64,4]{0,1:T(4,128)}, u32[]{:S(2)}) copy-start(s32[64,4]{0,1:T(4,128)} %param.10) | copy-start | bytes 3076
  2.2 32.1 %all-to-all-start = ((bf16[16,40,640]{2,1,0:T(8,128)(2,1)}), bf16[16,40,640]{2,1,0:T(8,128)(2,1)S(1)}, u32[]{:S(2)}, u32[]{:S(2)}) async-start(bf16[16,40,640]{2,1,0:T(8,128)(2,1)} %lay_out.1), calls=%async_computation | async-start | bytes 1638400 | tf_op jit(solution)/shard_map/all_to_all | solution.py:473
  35.0 15.8 %all-to-all-start.1 = ((bf16[16,5,8,128]{3,2,1,0:T(8,128)(2,1)}), bf16[16,5,8,128]{3,2,1,0:T(8,128)(2,1)S(1)}, u32[]{:S(2)}, u32[]{:S(2)}) async-start(bf16[16,5,8,128]{3,2,1,0:T(8,128)(2,1)} %cut.1), calls=%async_computation.1 | async-start | bytes 327680 | tf_op jit(solution)/shard_map/all_to_all | solution.py:474
  51.5 14.2 %collective-permute-start.3 = (bf16[32,8,128]{2,1,0:T(8,128)(2,1)S(1)}, bf16[32,8,128]{2,1,0:T(8,128)(2,1)S(1)}, u32[]{:S(2)}, u32[]{:S(2)}) collective-permute-start(bf16[32,8,128]{2,1,0:T(8,128)(2,1)S(1)} %choose.1.x_ref), channel_id=1, source_target_pairs={{0,128},{128,256},{256,0},{1,129},{129,257},{257,1},{2,130},{130,2... | collective-permute-start | bytes 196616 | tf_op jit(solution)/shard_map/ppermute | solution.py:487
  62.2 13.4 %collective-permute-start.4 = (bf16[32,8,128]{2,1,0:T(8,128)(2,1)S(1)}, bf16[32,8,128]{2,1,0:T(8,128)(2,1)S(1)}, u32[]{:S(2)}, u32[]{:S(2)}) collective-permute-start(bf16[32,8,128]{2,1,0:T(8,128)(2,1)S(1)} %choose.1.x_ref), channel_id=1, source_target_pairs={{0,256},{128,0},{256,128},{1,257},{129,1},{257,129},{2,258},{130,2... | collective-permute-start | bytes 196616 | tf_op jit(solution)/shard_map/ppermute | solution.py:488
  76.4 41.0 %all-to-all-start.2 = ((bf16[32,8,8,128]{3,2,1,0:T(8,128)(2,1)}), bf16[32,8,8,128]{3,2,1,0:T(8,128)(2,1)S(1)}, u32[]{:S(2)}, u32[]{:S(2)}) async-start(bf16[32,8,8,128]{3,2,1,0:T(8,128)(2,1)} %add_up.1), calls=%async_computation.2 | async-start | bytes 1048576 | tf_op jit(solution)/shard_map/all_to_all | solution.py:490
  81.0 4.2 %collective-permute-start = (bf16[640,640]{1,0:T(8,128)(2,1)S(1)}, bf16[640,640]{1,0:T(8,128)(2,1)S(1)}, u32[]{:S(2)}, u32[]{:S(2)}) collective-permute-start(bf16[640,640]{1,0:T(8,128)(2,1)S(1)} %bitcast.8), channel_id=1, source_target_pairs={{0,16},{16,0},{1,17},{17,1},{2,18},{18,2},{3,19},{19,3},{4,20},{20... | collective-permute-start | bytes 2457608 | tf_op jit(solution)/shard_map/ppermute | solution.py:476
  85.3 13.6 %collective-permute-start.1 = (bf16[1280,128]{1,0:T(8,128)(2,1)S(1)}, bf16[1280,128]{1,0:T(8,128)(2,1)S(1)}, u32[]{:S(2)}, u32[]{:S(2)}) collective-permute-start(bf16[1280,128]{1,0:T(8,128)(2,1)S(1)} %stack.13), channel_id=1, source_target_pairs={{0,1},{1,0},{2,3},{3,2},{4,5},{5,4},{6,7},{7,6},{8,9},{9,8},{10,11... | collective-permute-start | bytes 983048 | tf_op jit(solution)/shard_map/ppermute | solution.py:478
  99.6 13.3 %collective-permute-start.2 = (bf16[640,256]{1,0:T(8,128)(2,1)S(1)}, bf16[640,256]{1,0:T(8,128)(2,1)S(1)}, u32[]{:S(2)}, u32[]{:S(2)}) collective-permute-start(bf16[640,256]{1,0:T(8,128)(2,1)S(1)} %newest.1), channel_id=1, source_target_pairs={{0,32},{32,64},{64,96},{96,128},{128,160},{160,192},{192,224},{224... | collective-permute-start | bytes 983048 | tf_op jit(solution)/shard_map/ppermute | solution.py:480
  117.4 31.3 %copy-start.1 = (s32[64]{0:T(128)S(1)}, s32[64]{0:T(128)}, u32[]{:S(2)}) copy-start(s32[64]{0:T(128)} %assign.1) | copy-start | bytes 772

commit v7 on v6

--- a/solution.py
+++ b/solution.py
@@ -24,13 +24,13 @@
 CHIP_WIDE = CORES * SLOTS * HD
 WIDE = CHIP_WIDE + HD
 MINE = SLOTS * NV
-PAIR_SLOTS = 2 * CORES * MINE
 CH = 8
+PARTS = 3
 SUB = 16
 ALL = ("xl", "za", "zb", "c", "xh", "ya", "yb")
+SEQ = ("xl", "za", "zb", "c")
 HEAD = ("xh", "ya", "yb")
 SPLIT = ("c", "xh", "ya", "yb")
-PART = ("xl", "zb", "c")
 SCALE = 1.0 / math.sqrt(HD)
 NEG = float("-inf")
 SMALL = 4 * 1024 * 1024
@@ -54,14 +54,11 @@
     return pltpu.with_memory_space_constraint(x, pltpu.HBM)
 
 
-def both_kinds(meta, here_ref, other_ref, pair_ref):
+def both_kinds(meta, here_ref, other_ref, pair_ref, diag_ref):
     own = pl.ds(pl.multiple_of(meta[2] * HD, HD), HD)
     rest = pl.ds(pl.multiple_of((1 - meta[2]) * HD, HD), HD)
     x = slice(CHIP_WIDE, WIDE)
-    return (
-        (own, here_ref.at[:, x], other_ref.at[:, x]),
-        (rest, pair_ref.at[0:SEQ_ROWS], pair_ref.at[SEQ_ROWS:TOKENS]),
-    )
+    return ((own, here_ref.at[:, x], other_ref.at[:, x]), (rest, pair_ref, diag_ref))
 
 
 def near_part(
@@ -69,6 +66,7 @@
     here_ref,
     other_ref,
     pair_ref,
+    diag_ref,
     prev_ref,
     acc_hbm,
     top_hbm,
@@ -88,7 +86,7 @@
     mine = pl.multiple_of(core * SEQ_ROWS, SEQ_ROWS)
     theirs = pl.multiple_of((1 - core) * SEQ_ROWS, SEQ_ROWS)
     win[0:SEQ_ROWS, :] = prev_ref[...]
-    for lanes, inner, outer in both_kinds(meta, here_ref, other_ref, pair_ref):
+    for lanes, inner, outer in both_kinds(meta, here_ref, other_ref, pair_ref, diag_ref):
         win[pl.ds(SEQ_ROWS + mine, SEQ_ROWS), lanes] = inner[...]
         win[pl.ds(SEQ_ROWS + theirs, SEQ_ROWS), lanes] = outer[...]
     q_ref[pl.ds(mine, SEQ_ROWS), :] = here_ref[:, my_lanes]
@@ -148,7 +146,7 @@
             copy.wait()
 
 
-def near(meta, here, other, pair, prev):
+def near(meta, here, other, pair, diag, prev):
     vm = pl.BlockSpec(memory_space=pltpu.VMEM)
     return pl.pallas_call(
         near_part,
@@ -157,7 +155,7 @@
             pltpu.HBM((TOKENS, SLOTS * HD), jnp.float32),
             pltpu.HBM((TOKENS, SLOTS * HD), jnp.bfloat16),
         ),
-        in_specs=[pl.BlockSpec(memory_space=pltpu.SMEM), vm, vm, vm, vm],
+        in_specs=[pl.BlockSpec(memory_space=pltpu.SMEM), vm, vm, vm, vm, vm],
         out_specs=tuple(pl.BlockSpec(memory_space=pltpu.HBM) for _ in range(3)),
         scratch_shapes=[
             pltpu.VMEM((TOKENS, 2 * SLOTS * HD), jnp.float32),
@@ -170,7 +168,7 @@
         ],
         name="near",
         compiler_params=pltpu.CompilerParams(vmem_limit_bytes=LARGE),
-    )(in_smem(meta), *(in_vmem(x) for x in (here, other, pair, prev)))
+    )(in_smem(meta), *(in_vmem(x) for x in (here, other, pair, diag, prev)))
 
 
 def far_part(
@@ -280,44 +278,33 @@
     )(in_smem(meta), in_hbm(q), in_hbm(acc), in_hbm(top), in_vmem(vert))
 
 
-def cut(here_ref, o_ref):
+def cut(here_ref, o_ref, x_ref):
+    x_ref[...] = here_ref[:, CHIP_WIDE:WIDE]
     for j in range(LB):
         x = here_ref[j * BT : (j + 1) * BT, CHIP_WIDE:WIDE].astype(jnp.float32)
         for r in range(SUB):
-            o_ref[r, j] = x[r * CH : (r + 1) * CH].astype(jnp.bfloat16)
+            chunk = x[r * CH : (r + 1) * CH].astype(jnp.bfloat16)
+            for part in range(PARTS):
+                o_ref[r // 8 * 8 * PARTS + part * 8 + r % 8, j] = chunk
 
 
 def in_chunks(here):
     vm = pl.BlockSpec(memory_space=pltpu.VMEM)
     return pl.pallas_call(
         cut,
-        out_shape=pltpu.VMEM((SUB, LB, CH, HD), jnp.bfloat16),
+        out_shape=(
+            pltpu.VMEM((SUB * PARTS, LB, CH, HD), jnp.bfloat16),
+            pltpu.VMEM((SEQ_ROWS, HD), jnp.bfloat16),
+        ),
         in_specs=[vm],
-        out_specs=vm,
+        out_specs=(vm, vm),
         name="cut",
         compiler_params=pltpu.CompilerParams(vmem_limit_bytes=SMALL),
     )(in_vmem(here))
 
 
-def stack(here_ref, other_ref, o_ref):
-    o_ref[0:SEQ_ROWS, :] = here_ref[:, CHIP_WIDE:WIDE]
-    o_ref[SEQ_ROWS:TOKENS, :] = other_ref[:, CHIP_WIDE:WIDE]
-
-
-def both_windows(here, other):
-    vm = pl.BlockSpec(memory_space=pltpu.VMEM)
-    return pl.pallas_call(
-        stack,
-        out_shape=pltpu.VMEM((TOKENS, HD), jnp.bfloat16),
-        in_specs=[vm, vm],
-        out_specs=vm,
-        name="stack",
-        compiler_params=pltpu.CompilerParams(vmem_limit_bytes=SMALL),
-    )(in_vmem(here), in_vmem(other))
-
-
-def newest(meta, here_ref, other_ref, pair_ref, o_ref):
-    for lanes, inner, outer in both_kinds(meta, here_ref, other_ref, pair_ref):
+def newest(meta, here_ref, other_ref, pair_ref, diag_ref, o_ref):
+    for lanes, inner, outer in both_kinds(meta, here_ref, other_ref, pair_ref, diag_ref):
 
         @pl.when(meta[1] == 1)
         def _():
@@ -328,58 +315,37 @@
             o_ref[:, lanes] = outer[...]
 
 
-def last_window(meta, here, other, pair):
+def last_window(meta, here, other, pair, diag):
     vm = pl.BlockSpec(memory_space=pltpu.VMEM)
     return pl.pallas_call(
         newest,
         out_shape=pltpu.VMEM((SEQ_ROWS, 2 * HD), jnp.bfloat16),
-        in_specs=[pl.BlockSpec(memory_space=pltpu.SMEM), vm, vm, vm],
+        in_specs=[pl.BlockSpec(memory_space=pltpu.SMEM), vm, vm, vm, vm],
         out_specs=vm,
         name="newest",
         compiler_params=pltpu.CompilerParams(vmem_limit_bytes=SMALL),
-    )(in_smem(meta), *(in_vmem(x) for x in (here, other, pair)))
-
-
-def choose(spots, held_ref, o_ref):
+    )(in_smem(meta), *(in_vmem(x) for x in (here, other, pair, diag)))
+
+
+def choose(verts, held_ref, o_ref):
     for pair in range(2):
         for c in range(CORES):
             for j in range(MINE):
-                at = (pair * CORES + c) * MINE + j
-                mine = jnp.where(spots[PAIR_SLOTS + at] == 1, 1.0, 0.0).astype(jnp.bfloat16)
-                o_ref[at] = held_ref[spots[at]] * mine
-
-
-def chosen_chunks(spots, held):
+                x = held_ref[verts[(pair * CORES + c) * MINE + j]]
+                for part in range(8):
+                    o_ref[(part * CORES + c) * 2 + pair, j] = x
+
+
+def chosen_chunks(verts, held):
     vm = pl.BlockSpec(memory_space=pltpu.VMEM)
     return pl.pallas_call(
         choose,
-        out_shape=pltpu.VMEM((PAIR_SLOTS, CH, HD), jnp.bfloat16),
+        out_shape=pltpu.VMEM((8 * CORES * 2, MINE, CH, HD), jnp.bfloat16),
         in_specs=[pl.BlockSpec(memory_space=pltpu.SMEM), vm],
         out_specs=vm,
         name="choose",
         compiler_params=pltpu.CompilerParams(vmem_limit_bytes=SMALL),
-    )(in_smem(spots), in_vmem(held))
-
-
-def add_up(x_ref, one_ref, two_ref, o_ref):
-    for pair in range(2):
-        for c in range(CORES):
-            slots = slice((pair * CORES + c) * MINE, (pair * CORES + c + 1) * MINE)
-            total = x_ref[slots] + one_ref[slots] + two_ref[slots]
-            for part in range(8):
-                o_ref[(part * CORES + c) * 2 + pair] = total
-
-
-def copies_of_sum(x, one, two):
-    vm = pl.BlockSpec(memory_space=pltpu.VMEM)
-    return pl.pallas_call(
-        add_up,
-        out_shape=pltpu.VMEM((8 * CORES * 2, MINE, CH, HD), jnp.bfloat16),
-        in_specs=[vm, vm, vm],
-        out_specs=vm,
-        name="add_up",
-        compiler_params=pltpu.CompilerParams(vmem_limit_bytes=SMALL),
-    )(in_vmem(x), in_vmem(one), in_vmem(two))
+    )(in_smem(verts), in_vmem(held))
 
 
 def lay_out(q_hbm, k_hbm, v_hbm, o_ref, q_ref, k_ref, v_ref, sems):
@@ -459,7 +425,6 @@
     core = lax.axis_index("c")
     odd = lax.axis_index("yb")
     chip = lax.axis_index(("xl", "za", "zb"))
-    za = lax.axis_index("za")
     pair_heads = 2 * CORES * SLOTS
     verts = lax.dynamic_slice_in_dim(vertical_blocks, group // 2 * pair_heads, pair_heads)
     verts = verts.reshape(-1)
@@ -471,24 +436,19 @@
 
     sent = pack(q_rows, k_rows, v_rows)
     here = lax.all_to_all(sent, HEAD, 0, 0, tiled=True).reshape(SEQ_ROWS, WIDE)
-    held = lax.all_to_all(in_chunks(here), PART, 0, 0, tiled=True)
+    here, verts, meta = lax.optimization_barrier((here, verts, meta))
+    chunks, x_here = in_chunks(here)
+    held = lax.all_to_all(chunks, SEQ, 0, 0, tiled=True)
 
     other = lax.ppermute(here, "c", [(0, 1), (1, 0)])
-    windows = both_windows(here, other)
-    pair = lax.ppermute(windows, "yb", [(0, 1), (1, 0)])
-    last = last_window(meta, here, other, pair)
+    pair = lax.ppermute(x_here, "yb", [(0, 1), (1, 0)])
+    diag = lax.ppermute(x_here, ("c", "yb"), [(0, 3), (1, 2), (2, 1), (3, 0)])
+    last = last_window(meta, here, other, pair, diag)
     kv_before = lax.ppermute(last, ("xl", "za", "zb"), [(i, i + 1) for i in range(23)])
 
-    owner = verts // LB
-    z = (owner % 24) // 2
-    spot = ((owner // 24) * 8 + (z % 4) * 2 + owner % 2) * LB + verts % LB
-    spots = jnp.concatenate([spot, (z // 4 == za).astype(jnp.int32)])
-    chosen = chosen_chunks(spots, held.reshape(SUB * LB, CH, HD))
-    one = lax.ppermute(chosen, "za", [(0, 1), (1, 2), (2, 0)])
-    two = lax.ppermute(chosen, "za", [(0, 2), (1, 0), (2, 1)])
-    spread = copies_of_sum(chosen, one, two)
+    spread = chosen_chunks(verts, held.reshape(SUB * PARTS * LB, CH, HD))
     vert = lax.all_to_all(spread, ("xl", "zb", "c", "yb"), 0, 0, tiled=True)
-    acc, top, q_here = near(meta, here, other, pair, kv_before)
+    acc, top, q_here = near(meta, here, other, pair, diag, kv_before)
     out = far(meta, q_here, acc, top, vert.reshape(SUB, 2, MINE, CH, HD))
     back = lax.all_to_all(
         out.reshape(CORES * GROUPS, ROWS, SLOTS * HD), SPLIT, 0, 0, tiled=True

time: 151 us -> 149 us (0.987)
  blocking collectives: 26.7 us -> 63.7 us
  waiting for transfers between devices: 63 us -> 40.6 us
  starting transfers between devices: 43.4 us -> 28 us
    all_to_all x0 -> x1, blocking collectives: none -> 36.8 us  [per_device(): held = lax.all_to_all(chunks, SEQ, 0, 0, tiled=True)]
    ppermute x3 -> x2, waiting for transfers between devices: 20.8 us -> 8.03 us  [the longest x1 5.67 us: per_device(): pair = lax.ppermute(x_here, 'yb', [(0, 1), (1, 0)])]
    ppermute x3 -> x2, starting transfers between devices: 16.2 us -> 5.56 us  [the longest x1 3.09 us: per_device(): diag = lax.ppermute(x_here, ('c', 'yb'), [(0, 3), (1, 2), (2, 1), (3, 0)])]
    all_to_all x1 -> x0, starting transfers between devices: 8.74 us -> none  [per_device(): held = lax.all_to_all(in_chunks(here), PART, 0, 0, tiled=True)]
    all_to_all x1 -> x0, waiting for transfers between devices: 6.93 us -> none  [per_device(): held = lax.all_to_all(in_chunks(here), PART, 0, 0, tiled=True)]
    all_to_all x1, starting transfers between devices: 4.6 us -> 7.71 us  [per_device(): vert = lax.all_to_all(spread, ('xl', 'zb', 'c', 'yb'), 0, 0, tiled=True)]
    ppermute x1, waiting for transfers between devices: 2.18 us -> 0.01 us  [per_device(): other = lax.ppermute(here, 'c', [(0, 1), (1, 0)])]
  transfers between devices with their start and end apart: 8 -> 6, of which waited for: 7 -> 4; matrix products, arithmetic and copies ran while one was open for 1% -> 1% of each run, Pallas kernels for 3% -> 3%
where the time goes in v7:
time: 149 us
  blocking collectives  63.7 us (43%)
  waiting for transfers between devices  40.6 us (27%)
  starting transfers between devices  28 us (19%)
  Pallas kernels  15.5 us (10%)
    all_to_all x1, blocking collectives, per_device(): held = lax.all_to_all(chunks, SEQ, 0, 0, tiled=True)  36.8 us
    all_to_all x1, blocking collectives, per_device(): lax.all_to_all(out.reshape(CORES * GROUPS, ROWS, SLOTS * HD), SPLIT, 0, 0...  26.9 us
    all_to_all x1, waiting for transfers between devices, per_device(): here = lax.all_to_all(sent, HEAD, 0, 0, tiled=True).reshape(SEQ_ROWS, WIDE)  22.1 us
    ppermute x1, waiting for transfers between devices, per_device(): lax.ppermute(last, ('xl', 'za', 'zb'), [(i, i + 1) for i in range(23)])  10.4 us
    all_to_all x1, starting transfers between devices, per_device(): here = lax.all_to_all(sent, HEAD, 0, 0, tiled=True).reshape(SEQ_ROWS, WIDE)  9.14 us
    all_to_all x1, starting transfers between devices, per_device(): vert = lax.all_to_all(spread, ('xl', 'zb', 'c', 'yb'), 0, 0, tiled=True)  7.71 us
    ppermute x1, waiting for transfers between devices, per_device(): pair = lax.ppermute(x_here, 'yb', [(0, 1), (1, 0)])  5.67 us
    pallas_call x1, Pallas kernels, far(): pl.pallas_call(far_part, out_shape=pltpu.VMEM((TOKENS, SLOTS * HD), jnp.b...  4.66 us
  transfers between devices with their start and end apart: 6, of which 4 were waited for; matrix products, arithmetic and copies ran while one was open for 1% of the time, Pallas kernels for 3%

profile of v7, /device:TPU:10, one launch (start us, length us, event | category | flops | bytes accessed | tf_op | source)
XLA Modules:
  0.0 148.7 jit_solution(8280615499897565858)
XLA Ops:
  0.0 2.2 %lay_out.1 = bf16[16,40,640]{2,1,0:T(8,128)(2,1)} custom-call(bf16[40,8192]{1,0:T(8,128)(2,1)} %q_hbm.1, bf16[40,1024]{1,0:T(8,128)(2,1)} %k_hbm.1, bf16[40,1024]{1,0:T(8,128)(2,1)} %v_hbm.1), custom_call_target="tpu_custom_call" | custom-call | tf_op jit(solution)/shard_map/lay_out/pallas_call | solution.py:376
  2.2 9.1 %all-to-all-start = ((bf16[16,40,640]{2,1,0:T(8,128)(2,1)}), bf16[16,40,640]{2,1,0:T(8,128)(2,1)S(1)}, u32[]{:S(2)}, u32[]{:S(2)}) async-start(bf16[16,40,640]{2,1,0:T(8,128)(2,1)} %lay_out.1), calls=%async_computation | async-start | bytes 1638400 | tf_op jit(solution)/shard_map/all_to_all | solution.py:438
  11.4 0.1 constant_dynamic-slice_fusion.2
  11.5 0.1 copy.10
  11.5 0.1 reshape.22.verts
  11.6 0.1 constant_dynamic-slice_fusion.1
  11.7 0.1 copy.11
  11.8 0.1 reshape.23
  11.9 0.1 constant_dynamic-slice_fusion
  11.9 0.1 copy.12
  12.0 0.1 reshape.24
  12.1 0.1 concatenate.3.meta
  12.2 22.1 %all-to-all-done = bf16[16,40,640]{2,1,0:T(8,128)(2,1)S(1)} async-done(((bf16[16,40,640]{2,1,0:T(8,128)(2,1)}), bf16[16,40,640]{2,1,0:T(8,128)(2,1)S(1)}, u32[]{:S(2)}, u32[]{:S(2)}) %all-to-all-start) | async-done | bytes 819232 | tf_op jit(solution)/shard_map/all_to_all | solution.py:438
  34.3 0.1 cut.1
  34.4 36.8 %all_to_all.20 = bf16[48,5,8,128]{3,2,1,0:T(8,128)(2,1)S(1)} all-to-all(bf16[48,5,8,128]{3,2,1,0:T(8,128)(2,1)S(1)} %get-tuple-element.20), channel_id=1, replica_groups=mesh['xl'=2,'za'=3,'zb'=4,'c'=2,'xh'=2,'ya'=4,'yb'=2] {'xl','za','zb','c'}, dimensions={0} | all-to-all | bytes 983040 | tf_op jit(solution)/shard_map/all_to_all | solution.py:441
  71.2 1.4 choose.1
  72.6 7.7 %all-to-all-start.2 = ((bf16[32,8,8,128]{3,2,1,0:T(8,128)(2,1)}), bf16[32,8,8,128]{3,2,1,0:T(8,128)(2,1)S(1)}, u32[]{:S(2)}, u32[]{:S(2)}) async-start(bf16[32,8,8,128]{3,2,1,0:T(8,128)(2,1)} %choose.1), calls=%async_computation.2 | async-start | bytes 1048576 | tf_op jit(solution)/shard_map/all_to_all | solution.py:450
  80.3 2.0 %collective-permute-start = (bf16[640,640]{1,0:T(8,128)(2,1)S(1)}, bf16[640,640]{1,0:T(8,128)(2,1)S(1)}, u32[]{:S(2)}, u32[]{:S(2)}) collective-permute-start(bf16[640,640]{1,0:T(8,128)(2,1)S(1)} %bitcast.8), channel_id=1, source_target_pairs={{0,16},{16,0},{1,17},{17,1},{2,18},{18,2},{3,19},{19,3},{4,20},{20... | collective-permute-start | bytes 2457608 | tf_op jit(solution)/shard_map/ppermute | solution.py:443
  82.3 2.5 %collective-permute-start.1 = (bf16[640,128]{1,0:T(8,128)(2,1)S(1)}, bf16[640,128]{1,0:T(8,128)(2,1)S(1)}, u32[]{:S(2)}, u32[]{:S(2)}) collective-permute-start(bf16[640,128]{1,0:T(8,128)(2,1)S(1)} %get-tuple-element.15), channel_id=1, source_target_pairs={{0,1},{1,0},{2,3},{3,2},{4,5},{5,4},{6,7},{7,6},{8,9},{9,8},{10,11... | collective-permute-start | bytes 491528 | tf_op jit(solution)/shard_map/ppermute | solution.py:444
  84.8 3.1 %collective-permute-start.2 = (bf16[640,128]{1,0:T(8,128)(2,1)S(1)}, bf16[640,128]{1,0:T(8,128)(2,1)S(1)}, u32[]{:S(2)}, u32[]{:S(2)}) collective-permute-start(bf16[640,128]{1,0:T(8,128)(2,1)S(1)} %get-tuple-element.15), channel_id=1, source_target_pairs={{0,17},{1,16},{16,1},{17,0},{2,19},{3,18},{18,3},{19,2},{4,21},{5,... | collective-permute-start | bytes 491528 | tf_op jit(solution)/shard_map/ppermute | solution.py:445
  87.9 5.7 %collective-permute-done.1.pair_ref = bf16[640,128]{1,0:T(8,128)(2,1)S(1)} collective-permute-done((bf16[640,128]{1,0:T(8,128)(2,1)S(1)}, bf16[640,128]{1,0:T(8,128)(2,1)S(1)}, u32[]{:S(2)}, u32[]{:S(2)}) %collective-permute-start.1) | collective-permute-done | bytes 163872 | tf_op jit(solution)/shard_map/ppermute | solution.py:444
  93.6 2.4 %collective-permute-done.2.diag_ref = bf16[640,128]{1,0:T(8,128)(2,1)S(1)} collective-permute-done((bf16[640,128]{1,0:T(8,128)(2,1)S(1)}, bf16[640,128]{1,0:T(8,128)(2,1)S(1)}, u32[]{:S(2)}, u32[]{:S(2)}) %collective-permute-start.2) | collective-permute-done | bytes 163872 | tf_op jit(solution)/shard_map/ppermute | solution.py:445
  95.9 0.0 collective-permute-done.other_ref
  95.9 0.6 newest.1
  96.6 3.6 %collective-permute-start.3 = (bf16[640,256]{1,0:T(8,128)(2,1)S(1)}, bf16[640,256]{1,0:T(8,128)(2,1)S(1)}, u32[]{:S(2)}, u32[]{:S(2)}) collective-permute-start(bf16[640,256]{1,0:T(8,128)(2,1)S(1)} %newest.1), channel_id=1, source_target_pairs={{0,32},{32,64},{64,96},{96,128},{128,160},{160,192},{192,224},{224... | collective-permute-start | bytes 983048 | tf_op jit(solution)/shard_map/ppermute | solution.py:447
  100.2 10.4 %collective-permute-done.3.prev_ref = bf16[640,256]{1,0:T(8,128)(2,1)S(1)} collective-permute-done((bf16[640,256]{1,0:T(8,128)(2,1)S(1)}, bf16[640,256]{1,0:T(8,128)(2,1)S(1)}, u32[]{:S(2)}, u32[]{:S(2)}) %collective-permute-start.3) | collective-permute-done | bytes 327712 | tf_op jit(solution)/shard_map/ppermute | solution.py:447
  110.6 4.5 %near.1 = (f32[1280,512]{1,0:T(8,128)}, f32[1280,256]{1,0:T(8,128)}, bf16[1280,256]{1,0:T(8,128)(2,1)}) custom-call(s32[17]{0:T(128)S(1)} %concatenate.3.meta, bf16[640,640]{1,0:T(8,128)(2,1)S(1)} %bitcast.10, bf16[640,640]{1,0:T(8,128)(2,1)S(1)} %collective-permute-done.other_ref, bf16[640,128]{1,0:T(8,128)(2,1)S(1)} %collective-permute-done.1.pair_ref, ...), custom_call_target="tpu_custom_call" | custom-call | tf_op jit(solution)/shard_map/near/pallas_call | solution.py:151
  115.1 0.0 all-to-all-done.2
  115.1 0.0 copy-start.1
  115.1 4.7 %far.1 = bf16[1280,256]{1,0:T(8,128)(2,1)S(1)} custom-call(s32[17]{0:T(128)S(1)} %concatenate.3.meta, bf16[1280,256]{1,0:T(8,128)(2,1)} %get-tuple-element.16.q_hbm, f32[1280,512]{1,0:T(8,128)} %get-tuple-element.17.acc_hbm, f32[1280,256]{1,0:T(8,128)} %get-tuple-element.18.top_hbm, bf16[16,2,8,8,128]{4,3,2,1,0:T(8,128)(2,1)S(1)} %bitcast.12), custom_call_target="tpu_custom_call" | custom-call | tf_op jit(solution)/shard_map/far/pallas_call | solution.py:263
  119.8 26.9 %all_to_all.21.x_ref = bf16[32,40,256]{2,1,0:T(8,128)(2,1)S(1)} all-to-all(bf16[32,40,256]{2,1,0:T(8,128)(2,1)S(1)} %bitcast.11), channel_id=1, replica_groups=mesh['xl'=2,'za'=3,'zb'=4,'c'=2,'xh'=2,'ya'=4,'yb'=2] {'c','xh','ya','yb'}, dimensions={0} | all-to-all | bytes 1310720 | tf_op jit(solution)/shard_map/all_to_all | solution.py:453
  146.7 2.0 %to_slots.1 = bf16[40,8192]{1,0:T(8,128)(2,1)} custom-call(s32[64]{0:T(128)S(1)} %copy-done.1, bf16[32,40,256]{2,1,0:T(8,128)(2,1)S(1)} %all_to_all.21.x_ref), custom_call_target="tpu_custom_call" | custom-call | tf_op jit(solution)/shard_map/to_slots/pallas_call | solution.py:409
  (5 shorter events, 0.0 us)
Async XLA Ops:
  0.0 11.4 %copy-start = (s32[64,4]{0,1:T(4,128)S(1)}, s32[64,4]{0,1:T(4,128)}, u32[]{:S(2)}) copy-start(s32[64,4]{0,1:T(4,128)} %param.10) | copy-start | bytes 3076
  0.0 11.9 %copy-start.2 = (s32[64,3]{0,1:T(4,128)S(1)}, s32[64,3]{0,1:T(4,128)}, u32[]{:S(2)}) copy-start(s32[64,3]{0,1:T(4,128)} %param.11) | copy-start | bytes 2308
  2.2 32.1 %all-to-all-start = ((bf16[16,40,640]{2,1,0:T(8,128)(2,1)}), bf16[16,40,640]{2,1,0:T(8,128)(2,1)S(1)}, u32[]{:S(2)}, u32[]{:S(2)}) async-start(bf16[16,40,640]{2,1,0:T(8,128)(2,1)} %lay_out.1), calls=%async_computation | async-start | bytes 1638400 | tf_op jit(solution)/shard_map/all_to_all | solution.py:438
  72.6 42.5 %all-to-all-start.2 = ((bf16[32,8,8,128]{3,2,1,0:T(8,128)(2,1)}), bf16[32,8,8,128]{3,2,1,0:T(8,128)(2,1)S(1)}, u32[]{:S(2)}, u32[]{:S(2)}) async-start(bf16[32,8,8,128]{3,2,1,0:T(8,128)(2,1)} %choose.1), calls=%async_computation.2 | async-start | bytes 1048576 | tf_op jit(solution)/shard_map/all_to_all | solution.py:450
  80.3 15.6 %collective-permute-start = (bf16[640,640]{1,0:T(8,128)(2,1)S(1)}, bf16[640,640]{1,0:T(8,128)(2,1)S(1)}, u32[]{:S(2)}, u32[]{:S(2)}) collective-permute-start(bf16[640,640]{1,0:T(8,128)(2,1)S(1)} %bitcast.8), channel_id=1, source_target_pairs={{0,16},{16,0},{1,17},{17,1},{2,18},{18,2},{3,19},{19,3},{4,20},{20... | collective-permute-start | bytes 2457608 | tf_op jit(solution)/shard_map/ppermute | solution.py:443
  82.3 11.2 %collective-permute-start.1 = (bf16[640,128]{1,0:T(8,128)(2,1)S(1)}, bf16[640,128]{1,0:T(8,128)(2,1)S(1)}, u32[]{:S(2)}, u32[]{:S(2)}) collective-permute-start(bf16[640,128]{1,0:T(8,128)(2,1)S(1)} %get-tuple-element.15), channel_id=1, source_target_pairs={{0,1},{1,0},{2,3},{3,2},{4,5},{5,4},{6,7},{7,6},{8,9},{9,8},{10,11... | collective-permute-start | bytes 491528 | tf_op jit(solution)/shard_map/ppermute | solution.py:444
  84.8 11.1 %collective-permute-start.2 = (bf16[640,128]{1,0:T(8,128)(2,1)S(1)}, bf16[640,128]{1,0:T(8,128)(2,1)S(1)}, u32[]{:S(2)}, u32[]{:S(2)}) collective-permute-start(bf16[640,128]{1,0:T(8,128)(2,1)S(1)} %get-tuple-element.15), channel_id=1, source_target_pairs={{0,17},{1,16},{16,1},{17,0},{2,19},{3,18},{18,3},{19,2},{4,21},{5,... | collective-permute-start | bytes 491528 | tf_op jit(solution)/shard_map/ppermute | solution.py:445
  96.6 14.0 %collective-permute-start.3 = (bf16[640,256]{1,0:T(8,128)(2,1)S(1)}, bf16[640,256]{1,0:T(8,128)(2,1)S(1)}, u32[]{:S(2)}, u32[]{:S(2)}) collective-permute-start(bf16[640,256]{1,0:T(8,128)(2,1)S(1)} %newest.1), channel_id=1, source_target_pairs={{0,32},{32,64},{64,96},{96,128},{128,160},{160,192},{192,224},{224... | collective-permute-start | bytes 983048 | tf_op jit(solution)/shard_map/ppermute | solution.py:447
  115.1 31.6 %copy-start.1 = (s32[64]{0:T(128)S(1)}, s32[64]{0:T(128)}, u32[]{:S(2)}) copy-start(s32[64]{0:T(128)} %assign.1) | copy-start | bytes 772

commit v8 on v7

--- a/solution.py
+++ b/solution.py
@@ -24,6 +24,7 @@
 CHIP_WIDE = CORES * SLOTS * HD
 WIDE = CHIP_WIDE + HD
 MINE = SLOTS * NV
+PAIR_SLOTS = 2 * CORES * MINE
 CH = 8
 PARTS = 3
 SUB = 16
@@ -68,6 +69,7 @@
     pair_ref,
     diag_ref,
     prev_ref,
+    rest_ref,
     acc_hbm,
     top_hbm,
     q_hbm,
@@ -85,7 +87,8 @@
     my_lanes = pl.ds(pl.multiple_of(core * wide, wide), wide)
     mine = pl.multiple_of(core * SEQ_ROWS, SEQ_ROWS)
     theirs = pl.multiple_of((1 - core) * SEQ_ROWS, SEQ_ROWS)
-    win[0:SEQ_ROWS, :] = prev_ref[...]
+    win[0:SEQ_ROWS, pl.ds(pl.multiple_of(core * HD, HD), HD)] = prev_ref[...]
+    win[0:SEQ_ROWS, pl.ds(pl.multiple_of((1 - core) * HD, HD), HD)] = rest_ref[...]
     for lanes, inner, outer in both_kinds(meta, here_ref, other_ref, pair_ref, diag_ref):
         win[pl.ds(SEQ_ROWS + mine, SEQ_ROWS), lanes] = inner[...]
         win[pl.ds(SEQ_ROWS + theirs, SEQ_ROWS), lanes] = outer[...]
@@ -146,7 +149,7 @@
             copy.wait()
 
 
-def near(meta, here, other, pair, diag, prev):
+def near(meta, here, other, pair, diag, prev, rest):
     vm = pl.BlockSpec(memory_space=pltpu.VMEM)
     return pl.pallas_call(
         near_part,
@@ -155,7 +158,7 @@
             pltpu.HBM((TOKENS, SLOTS * HD), jnp.float32),
             pltpu.HBM((TOKENS, SLOTS * HD), jnp.bfloat16),
         ),
-        in_specs=[pl.BlockSpec(memory_space=pltpu.SMEM), vm, vm, vm, vm, vm],
+        in_specs=[pl.BlockSpec(memory_space=pltpu.SMEM), vm, vm, vm, vm, vm, vm],
         out_specs=tuple(pl.BlockSpec(memory_space=pltpu.HBM) for _ in range(3)),
         scratch_shapes=[
             pltpu.VMEM((TOKENS, 2 * SLOTS * HD), jnp.float32),
@@ -168,7 +171,7 @@
         ],
         name="near",
         compiler_params=pltpu.CompilerParams(vmem_limit_bytes=LARGE),
-    )(in_smem(meta), *(in_vmem(x) for x in (here, other, pair, diag, prev)))
+    )(in_smem(meta), *(in_vmem(x) for x in (here, other, pair, diag, prev, rest)))
 
 
 def far_part(
@@ -278,14 +281,25 @@
     )(in_smem(meta), in_hbm(q), in_hbm(acc), in_hbm(top), in_vmem(vert))
 
 
-def cut(here_ref, o_ref, x_ref):
-    x_ref[...] = here_ref[:, CHIP_WIDE:WIDE]
+def cut(here_ref, o_hbm, x_ref, one_ref, sems):
     for j in range(LB):
         x = here_ref[j * BT : (j + 1) * BT, CHIP_WIDE:WIDE].astype(jnp.float32)
         for r in range(SUB):
-            chunk = x[r * CH : (r + 1) * CH].astype(jnp.bfloat16)
-            for part in range(PARTS):
-                o_ref[r // 8 * 8 * PARTS + part * 8 + r % 8, j] = chunk
+            one_ref[r, j] = x[r * CH : (r + 1) * CH].astype(jnp.bfloat16)
+    copies = [
+        pltpu.make_async_copy(
+            one_ref.at[pl.ds(half * 8, 8)],
+            o_hbm.at[pl.ds((half * PARTS + part) * 8, 8)],
+            sems.at[half, part],
+        )
+        for half in range(2)
+        for part in range(PARTS)
+    ]
+    for copy in copies:
+        copy.start()
+    x_ref[...] = here_ref[:, CHIP_WIDE:WIDE]
+    for copy in copies:
+        copy.wait()
 
 
 def in_chunks(here):
@@ -293,33 +307,37 @@
     return pl.pallas_call(
         cut,
         out_shape=(
-            pltpu.VMEM((SUB * PARTS, LB, CH, HD), jnp.bfloat16),
+            pltpu.HBM((SUB * PARTS, LB, CH, HD), jnp.bfloat16),
             pltpu.VMEM((SEQ_ROWS, HD), jnp.bfloat16),
         ),
         in_specs=[vm],
-        out_specs=(vm, vm),
+        out_specs=(pl.BlockSpec(memory_space=pltpu.HBM), vm),
+        scratch_shapes=[
+            pltpu.VMEM((SUB, LB, CH, HD), jnp.bfloat16),
+            pltpu.SemaphoreType.DMA((2, PARTS)),
+        ],
         name="cut",
         compiler_params=pltpu.CompilerParams(vmem_limit_bytes=SMALL),
     )(in_vmem(here))
 
 
 def newest(meta, here_ref, other_ref, pair_ref, diag_ref, o_ref):
-    for lanes, inner, outer in both_kinds(meta, here_ref, other_ref, pair_ref, diag_ref):
-
-        @pl.when(meta[1] == 1)
-        def _():
-            o_ref[:, lanes] = inner[...]
-
-        @pl.when(meta[1] != 1)
-        def _():
-            o_ref[:, lanes] = outer[...]
-
-
-def last_window(meta, here, other, pair, diag):
+    x = slice(CHIP_WIDE, WIDE)
+    core, odd = meta[1], meta[2]
+    sources = ((other_ref.at[:, x], diag_ref), (pair_ref, here_ref.at[:, x]))
+    for c in range(CORES):
+        for parity in range(2):
+
+            @pl.when((core == c) & (odd == parity))
+            def _():
+                o_ref[...] = sources[c][parity][...]
+
+
+def half_window(meta, here, other, pair, diag):
     vm = pl.BlockSpec(memory_space=pltpu.VMEM)
     return pl.pallas_call(
         newest,
-        out_shape=pltpu.VMEM((SEQ_ROWS, 2 * HD), jnp.bfloat16),
+        out_shape=pltpu.VMEM((SEQ_ROWS, HD), jnp.bfloat16),
         in_specs=[pl.BlockSpec(memory_space=pltpu.SMEM), vm, vm, vm, vm],
         out_specs=vm,
         name="newest",
@@ -327,35 +345,46 @@
     )(in_smem(meta), *(in_vmem(x) for x in (here, other, pair, diag)))
 
 
-def choose(verts, held_ref, o_ref):
-    for pair in range(2):
-        for c in range(CORES):
-            for j in range(MINE):
-                x = held_ref[verts[(pair * CORES + c) * MINE + j]]
-                for part in range(8):
-                    o_ref[(part * CORES + c) * 2 + pair, j] = x
+def choose(verts, held_ref, o_hbm, one_ref, sems):
+    for at in range(PAIR_SLOTS):
+        pair, c, j = at // (CORES * MINE), at // MINE % CORES, at % MINE
+        one_ref[c * 2 + pair, j] = held_ref[verts[at]]
+    copies = [
+        pltpu.make_async_copy(one_ref, o_hbm.at[pl.ds(part * 4, 4)], sems.at[part])
+        for part in range(8)
+    ]
+    for copy in copies:
+        copy.start()
+    for copy in copies:
+        copy.wait()
 
 
 def chosen_chunks(verts, held):
-    vm = pl.BlockSpec(memory_space=pltpu.VMEM)
     return pl.pallas_call(
         choose,
-        out_shape=pltpu.VMEM((8 * CORES * 2, MINE, CH, HD), jnp.bfloat16),
-        in_specs=[pl.BlockSpec(memory_space=pltpu.SMEM), vm],
-        out_specs=vm,
+        out_shape=pltpu.HBM((8 * CORES * 2, MINE, CH, HD), jnp.bfloat16),
+        in_specs=[
+            pl.BlockSpec(memory_space=pltpu.SMEM),
+            pl.BlockSpec(memory_space=pltpu.VMEM),
+        ],
+        out_specs=pl.BlockSpec(memory_space=pltpu.HBM),
+        scratch_shapes=[
+            pltpu.VMEM((CORES * 2, MINE, CH, HD), jnp.bfloat16),
+            pltpu.SemaphoreType.DMA((8,)),
+        ],
         name="choose",
         compiler_params=pltpu.CompilerParams(vmem_limit_bytes=SMALL),
     )(in_smem(verts), in_vmem(held))
 
 
-def lay_out(q_hbm, k_hbm, v_hbm, o_ref, q_ref, k_ref, v_ref, sems):
+def lay_out(q_hbm, k_hbm, v_hbm, o_hbm, q_ref, k_ref, v_ref, sent, sems):
     step = 8
+    spans = [pl.ds(row, step) for row in range(0, ROWS, step)]
     copies = [
         pltpu.make_async_copy(k_hbm, k_ref, sems.at[0]),
         pltpu.make_async_copy(v_hbm, v_ref, sems.at[1]),
     ]
-    for n, row in enumerate(range(0, ROWS, step)):
-        rows = pl.ds(row, step)
+    for n, rows in enumerate(spans):
         copies.append(pltpu.make_async_copy(q_hbm.at[rows], q_ref.at[rows], sems.at[2 + n]))
     for copy in copies:
         copy.start()
@@ -363,26 +392,34 @@
     copies[1].wait()
     for g in range(GROUPS):
         m = g // 2 * HD
-        o_ref[g, :, CHIP_WIDE:WIDE] = (v_ref if g % 2 else k_ref)[:, m : m + HD]
-    for n, row in enumerate(range(0, ROWS, step)):
+        sent[g, :, CHIP_WIDE:WIDE] = (v_ref if g % 2 else k_ref)[:, m : m + HD]
+    out = []
+    for n, rows in enumerate(spans):
         copies[2 + n].wait()
         for g in range(GROUPS):
-            o_ref[g, row : row + step, 0:CHIP_WIDE] = q_ref[
-                row : row + step, g * CHIP_WIDE : (g + 1) * CHIP_WIDE
-            ]
+            sent[g, rows, 0:CHIP_WIDE] = q_ref[rows, g * CHIP_WIDE : (g + 1) * CHIP_WIDE]
+        out.append(
+            pltpu.make_async_copy(
+                sent.at[:, rows, :], o_hbm.at[:, rows, :], sems.at[2 + len(spans) + n]
+            )
+        )
+        out[-1].start()
+    for copy in out:
+        copy.wait()
 
 
 def pack(q, k, v):
     return pl.pallas_call(
         lay_out,
-        out_shape=pltpu.VMEM((GROUPS, ROWS, WIDE), jnp.bfloat16),
+        out_shape=pltpu.HBM((GROUPS, ROWS, WIDE), jnp.bfloat16),
         in_specs=[pl.BlockSpec(memory_space=pltpu.HBM)] * 3,
-        out_specs=pl.BlockSpec(memory_space=pltpu.VMEM),
+        out_specs=pl.BlockSpec(memory_space=pltpu.HBM),
         scratch_shapes=[
             pltpu.VMEM((ROWS, QUERY_HEADS * HD), jnp.bfloat16),
             pltpu.VMEM((ROWS, KEY_VALUE_HEADS * HD), jnp.bfloat16),
             pltpu.VMEM((ROWS, KEY_VALUE_HEADS * HD), jnp.bfloat16),
-            pltpu.SemaphoreType.DMA((2 + ROWS // 8,)),
+            pltpu.VMEM((GROUPS, ROWS, WIDE), jnp.bfloat16),
+            pltpu.SemaphoreType.DMA((2 + 2 * (ROWS // 8),)),
         ],
         name="lay_out",
         compiler_params=pltpu.CompilerParams(vmem_limit_bytes=SMALL),
@@ -443,12 +480,13 @@
     other = lax.ppermute(here, "c", [(0, 1), (1, 0)])
     pair = lax.ppermute(x_here, "yb", [(0, 1), (1, 0)])
     diag = lax.ppermute(x_here, ("c", "yb"), [(0, 3), (1, 2), (2, 1), (3, 0)])
-    last = last_window(meta, here, other, pair, diag)
-    kv_before = lax.ppermute(last, ("xl", "za", "zb"), [(i, i + 1) for i in range(23)])
+    last = half_window(meta, here, other, pair, diag)
+    prev = lax.ppermute(last, ("xl", "za", "zb"), [(i, i + 1) for i in range(23)])
+    rest = lax.ppermute(prev, "c", [(0, 1), (1, 0)])
 
     spread = chosen_chunks(verts, held.reshape(SUB * PARTS * LB, CH, HD))
     vert = lax.all_to_all(spread, ("xl", "zb", "c", "yb"), 0, 0, tiled=True)
-    acc, top, q_here = near(meta, here, other, pair, diag, kv_before)
+    acc, top, q_here = near(meta, here, other, pair, diag, prev, rest)
     out = far(meta, q_here, acc, top, vert.reshape(SUB, 2, MINE, CH, HD))
     back = lax.all_to_all(
         out.reshape(CORES * GROUPS, ROWS, SLOTS * HD), SPLIT, 0, 0, tiled=True

time: 149 us -> 150 us (level)
  waiting for transfers between devices: 40.6 us -> 38.5 us
  starting transfers between devices: 28 us -> 29.9 us
    ppermute x1, waiting for transfers between devices: 10.4 us -> 6.92 us  [per_device(): lax.ppermute(last, ('xl', 'za', 'zb'), [(i, i + 1) for i in range(23)])]
    ppermute x0 -> x1, starting transfers between devices: none -> 1.91 us  [per_device(): rest = lax.ppermute(prev, 'c', [(0, 1), (1, 0)])]
  transfers between devices with their start and end apart: 6 -> 7, of which waited for: 4 -> 5; matrix products, arithmetic and copies ran while one was open for 1% -> 1% of each run, Pallas kernels for 3% -> 3%
where the time goes in v8:
time: 150 us
  blocking collectives  63.9 us (43%)
  waiting for transfers between devices  38.5 us (26%)
  starting transfers between devices  29.9 us (20%)
  Pallas kernels  16.4 us (11%)
    all_to_all x1, blocking collectives, per_device(): held = lax.all_to_all(chunks, SEQ, 0, 0, tiled=True)  37 us
    all_to_all x1, blocking collectives, per_device(): lax.all_to_all(out.reshape(CORES * GROUPS, ROWS, SLOTS * HD), SPLIT, 0, 0...  26.9 us
    all_to_all x1, waiting for transfers between devices, per_device(): here = lax.all_to_all(sent, HEAD, 0, 0, tiled=True).reshape(SEQ_ROWS, WIDE)  22.1 us
    all_to_all x1, starting transfers between devices, per_device(): here = lax.all_to_all(sent, HEAD, 0, 0, tiled=True).reshape(SEQ_ROWS, WIDE)  9.14 us
    all_to_all x1, starting transfers between devices, per_device(): vert = lax.all_to_all(spread, ('xl', 'zb', 'c', 'yb'), 0, 0, tiled=True)  7.73 us
    ppermute x1, waiting for transfers between devices, per_device(): lax.ppermute(last, ('xl', 'za', 'zb'), [(i, i + 1) for i in range(23)])  6.92 us
    ppermute x1, waiting for transfers between devices, per_device(): pair = lax.ppermute(x_here, 'yb', [(0, 1), (1, 0)])  5.67 us
    pallas_call x1, Pallas kernels, far(): pl.pallas_call(far_part, out_shape=pltpu.VMEM((TOKENS, SLOTS * HD), jnp.b...  4.85 us
  transfers between devices with their start and end apart: 7, of which 5 were waited for; matrix products, arithmetic and copies ran while one was open for 1% of the time, Pallas kernels for 3%

profile of v8, /device:TPU:10, one launch (start us, length us, event | category | flops | bytes accessed | tf_op | source)
XLA Modules:
  0.0 149.7 jit_solution(3931059647927969175)
XLA Ops:
  0.0 2.1 %lay_out.1 = bf16[16,40,640]{2,1,0:T(8,128)(2,1)} custom-call(bf16[40,8192]{1,0:T(8,128)(2,1)} %q_hbm.1, bf16[40,1024]{1,0:T(8,128)(2,1)} %k_hbm.1, bf16[40,1024]{1,0:T(8,128)(2,1)} %v_hbm.1), custom_call_target="tpu_custom_call" | custom-call | tf_op jit(solution)/shard_map/lay_out/pallas_call | solution.py:412
  2.1 9.1 %all-to-all-start = ((bf16[16,40,640]{2,1,0:T(8,128)(2,1)}), bf16[16,40,640]{2,1,0:T(8,128)(2,1)S(1)}, u32[]{:S(2)}, u32[]{:S(2)}) async-start(bf16[16,40,640]{2,1,0:T(8,128)(2,1)} %lay_out.1), calls=%async_computation | async-start | bytes 1638400 | tf_op jit(solution)/shard_map/all_to_all | solution.py:475
  11.2 0.1 constant_dynamic-slice_fusion.2
  11.3 0.1 copy.10
  11.4 0.1 reshape.22.verts
  11.5 0.1 constant_dynamic-slice_fusion.1
  11.5 0.1 copy.11
  11.6 0.1 reshape.23
  11.7 0.1 constant_dynamic-slice_fusion
  11.8 0.1 copy.12
  11.9 0.1 reshape.24
  12.0 0.1 concatenate.3.meta
  12.1 22.1 %all-to-all-done = bf16[16,40,640]{2,1,0:T(8,128)(2,1)S(1)} async-done(((bf16[16,40,640]{2,1,0:T(8,128)(2,1)}), bf16[16,40,640]{2,1,0:T(8,128)(2,1)S(1)}, u32[]{:S(2)}, u32[]{:S(2)}) %all-to-all-start) | async-done | bytes 819232 | tf_op jit(solution)/shard_map/all_to_all | solution.py:475
  34.2 0.9 cut.1
  35.1 37.0 %all_to_all.20 = bf16[48,5,8,128]{3,2,1,0:T(8,128)(2,1)S(1)} all-to-all(bf16[48,5,8,128]{3,2,1,0:T(8,128)(2,1)} %get-tuple-element.20), channel_id=1, replica_groups=mesh['xl'=2,'za'=3,'zb'=4,'c'=2,'xh'=2,'ya'=4,'yb'=2] {'xl','za','zb','c'}, dimensions={0} | all-to-all | bytes 983040 | tf_op jit(solution)/shard_map/all_to_all | solution.py:478
  72.0 1.4 choose.1
  73.5 7.7 %all-to-all-start.2 = ((bf16[32,8,8,128]{3,2,1,0:T(8,128)(2,1)}), bf16[32,8,8,128]{3,2,1,0:T(8,128)(2,1)S(1)}, u32[]{:S(2)}, u32[]{:S(2)}) async-start(bf16[32,8,8,128]{3,2,1,0:T(8,128)(2,1)} %choose.1), calls=%async_computation.2 | async-start | bytes 1048576 | tf_op jit(solution)/shard_map/all_to_all | solution.py:488
  81.2 2.0 %collective-permute-start = (bf16[640,640]{1,0:T(8,128)(2,1)S(1)}, bf16[640,640]{1,0:T(8,128)(2,1)S(1)}, u32[]{:S(2)}, u32[]{:S(2)}) collective-permute-start(bf16[640,640]{1,0:T(8,128)(2,1)S(1)} %bitcast.8), channel_id=1, source_target_pairs={{0,16},{16,0},{1,17},{17,1},{2,18},{18,2},{3,19},{19,3},{4,20},{20... | collective-permute-start | bytes 2457608 | tf_op jit(solution)/shard_map/ppermute | solution.py:480
  83.2 2.5 %collective-permute-start.1 = (bf16[640,128]{1,0:T(8,128)(2,1)S(1)}, bf16[640,128]{1,0:T(8,128)(2,1)S(1)}, u32[]{:S(2)}, u32[]{:S(2)}) collective-permute-start(bf16[640,128]{1,0:T(8,128)(2,1)S(1)} %get-tuple-element.15), channel_id=1, source_target_pairs={{0,1},{1,0},{2,3},{3,2},{4,5},{5,4},{6,7},{7,6},{8,9},{9,8},{10,11... | collective-permute-start | bytes 491528 | tf_op jit(solution)/shard_map/ppermute | solution.py:481
  85.7 3.1 %collective-permute-start.2 = (bf16[640,128]{1,0:T(8,128)(2,1)S(1)}, bf16[640,128]{1,0:T(8,128)(2,1)S(1)}, u32[]{:S(2)}, u32[]{:S(2)}) collective-permute-start(bf16[640,128]{1,0:T(8,128)(2,1)S(1)} %get-tuple-element.15), channel_id=1, source_target_pairs={{0,17},{1,16},{16,1},{17,0},{2,19},{3,18},{18,3},{19,2},{4,21},{5,... | collective-permute-start | bytes 491528 | tf_op jit(solution)/shard_map/ppermute | solution.py:482
  88.8 5.7 %collective-permute-done.1.pair_ref = bf16[640,128]{1,0:T(8,128)(2,1)S(1)} collective-permute-done((bf16[640,128]{1,0:T(8,128)(2,1)S(1)}, bf16[640,128]{1,0:T(8,128)(2,1)S(1)}, u32[]{:S(2)}, u32[]{:S(2)}) %collective-permute-start.1) | collective-permute-done | bytes 163872 | tf_op jit(solution)/shard_map/ppermute | solution.py:481
  94.5 2.4 %collective-permute-done.2.diag_ref = bf16[640,128]{1,0:T(8,128)(2,1)S(1)} collective-permute-done((bf16[640,128]{1,0:T(8,128)(2,1)S(1)}, bf16[640,128]{1,0:T(8,128)(2,1)S(1)}, u32[]{:S(2)}, u32[]{:S(2)}) %collective-permute-start.2) | collective-permute-done | bytes 163872 | tf_op jit(solution)/shard_map/ppermute | solution.py:482
  96.8 0.6 newest.1
  97.4 3.6 %collective-permute-start.3 = (bf16[640,128]{1,0:T(8,128)(2,1)S(1)}, bf16[640,128]{1,0:T(8,128)(2,1)S(1)}, u32[]{:S(2)}, u32[]{:S(2)}) collective-permute-start(bf16[640,128]{1,0:T(8,128)(2,1)S(1)} %newest.1), channel_id=1, source_target_pairs={{0,32},{32,64},{64,96},{96,128},{128,160},{160,192},{192,224},{224... | collective-permute-start | bytes 491528 | tf_op jit(solution)/shard_map/ppermute | solution.py:484
  101.0 6.9 %collective-permute-done.3.prev_ref = bf16[640,128]{1,0:T(8,128)(2,1)S(1)} collective-permute-done((bf16[640,128]{1,0:T(8,128)(2,1)S(1)}, bf16[640,128]{1,0:T(8,128)(2,1)S(1)}, u32[]{:S(2)}, u32[]{:S(2)}) %collective-permute-start.3) | collective-permute-done | bytes 163872 | tf_op jit(solution)/shard_map/ppermute | solution.py:484
  107.9 1.9 %collective-permute-start.4 = (bf16[640,128]{1,0:T(8,128)(2,1)S(1)}, bf16[640,128]{1,0:T(8,128)(2,1)S(1)}, u32[]{:S(2)}, u32[]{:S(2)}) collective-permute-start(bf16[640,128]{1,0:T(8,128)(2,1)S(1)} %collective-permute-done.3.prev_ref), channel_id=1, source_target_pairs={{0,16},{16,0},{1,17},{17,1},{2,18},{18,2},{3,19},{19,3},{4,20},{20... | collective-permute-start | bytes 491528 | tf_op jit(solution)/shard_map/ppermute | solution.py:485
  109.9 1.4 collective-permute-done.4.rest_ref
  111.2 4.6 %near.1 = (f32[1280,512]{1,0:T(8,128)}, f32[1280,256]{1,0:T(8,128)}, bf16[1280,256]{1,0:T(8,128)(2,1)}) custom-call(s32[17]{0:T(128)S(1)} %concatenate.3.meta, bf16[640,640]{1,0:T(8,128)(2,1)S(1)} %bitcast.10, bf16[640,640]{1,0:T(8,128)(2,1)S(1)} %collective-permute-done.other_ref, bf16[640,128]{1,0:T(8,128)(2,1)S(1)} %collective-permute-done.1.pair_ref, ...), custom_call_target="tpu_custom_call" | custom-call | tf_op jit(solution)/shard_map/near/pallas_call | solution.py:154
  115.9 0.0 copy-start.1
  115.9 4.8 %far.1 = bf16[1280,256]{1,0:T(8,128)(2,1)S(1)} custom-call(s32[17]{0:T(128)S(1)} %concatenate.3.meta, bf16[1280,256]{1,0:T(8,128)(2,1)} %get-tuple-element.16.q_hbm, f32[1280,512]{1,0:T(8,128)} %get-tuple-element.17.acc_hbm, f32[1280,256]{1,0:T(8,128)} %get-tuple-element.18.top_hbm, bf16[16,2,8,8,128]{4,3,2,1,0:T(8,128)(2,1)S(1)} %bitcast.12), custom_call_target="tpu_custom_call" | custom-call | tf_op jit(solution)/shard_map/far/pallas_call | solution.py:266
  120.8 26.9 %all_to_all.21.x_ref = bf16[32,40,256]{2,1,0:T(8,128)(2,1)S(1)} all-to-all(bf16[32,40,256]{2,1,0:T(8,128)(2,1)S(1)} %bitcast.11), channel_id=1, replica_groups=mesh['xl'=2,'za'=3,'zb'=4,'c'=2,'xh'=2,'ya'=4,'yb'=2] {'c','xh','ya','yb'}, dimensions={0} | all-to-all | bytes 1310720 | tf_op jit(solution)/shard_map/all_to_all | solution.py:491
  147.7 2.0 %to_slots.1 = bf16[40,8192]{1,0:T(8,128)(2,1)} custom-call(s32[64]{0:T(128)S(1)} %copy-done.1, bf16[32,40,256]{2,1,0:T(8,128)(2,1)S(1)} %all_to_all.21.x_ref), custom_call_target="tpu_custom_call" | custom-call | tf_op jit(solution)/shard_map/to_slots/pallas_call | solution.py:446
  (7 shorter events, 0.0 us)
Async XLA Ops:
  0.0 11.2 %copy-start = (s32[64,4]{0,1:T(4,128)S(1)}, s32[64,4]{0,1:T(4,128)}, u32[]{:S(2)}) copy-start(s32[64,4]{0,1:T(4,128)} %param.10) | copy-start | bytes 3076
  0.0 11.7 %copy-start.2 = (s32[64,3]{0,1:T(4,128)S(1)}, s32[64,3]{0,1:T(4,128)}, u32[]{:S(2)}) copy-start(s32[64,3]{0,1:T(4,128)} %param.11) | copy-start | bytes 2308
  2.1 32.1 %all-to-all-start = ((bf16[16,40,640]{2,1,0:T(8,128)(2,1)}), bf16[16,40,640]{2,1,0:T(8,128)(2,1)S(1)}, u32[]{:S(2)}, u32[]{:S(2)}) async-start(bf16[16,40,640]{2,1,0:T(8,128)(2,1)} %lay_out.1), calls=%async_computation | async-start | bytes 1638400 | tf_op jit(solution)/shard_map/all_to_all | solution.py:475
  73.5 42.4 %all-to-all-start.2 = ((bf16[32,8,8,128]{3,2,1,0:T(8,128)(2,1)}), bf16[32,8,8,128]{3,2,1,0:T(8,128)(2,1)S(1)}, u32[]{:S(2)}, u32[]{:S(2)}) async-start(bf16[32,8,8,128]{3,2,1,0:T(8,128)(2,1)} %choose.1), calls=%async_computation.2 | async-start | bytes 1048576 | tf_op jit(solution)/shard_map/all_to_all | solution.py:488
  81.2 15.6 %collective-permute-start = (bf16[640,640]{1,0:T(8,128)(2,1)S(1)}, bf16[640,640]{1,0:T(8,128)(2,1)S(1)}, u32[]{:S(2)}, u32[]{:S(2)}) collective-permute-start(bf16[640,640]{1,0:T(8,128)(2,1)S(1)} %bitcast.8), channel_id=1, source_target_pairs={{0,16},{16,0},{1,17},{17,1},{2,18},{18,2},{3,19},{19,3},{4,20},{20... | collective-permute-start | bytes 2457608 | tf_op jit(solution)/shard_map/ppermute | solution.py:480
  83.2 11.2 %collective-permute-start.1 = (bf16[640,128]{1,0:T(8,128)(2,1)S(1)}, bf16[640,128]{1,0:T(8,128)(2,1)S(1)}, u32[]{:S(2)}, u32[]{:S(2)}) collective-permute-start(bf16[640,128]{1,0:T(8,128)(2,1)S(1)} %get-tuple-element.15), channel_id=1, source_target_pairs={{0,1},{1,0},{2,3},{3,2},{4,5},{5,4},{6,7},{7,6},{8,9},{9,8},{10,11... | collective-permute-start | bytes 491528 | tf_op jit(solution)/shard_map/ppermute | solution.py:481
  85.7 11.1 %collective-permute-start.2 = (bf16[640,128]{1,0:T(8,128)(2,1)S(1)}, bf16[640,128]{1,0:T(8,128)(2,1)S(1)}, u32[]{:S(2)}, u32[]{:S(2)}) collective-permute-start(bf16[640,128]{1,0:T(8,128)(2,1)S(1)} %get-tuple-element.15), channel_id=1, source_target_pairs={{0,17},{1,16},{16,1},{17,0},{2,19},{3,18},{18,3},{19,2},{4,21},{5,... | collective-permute-start | bytes 491528 | tf_op jit(solution)/shard_map/ppermute | solution.py:482
  97.4 10.5 %collective-permute-start.3 = (bf16[640,128]{1,0:T(8,128)(2,1)S(1)}, bf16[640,128]{1,0:T(8,128)(2,1)S(1)}, u32[]{:S(2)}, u32[]{:S(2)}) collective-permute-start(bf16[640,128]{1,0:T(8,128)(2,1)S(1)} %newest.1), channel_id=1, source_target_pairs={{0,32},{32,64},{64,96},{96,128},{128,160},{160,192},{192,224},{224... | collective-permute-start | bytes 491528 | tf_op jit(solution)/shard_map/ppermute | solution.py:484
  107.9 3.3 %collective-permute-start.4 = (bf16[640,128]{1,0:T(8,128)(2,1)S(1)}, bf16[640,128]{1,0:T(8,128)(2,1)S(1)}, u32[]{:S(2)}, u32[]{:S(2)}) collective-permute-start(bf16[640,128]{1,0:T(8,128)(2,1)S(1)} %collective-permute-done.3.prev_ref), channel_id=1, source_target_pairs={{0,16},{16,0},{1,17},{17,1},{2,18},{18,2},{3,19},{19,3},{4,20},{20... | collective-permute-start | bytes 491528 | tf_op jit(solution)/shard_map/ppermute | solution.py:485
  115.9 31.8 %copy-start.1 = (s32[64]{0:T(128)S(1)}, s32[64]{0:T(128)}, u32[]{:S(2)}) copy-start(s32[64]{0:T(128)} %assign.1) | copy-start | bytes 772

commit v9 on v7

--- a/solution.py
+++ b/solution.py
@@ -34,8 +34,8 @@
 SCALE = 1.0 / math.sqrt(HD)
 NEG = float("-inf")
 SMALL = 4 * 1024 * 1024
-PAIR = 5
-LARGE = 12 * 1024 * 1024
+PAIR = 10
+LARGE = 16 * 1024 * 1024
 
 
 LOG2E_SCALE = SCALE * math.log2(math.e)
@@ -348,14 +348,14 @@
     )(in_smem(verts), in_vmem(held))
 
 
-def lay_out(q_hbm, k_hbm, v_hbm, o_ref, q_ref, k_ref, v_ref, sems):
+def lay_out(q_hbm, k_hbm, v_hbm, o_hbm, q_ref, k_ref, v_ref, sent, sems):
     step = 8
+    spans = [pl.ds(row, step) for row in range(0, ROWS, step)]
     copies = [
         pltpu.make_async_copy(k_hbm, k_ref, sems.at[0]),
         pltpu.make_async_copy(v_hbm, v_ref, sems.at[1]),
     ]
-    for n, row in enumerate(range(0, ROWS, step)):
-        rows = pl.ds(row, step)
+    for n, rows in enumerate(spans):
         copies.append(pltpu.make_async_copy(q_hbm.at[rows], q_ref.at[rows], sems.at[2 + n]))
     for copy in copies:
         copy.start()
@@ -363,26 +363,34 @@
     copies[1].wait()
     for g in range(GROUPS):
         m = g // 2 * HD
-        o_ref[g, :, CHIP_WIDE:WIDE] = (v_ref if g % 2 else k_ref)[:, m : m + HD]
-    for n, row in enumerate(range(0, ROWS, step)):
+        sent[g, :, CHIP_WIDE:WIDE] = (v_ref if g % 2 else k_ref)[:, m : m + HD]
+    out = []
+    for n, rows in enumerate(spans):
         copies[2 + n].wait()
         for g in range(GROUPS):
-            o_ref[g, row : row + step, 0:CHIP_WIDE] = q_ref[
-                row : row + step, g * CHIP_WIDE : (g + 1) * CHIP_WIDE
-            ]
+            sent[g, rows, 0:CHIP_WIDE] = q_ref[rows, g * CHIP_WIDE : (g + 1) * CHIP_WIDE]
+        out.append(
+            pltpu.make_async_copy(
+                sent.at[:, rows, :], o_hbm.at[:, rows, :], sems.at[2 + len(spans) + n]
+            )
+        )
+        out[-1].start()
+    for copy in out:
+        copy.wait()
 
 
 def pack(q, k, v):
     return pl.pallas_call(
         lay_out,
-        out_shape=pltpu.VMEM((GROUPS, ROWS, WIDE), jnp.bfloat16),
+        out_shape=pltpu.HBM((GROUPS, ROWS, WIDE), jnp.bfloat16),
         in_specs=[pl.BlockSpec(memory_space=pltpu.HBM)] * 3,
-        out_specs=pl.BlockSpec(memory_space=pltpu.VMEM),
+        out_specs=pl.BlockSpec(memory_space=pltpu.HBM),
         scratch_shapes=[
             pltpu.VMEM((ROWS, QUERY_HEADS * HD), jnp.bfloat16),
             pltpu.VMEM((ROWS, KEY_VALUE_HEADS * HD), jnp.bfloat16),
             pltpu.VMEM((ROWS, KEY_VALUE_HEADS * HD), jnp.bfloat16),
-            pltpu.SemaphoreType.DMA((2 + ROWS // 8,)),
+            pltpu.VMEM((GROUPS, ROWS, WIDE), jnp.bfloat16),
+            pltpu.SemaphoreType.DMA((2 + 2 * (ROWS // 8),)),
         ],
         name="lay_out",
         compiler_params=pltpu.CompilerParams(vmem_limit_bytes=SMALL),

time: 149 us -> 150 us (level)
  transfers between devices with their start and end apart: 6 -> 6, of which waited for: 4 -> 4; matrix products, arithmetic and copies ran while one was open for 1% -> 1% of each run, Pallas kernels for 3% -> 4%
where the time goes in v9:
time: 150 us; the launch traced here: 149 us
  blocking collectives  63.7 us (42%)
  waiting for transfers between devices  40.6 us (27%)
  starting transfers between devices  28 us (19%)
  Pallas kernels  15.7 us (10%)
    all_to_all x1, blocking collectives, per_device(): held = lax.all_to_all(chunks, SEQ, 0, 0, tiled=True)  36.8 us
    all_to_all x1, blocking collectives, per_device(): lax.all_to_all(out.reshape(CORES * GROUPS, ROWS, SLOTS * HD), SPLIT, 0, 0...  26.9 us
    all_to_all x1, waiting for transfers between devices, per_device(): here = lax.all_to_all(sent, HEAD, 0, 0, tiled=True).reshape(SEQ_ROWS, WIDE)  22.1 us
    ppermute x1, waiting for transfers between devices, per_device(): lax.ppermute(last, ('xl', 'za', 'zb'), [(i, i + 1) for i in range(23)])  10.4 us
    all_to_all x1, starting transfers between devices, per_device(): here = lax.all_to_all(sent, HEAD, 0, 0, tiled=True).reshape(SEQ_ROWS, WIDE)  9.14 us
    all_to_all x1, starting transfers between devices, per_device(): vert = lax.all_to_all(spread, ('xl', 'zb', 'c', 'yb'), 0, 0, tiled=True)  7.71 us
    ppermute x1, waiting for transfers between devices, per_device(): pair = lax.ppermute(x_here, 'yb', [(0, 1), (1, 0)])  5.67 us
    pallas_call x1, Pallas kernels, near(): pl.pallas_call(near_part, out_shape=(pltpu.HBM((TOKENS, 2 * SLOTS * HD),...  4.91 us
  transfers between devices with their start and end apart: 6, of which 4 were waited for; matrix products, arithmetic and copies ran while one was open for 1% of the time, Pallas kernels for 4%

profile of v9, /device:TPU:10, one launch (start us, length us, event | category | flops | bytes accessed | tf_op | source)
XLA Modules:
  0.0 148.9 jit_solution(9007454296717245815)
XLA Ops:
  0.0 2.1 %lay_out.1 = bf16[16,40,640]{2,1,0:T(8,128)(2,1)} custom-call(bf16[40,8192]{1,0:T(8,128)(2,1)} %q_hbm.1, bf16[40,1024]{1,0:T(8,128)(2,1)} %k_hbm.1, bf16[40,1024]{1,0:T(8,128)(2,1)} %v_hbm.1), custom_call_target="tpu_custom_call" | custom-call | tf_op jit(solution)/shard_map/lay_out/pallas_call | solution.py:383
  2.1 9.1 %all-to-all-start = ((bf16[16,40,640]{2,1,0:T(8,128)(2,1)}), bf16[16,40,640]{2,1,0:T(8,128)(2,1)S(1)}, u32[]{:S(2)}, u32[]{:S(2)}) async-start(bf16[16,40,640]{2,1,0:T(8,128)(2,1)} %lay_out.1), calls=%async_computation | async-start | bytes 1638400 | tf_op jit(solution)/shard_map/all_to_all | solution.py:446
  11.2 0.1 constant_dynamic-slice_fusion.2
  11.3 0.1 copy.10
  11.4 0.1 reshape.22.verts
  11.5 0.1 constant_dynamic-slice_fusion.1
  11.5 0.1 copy.11
  11.6 0.1 reshape.23
  11.7 0.1 constant_dynamic-slice_fusion
  11.8 0.1 copy.12
  11.9 0.1 reshape.24
  12.0 0.1 concatenate.3.meta
  12.1 22.1 %all-to-all-done = bf16[16,40,640]{2,1,0:T(8,128)(2,1)S(1)} async-done(((bf16[16,40,640]{2,1,0:T(8,128)(2,1)}), bf16[16,40,640]{2,1,0:T(8,128)(2,1)S(1)}, u32[]{:S(2)}, u32[]{:S(2)}) %all-to-all-start) | async-done | bytes 819232 | tf_op jit(solution)/shard_map/all_to_all | solution.py:446
  34.2 0.1 cut.1
  34.3 36.8 %all_to_all.20 = bf16[48,5,8,128]{3,2,1,0:T(8,128)(2,1)S(1)} all-to-all(bf16[48,5,8,128]{3,2,1,0:T(8,128)(2,1)S(1)} %get-tuple-element.20), channel_id=1, replica_groups=mesh['xl'=2,'za'=3,'zb'=4,'c'=2,'xh'=2,'ya'=4,'yb'=2] {'xl','za','zb','c'}, dimensions={0} | all-to-all | bytes 983040 | tf_op jit(solution)/shard_map/all_to_all | solution.py:449
  71.0 1.4 choose.1
  72.4 7.7 %all-to-all-start.2 = ((bf16[32,8,8,128]{3,2,1,0:T(8,128)(2,1)}), bf16[32,8,8,128]{3,2,1,0:T(8,128)(2,1)S(1)}, u32[]{:S(2)}, u32[]{:S(2)}) async-start(bf16[32,8,8,128]{3,2,1,0:T(8,128)(2,1)} %choose.1), calls=%async_computation.2 | async-start | bytes 1048576 | tf_op jit(solution)/shard_map/all_to_all | solution.py:458
  80.2 2.0 %collective-permute-start = (bf16[640,640]{1,0:T(8,128)(2,1)S(1)}, bf16[640,640]{1,0:T(8,128)(2,1)S(1)}, u32[]{:S(2)}, u32[]{:S(2)}) collective-permute-start(bf16[640,640]{1,0:T(8,128)(2,1)S(1)} %bitcast.8), channel_id=1, source_target_pairs={{0,16},{16,0},{1,17},{17,1},{2,18},{18,2},{3,19},{19,3},{4,20},{20... | collective-permute-start | bytes 2457608 | tf_op jit(solution)/shard_map/ppermute | solution.py:451
  82.2 2.5 %collective-permute-start.1 = (bf16[640,128]{1,0:T(8,128)(2,1)S(1)}, bf16[640,128]{1,0:T(8,128)(2,1)S(1)}, u32[]{:S(2)}, u32[]{:S(2)}) collective-permute-start(bf16[640,128]{1,0:T(8,128)(2,1)S(1)} %get-tuple-element.15), channel_id=1, source_target_pairs={{0,1},{1,0},{2,3},{3,2},{4,5},{5,4},{6,7},{7,6},{8,9},{9,8},{10,11... | collective-permute-start | bytes 491528 | tf_op jit(solution)/shard_map/ppermute | solution.py:452
  84.7 3.1 %collective-permute-start.2 = (bf16[640,128]{1,0:T(8,128)(2,1)S(1)}, bf16[640,128]{1,0:T(8,128)(2,1)S(1)}, u32[]{:S(2)}, u32[]{:S(2)}) collective-permute-start(bf16[640,128]{1,0:T(8,128)(2,1)S(1)} %get-tuple-element.15), channel_id=1, source_target_pairs={{0,17},{1,16},{16,1},{17,0},{2,19},{3,18},{18,3},{19,2},{4,21},{5,... | collective-permute-start | bytes 491528 | tf_op jit(solution)/shard_map/ppermute | solution.py:453
  87.8 5.7 %collective-permute-done.1.pair_ref = bf16[640,128]{1,0:T(8,128)(2,1)S(1)} collective-permute-done((bf16[640,128]{1,0:T(8,128)(2,1)S(1)}, bf16[640,128]{1,0:T(8,128)(2,1)S(1)}, u32[]{:S(2)}, u32[]{:S(2)}) %collective-permute-start.1) | collective-permute-done | bytes 163872 | tf_op jit(solution)/shard_map/ppermute | solution.py:452
  93.4 2.4 %collective-permute-done.2.diag_ref = bf16[640,128]{1,0:T(8,128)(2,1)S(1)} collective-permute-done((bf16[640,128]{1,0:T(8,128)(2,1)S(1)}, bf16[640,128]{1,0:T(8,128)(2,1)S(1)}, u32[]{:S(2)}, u32[]{:S(2)}) %collective-permute-start.2) | collective-permute-done | bytes 163872 | tf_op jit(solution)/shard_map/ppermute | solution.py:453
  95.8 0.0 collective-permute-done.other_ref
  95.8 0.6 newest.1
  96.4 3.6 %collective-permute-start.3 = (bf16[640,256]{1,0:T(8,128)(2,1)S(1)}, bf16[640,256]{1,0:T(8,128)(2,1)S(1)}, u32[]{:S(2)}, u32[]{:S(2)}) collective-permute-start(bf16[640,256]{1,0:T(8,128)(2,1)S(1)} %newest.1), channel_id=1, source_target_pairs={{0,32},{32,64},{64,96},{96,128},{128,160},{160,192},{192,224},{224... | collective-permute-start | bytes 983048 | tf_op jit(solution)/shard_map/ppermute | solution.py:455
  100.0 10.4 %collective-permute-done.3.prev_ref = bf16[640,256]{1,0:T(8,128)(2,1)S(1)} collective-permute-done((bf16[640,256]{1,0:T(8,128)(2,1)S(1)}, bf16[640,256]{1,0:T(8,128)(2,1)S(1)}, u32[]{:S(2)}, u32[]{:S(2)}) %collective-permute-start.3) | collective-permute-done | bytes 327712 | tf_op jit(solution)/shard_map/ppermute | solution.py:455
  110.4 4.9 %near.1 = (f32[1280,512]{1,0:T(8,128)}, f32[1280,256]{1,0:T(8,128)}, bf16[1280,256]{1,0:T(8,128)(2,1)}) custom-call(s32[17]{0:T(128)S(1)} %concatenate.3.meta, bf16[640,640]{1,0:T(8,128)(2,1)S(1)} %bitcast.10, bf16[640,640]{1,0:T(8,128)(2,1)S(1)} %collective-permute-done.other_ref, bf16[640,128]{1,0:T(8,128)(2,1)S(1)} %collective-permute-done.1.pair_ref, ...), custom_call_target="tpu_custom_call" | custom-call | tf_op jit(solution)/shard_map/near/pallas_call | solution.py:151
  115.4 0.0 all-to-all-done.2
  115.4 0.0 copy-start.1
  115.4 4.6 %far.1 = bf16[1280,256]{1,0:T(8,128)(2,1)S(1)} custom-call(s32[17]{0:T(128)S(1)} %concatenate.3.meta, bf16[1280,256]{1,0:T(8,128)(2,1)} %get-tuple-element.16.q_hbm, f32[1280,512]{1,0:T(8,128)} %get-tuple-element.17.acc_hbm, f32[1280,256]{1,0:T(8,128)} %get-tuple-element.18.top_hbm, bf16[16,2,8,8,128]{4,3,2,1,0:T(8,128)(2,1)S(1)} %bitcast.12), custom_call_target="tpu_custom_call" | custom-call | tf_op jit(solution)/shard_map/far/pallas_call | solution.py:263
  120.0 26.9 %all_to_all.21.x_ref = bf16[32,40,256]{2,1,0:T(8,128)(2,1)S(1)} all-to-all(bf16[32,40,256]{2,1,0:T(8,128)(2,1)S(1)} %bitcast.11), channel_id=1, replica_groups=mesh['xl'=2,'za'=3,'zb'=4,'c'=2,'xh'=2,'ya'=4,'yb'=2] {'c','xh','ya','yb'}, dimensions={0} | all-to-all | bytes 1310720 | tf_op jit(solution)/shard_map/all_to_all | solution.py:461
  146.9 2.0 %to_slots.1 = bf16[40,8192]{1,0:T(8,128)(2,1)} custom-call(s32[64]{0:T(128)S(1)} %copy-done.1, bf16[32,40,256]{2,1,0:T(8,128)(2,1)S(1)} %all_to_all.21.x_ref), custom_call_target="tpu_custom_call" | custom-call | tf_op jit(solution)/shard_map/to_slots/pallas_call | solution.py:417
  (5 shorter events, 0.0 us)
Async XLA Ops:
  0.0 11.2 %copy-start = (s32[64,4]{0,1:T(4,128)S(1)}, s32[64,4]{0,1:T(4,128)}, u32[]{:S(2)}) copy-start(s32[64,4]{0,1:T(4,128)} %param.10) | copy-start | bytes 3076
  0.0 11.7 %copy-start.2 = (s32[64,3]{0,1:T(4,128)S(1)}, s32[64,3]{0,1:T(4,128)}, u32[]{:S(2)}) copy-start(s32[64,3]{0,1:T(4,128)} %param.11) | copy-start | bytes 2308
  2.1 32.1 %all-to-all-start = ((bf16[16,40,640]{2,1,0:T(8,128)(2,1)}), bf16[16,40,640]{2,1,0:T(8,128)(2,1)S(1)}, u32[]{:S(2)}, u32[]{:S(2)}) async-start(bf16[16,40,640]{2,1,0:T(8,128)(2,1)} %lay_out.1), calls=%async_computation | async-start | bytes 1638400 | tf_op jit(solution)/shard_map/all_to_all | solution.py:446
  72.4 42.9 %all-to-all-start.2 = ((bf16[32,8,8,128]{3,2,1,0:T(8,128)(2,1)}), bf16[32,8,8,128]{3,2,1,0:T(8,128)(2,1)S(1)}, u32[]{:S(2)}, u32[]{:S(2)}) async-start(bf16[32,8,8,128]{3,2,1,0:T(8,128)(2,1)} %choose.1), calls=%async_computation.2 | async-start | bytes 1048576 | tf_op jit(solution)/shard_map/all_to_all | solution.py:458
  80.2 15.6 %collective-permute-start = (bf16[640,640]{1,0:T(8,128)(2,1)S(1)}, bf16[640,640]{1,0:T(8,128)(2,1)S(1)}, u32[]{:S(2)}, u32[]{:S(2)}) collective-permute-start(bf16[640,640]{1,0:T(8,128)(2,1)S(1)} %bitcast.8), channel_id=1, source_target_pairs={{0,16},{16,0},{1,17},{17,1},{2,18},{18,2},{3,19},{19,3},{4,20},{20... | collective-permute-start | bytes 2457608 | tf_op jit(solution)/shard_map/ppermute | solution.py:451
  82.2 11.2 %collective-permute-start.1 = (bf16[640,128]{1,0:T(8,128)(2,1)S(1)}, bf16[640,128]{1,0:T(8,128)(2,1)S(1)}, u32[]{:S(2)}, u32[]{:S(2)}) collective-permute-start(bf16[640,128]{1,0:T(8,128)(2,1)S(1)} %get-tuple-element.15), channel_id=1, source_target_pairs={{0,1},{1,0},{2,3},{3,2},{4,5},{5,4},{6,7},{7,6},{8,9},{9,8},{10,11... | collective-permute-start | bytes 491528 | tf_op jit(solution)/shard_map/ppermute | solution.py:452
  84.7 11.1 %collective-permute-start.2 = (bf16[640,128]{1,0:T(8,128)(2,1)S(1)}, bf16[640,128]{1,0:T(8,128)(2,1)S(1)}, u32[]{:S(2)}, u32[]{:S(2)}) collective-permute-start(bf16[640,128]{1,0:T(8,128)(2,1)S(1)} %get-tuple-element.15), channel_id=1, source_target_pairs={{0,17},{1,16},{16,1},{17,0},{2,19},{3,18},{18,3},{19,2},{4,21},{5,... | collective-permute-start | bytes 491528 | tf_op jit(solution)/shard_map/ppermute | solution.py:453
  96.4 14.0 %collective-permute-start.3 = (bf16[640,256]{1,0:T(8,128)(2,1)S(1)}, bf16[640,256]{1,0:T(8,128)(2,1)S(1)}, u32[]{:S(2)}, u32[]{:S(2)}) collective-permute-start(bf16[640,256]{1,0:T(8,128)(2,1)S(1)} %newest.1), channel_id=1, source_target_pairs={{0,32},{32,64},{64,96},{96,128},{128,160},{160,192},{192,224},{224... | collective-permute-start | bytes 983048 | tf_op jit(solution)/shard_map/ppermute | solution.py:455
  115.4 31.6 %copy-start.1 = (s32[64]{0:T(128)S(1)}, s32[64]{0:T(128)}, u32[]{:S(2)}) copy-start(s32[64]{0:T(128)} %assign.1) | copy-start | bytes 772
